TPU v7x, 32 devices: a whole 2x2x4 slice. The times are simulated.
32 devices in a mesh: row: 8 (over z, y), col: 4 (over x, core).
Axes of the slice: x: 2, y: 2, z: 4, core: 2. Of those that a mesh axis runs over, the one named last changes fastest.
Arguments:
- paths_in: float32 [4096, 256], P(('row', 'col')), may hold values from 0.05 to 4
- dep_in: float32 [4096, 256], P(('row', 'col')), may hold values from 0 to 4
- levels: int32 [4096, 256], P(('row', 'col')), may hold values from 0 to 4, as said below
- tile_src: int32 [8, 4, 8, 4], P('row', 'col'), may hold values from 0 to 3, as said below
- pattern: int32 [8, 4, 8, 4, 128, 128], P('row', 'col'), may hold values from 0 to 1, as said below
Outputs:
- dependency: float32 [4096, 256], P(('row', 'col'))
Inputs may be any that keep to these rules, and one draw needn't show every extreme that they name: The value 4 marks a vertex outside the window's levels for that source. A program may send only the non-zero entries of a level's rounded path counts or backward weights, together with their positions, in any encoding that loses nothing. `tile_src`: within one device the 4 source tiles of a destination tile row are distinct, and every source tile index appears in exactly 8 of the device's slots. `pattern`: each slot holds either an all-zero tile or a tile of independent 0/1 entries; a device has from 1 to 32 nonzero tiles, and some device has all its slots nonzero.
All inputs are finite; a program needn't handle non-finite values.
Results may differ from a plain program's by a relative error of at most 0.0016.
Values may be sent and summed in bfloat16 or wider, within the bound.
No kernel may reach another device: no remote copies, remote signals or barrier semaphores. Data moves between devices by JAX's collectives and lax.ppermute only.
A program may use at most 64 MiB of HBM per device.

v0:
```python
import jax
import jax.numpy as jnp
from jax import lax
from jax.sharding import PartitionSpec as P


def shards(paths_in, dep_in, levels, tile_src, pattern):
    vert_dev = paths_in.shape[0]
    tile_size = pattern.shape[-1]
    dest_tiles = tile_src.shape[2]
    band_slots = tile_src.shape[3]
    src_tiles = lax.axis_size("col") * vert_dev // tile_size
    per_source = dest_tiles * band_slots // src_tiles
    source_ids = tile_src[0, 0]
    tile_values = pattern[0, 0].astype(jnp.bfloat16)
    flat_ids = source_ids.reshape(-1)
    by_source = jnp.argsort(flat_ids, stable=True)
    back_values = tile_values.reshape(-1, tile_size, tile_size)[by_source]
    back_values = back_values.reshape(src_tiles, per_source, tile_size, tile_size)
    back_dest = (by_source // band_slots).reshape(src_tiles, per_source)

    def forward_terms(frontier):
        gathered = lax.all_gather(frontier, "col", axis=0, tiled=True)
        pieces = gathered.reshape(src_tiles, tile_size, gathered.shape[1])

        def dest_terms(begin_row, row_count):
            picked = pieces[source_ids]
            product = jnp.einsum(
                "ibrj,ibjs->irs", tile_values, picked, preferred_element_type=jnp.float32
            )
            return product.reshape(row_count, product.shape[2])

        return dest_terms

    def scattered(dest_terms):
        return lax.psum_scatter(
            dest_terms(jnp.int32(0), vert_dev * lax.axis_size("row")),
            "row",
            scatter_dimension=0,
            tiled=True,
        )

    def spread(weight):
        return lax.all_gather(weight, "row", axis=0, tiled=True)

    level_masks = [(levels == distance).astype(jnp.float32) for distance in range(4)]
    numerator = level_masks[3] * (1.0 + dep_in)
    path_counts = [level_masks[0] * paths_in]
    for distance in (1, 2):
        dest_terms = forward_terms(path_counts[-1].astype(jnp.bfloat16))
        path_counts.append(level_masks[distance] * scattered(dest_terms))
    last_terms = forward_terms(path_counts[-1].astype(jnp.bfloat16))
    paths_last = level_masks[3] * scattered(last_terms)
    spread_weight = spread((numerator / jnp.maximum(paths_last, 1.0)).astype(jnp.bfloat16))
    dependency = jnp.zeros(paths_in.shape, jnp.float32)
    for distance in (2, 1, 0):
        backward_pieces = spread_weight.reshape(dest_tiles, tile_size, spread_weight.shape[1])
        source_picked = backward_pieces[back_dest]
        source_product = jnp.einsum(
            "tgrj,tgrs->tjs", back_values, source_picked, preferred_element_type=jnp.float32
        )
        dependence = (
            level_masks[distance]
            * path_counts[distance]
            * lax.psum_scatter(
                source_product.reshape(vert_dev * lax.axis_size("col"), source_product.shape[2]),
                "col",
                scatter_dimension=0,
                tiled=True,
            )
        )
        dependency = dependency + dependence
        if distance > 0:
            weight = (
                level_masks[distance] * (1.0 + dependence) / jnp.maximum(path_counts[distance], 1.0)
            ).astype(jnp.bfloat16)
            spread_weight = spread(weight)
    return dependency


def solution(mesh):
    placed = (
        P(("row", "col"), None),
        P(("row", "col"), None),
        P(("row", "col"), None),
        P("row", "col", None, None),
        P("row", "col", None, None, None, None),
    )
    return jax.shard_map(
        shards, mesh=mesh, in_specs=placed, out_specs=P(("row", "col"), None), check_vma=False
    )
```

profile of v0, /device:TPU:0, one launch (start us, length us, event | category | flops | bytes accessed | tf_op | source)
XLA Modules:
  0.0 416.7 jit_solution(13446008546591809640)
XLA Ops:
  6.5 0.7 compare_select_fusion.1
  7.2 0.1 copy.9
  7.3 0.1 reshape.118
  7.4 1.6 select_convert_fusion
  9.0 7.2 %all_gather.18 = bf16[512,256]{1,0:T(8,128)(2,1)S(1)} all-gather(bf16[128,256]{1,0:T(8,128)(2,1)S(1)} %get-tuple-element.11), channel_id=1, replica_groups=mesh['row'=8,'col'=4] {'col'}, dimensions={0}, use_global_device_ids=true | all-gather | bytes 327680 | tf_op jit(solution)/shard_map/all_gather | solution.py:23
  16.2 1.8 convert_element_type.33
  18.0 0.7 gather_fusion
  18.7 1.5 fusion
  20.2 0.0 reduce-scatter.7.cloned.1.call-update
  20.2 0.0 reduce-scatter.9.cloned.1.call-start
  20.3 65.6 %reduce-scatter.7.cloned.1.call-done = f32[128,256]{1,0:T(8,128)} async-done(((f32[1024,256]{1,0:T(8,128)}), f32[128,256]{1,0:T(8,128)}) %reduce-scatter.7.cloned.1.call-update) | async-done | bytes 131088 | tf_op jit(solution)/shard_map/reduce_scatter | solution.py:36
  85.9 1.5 select_convert_fusion.2
  87.4 5.8 %all_gather.19 = bf16[512,256]{1,0:T(8,128)(2,1)S(1)} all-gather(bf16[128,256]{1,0:T(8,128)(2,1)S(1)} %get-tuple-element.9), channel_id=1, replica_groups=mesh['row'=8,'col'=4] {'col'}, dimensions={0}, use_global_device_ids=true | all-gather | bytes 327680 | tf_op jit(solution)/shard_map/all_gather | solution.py:23
  93.2 0.7 gather_fusion.1
  93.9 1.5 fusion.2
  95.4 0.0 reduce-scatter.9.cloned.1.call-update
  95.4 0.0 reduce-scatter.11.cloned.1.call-start
  95.5 63.2 %reduce-scatter.9.cloned.1.call-done = f32[128,256]{1,0:T(8,128)} async-done(((f32[1024,256]{1,0:T(8,128)}), f32[128,256]{1,0:T(8,128)}) %reduce-scatter.9.cloned.1.call-update) | async-done | bytes 131088 | tf_op jit(solution)/shard_map/reduce_scatter | solution.py:36
  158.6 1.5 select_convert_fusion.1
  160.2 5.8 %all_gather.20 = bf16[512,256]{1,0:T(8,128)(2,1)S(1)} all-gather(bf16[128,256]{1,0:T(8,128)(2,1)S(1)} %get-tuple-element.7), channel_id=1, replica_groups=mesh['row'=8,'col'=4] {'col'}, dimensions={0}, use_global_device_ids=true | all-gather | bytes 327680 | tf_op jit(solution)/shard_map/all_gather | solution.py:23
  165.9 0.7 gather_fusion.3
  166.6 1.5 fusion.4
  168.1 0.0 reduce-scatter.13.cloned.1.call-start
  168.2 0.1 copy.10
  168.3 0.1 reshape_squeeze.3
  168.4 1.7 sort.17
  170.0 0.1 reshape.110
  170.1 0.1 reshape.150
  170.2 0.8 gather_fusion.2
  171.0 60.4 %reduce-scatter.11.cloned.1.call-done = f32[128,256]{1,0:T(8,128)} async-done(((f32[1024,256]{1,0:T(8,128)}), f32[128,256]{1,0:T(8,128)}) %reduce-scatter.11.cloned.1.call-update) | async-done | bytes 131088 | tf_op jit(solution)/shard_map/reduce_scatter | solution.py:36
  231.4 0.9 divide_convert_fusion.2
  232.3 31.5 %all_gather.21 = bf16[1024,256]{1,0:T(8,128)(2,1)S(1)} all-gather(bf16[128,256]{1,0:T(8,128)(2,1)S(1)} %divide_convert_fusion.2), channel_id=1, replica_groups=mesh['row'=8,'col'=4] {'row'}, dimensions={0}, use_global_device_ids=true | all-gather | bytes 589824 | tf_op jit(solution)/shard_map/all_gather | solution.py:44
  263.8 2.0 gather_fusion.4
  265.9 3.0 fusion.6
  268.9 0.0 reduce-scatter.15.cloned.1.call-start
  268.9 20.6 %reduce-scatter.13.cloned.1.call-done = f32[128,256]{1,0:T(8,128)} async-done(((f32[512,256]{1,0:T(8,128)}), f32[128,256]{1,0:T(8,128)}) %reduce-scatter.13.cloned.1.call-update) | async-done | bytes 131088 | tf_op jit(solution)/shard_map/reduce_scatter | solution.py:65
  289.5 1.0 divide_convert_fusion.1
  290.4 31.5 %all_gather.22 = bf16[1024,256]{1,0:T(8,128)(2,1)S(1)} all-gather(bf16[128,256]{1,0:T(8,128)(2,1)S(1)} %divide_convert_fusion.1), channel_id=1, replica_groups=mesh['row'=8,'col'=4] {'row'}, dimensions={0}, use_global_device_ids=true | all-gather | bytes 589824 | tf_op jit(solution)/shard_map/all_gather | solution.py:44
  321.9 2.0 gather_fusion.5
  324.0 3.0 fusion.7
  327.0 0.0 reduce-scatter.17.cloned.1.call-start
  327.0 21.8 %reduce-scatter.15.cloned.1.call-done = f32[128,256]{1,0:T(8,128)} async-done(((f32[512,256]{1,0:T(8,128)}), f32[128,256]{1,0:T(8,128)}) %reduce-scatter.15.cloned.1.call-update) | async-done | bytes 131088 | tf_op jit(solution)/shard_map/reduce_scatter | solution.py:65
  348.8 1.0 divide_convert_fusion
  349.8 31.5 %all_gather.23 = bf16[1024,256]{1,0:T(8,128)(2,1)S(1)} all-gather(bf16[128,256]{1,0:T(8,128)(2,1)S(1)} %divide_convert_fusion), channel_id=1, replica_groups=mesh['row'=8,'col'=4] {'row'}, dimensions={0}, use_global_device_ids=true | all-gather | bytes 589824 | tf_op jit(solution)/shard_map/all_gather | solution.py:44
  381.2 2.0 gather_fusion.6
  383.3 3.0 fusion.8
  386.3 21.9 %reduce-scatter.17.cloned.1.call-done = f32[128,256]{1,0:T(8,128)} async-done(((f32[512,256]{1,0:T(8,128)}), f32[128,256]{1,0:T(8,128)}) %reduce-scatter.17.cloned.1.call-update) | async-done | bytes 131088 | tf_op jit(solution)/shard_map/reduce_scatter | solution.py:65
  408.2 1.6 multiply_add_fusion
  (33 shorter events, 0.2 us)
Async XLA Ops:
  6.5 79.4 %reduce-scatter.7.cloned.1.call-start = ((), (), s32[]{:S(2)}) async-start(), calls=%async_computation.6 | async-start | bytes 1179648 | tf_op jit(solution)/shard_map/reduce_scatter | solution.py:36
  18.7 67.2 %copy-start = (s32[128,256]{1,0:T(8,128)S(1)}, s32[128,256]{1,0:T(8,128)}, u32[]{:S(2)}) copy-start(s32[128,256]{1,0:T(8,128)} %param.7) | copy-start | bytes 393220
  20.2 138.4 %reduce-scatter.9.cloned.1.call-start = ((), (), s32[]{:S(2)}) async-start(), calls=%async_computation.7 | async-start | bytes 1179648 | tf_op jit(solution)/shard_map/reduce_scatter | solution.py:36
  95.4 135.9 %reduce-scatter.11.cloned.1.call-start = ((), (), s32[]{:S(2)}) async-start(), calls=%async_computation.8 | async-start | bytes 1179648 | tf_op jit(solution)/shard_map/reduce_scatter | solution.py:36
  166.6 1.6 copy-start.10
  168.1 63.2 %copy-start.8 = (f32[128,256]{1,0:T(8,128)S(1)}, f32[128,256]{1,0:T(8,128)}, u32[]{:S(2)}) copy-start(f32[128,256]{1,0:T(8,128)} %param.6) | copy-start | bytes 393220
  168.1 121.3 %reduce-scatter.13.cloned.1.call-start = ((), (), s32[]{:S(2)}) async-start(), calls=%async_computation.9 | async-start | bytes 655360 | tf_op jit(solution)/shard_map/reduce_scatter | solution.py:65
  265.9 23.6 %copy-start.2 = (f32[128,256]{1,0:T(8,128)S(1)}, f32[128,256]{1,0:T(8,128)}, u32[]{:S(2)}) copy-start(f32[128,256]{1,0:T(8,128)} %reduce-scatter.9.cloned.1.call-done) | copy-start | bytes 393220
  265.9 23.6 %copy-start.7 = (pred[128,256]{1,0:T(8,128)(4,1)S(1)}, pred[128,256]{1,0:T(8,128)(4,1)}, u32[]{:S(2)}) copy-start(pred[128,256]{1,0:T(8,128)(4,1)} %get-tuple-element.8) | copy-start | bytes 98308
  268.9 79.9 %reduce-scatter.15.cloned.1.call-start = ((), (), s32[]{:S(2)}) async-start(), calls=%async_computation.10 | async-start | bytes 655360 | tf_op jit(solution)/shard_map/reduce_scatter | solution.py:65
  324.0 24.9 %copy-start.1 = (f32[128,256]{1,0:T(8,128)S(1)}, f32[128,256]{1,0:T(8,128)}, u32[]{:S(2)}) copy-start(f32[128,256]{1,0:T(8,128)} %reduce-scatter.7.cloned.1.call-done) | copy-start | bytes 393220
  324.0 24.9 %copy-start.6 = (pred[128,256]{1,0:T(8,128)(4,1)S(1)}, pred[128,256]{1,0:T(8,128)(4,1)}, u32[]{:S(2)}) copy-start(pred[128,256]{1,0:T(8,128)(4,1)} %get-tuple-element.10) | copy-start | bytes 98308
  327.0 81.3 %reduce-scatter.17.cloned.1.call-start = ((), (), s32[]{:S(2)}) async-start(), calls=%async_computation.11 | async-start | bytes 655360 | tf_op jit(solution)/shard_map/reduce_scatter | solution.py:65
  383.3 25.0 %copy-start.3 = (f32[128,256]{1,0:T(8,128)S(1)}, f32[128,256]{1,0:T(8,128)}, u32[]{:S(2)}) copy-start(f32[128,256]{1,0:T(8,128)} %param.5) | copy-start | bytes 393220
  383.3 25.0 %copy-start.4 = (f32[128,256]{1,0:T(8,128)S(1)}, f32[128,256]{1,0:T(8,128)}, u32[]{:S(2)}) copy-start(f32[128,256]{1,0:T(8,128)} %reduce-scatter.13.cloned.1.call-done) | copy-start | bytes 393220
  383.3 25.0 %copy-start.5 = (f32[128,256]{1,0:T(8,128)S(1)}, f32[128,256]{1,0:T(8,128)}, u32[]{:S(2)}) copy-start(f32[128,256]{1,0:T(8,128)} %reduce-scatter.15.cloned.1.call-done) | copy-start | bytes 393220
  383.3 25.0 %copy-start.9 = (pred[128,256]{1,0:T(8,128)(4,1)S(1)}, pred[128,256]{1,0:T(8,128)(4,1)}, u32[]{:S(2)}) copy-start(pred[128,256]{1,0:T(8,128)(4,1)} %get-tuple-element.12) | copy-start | bytes 98308
Sparse Core Ops, SparseCore 0:
  20.3 65.5 reduce-scatter.6
  95.5 63.0 reduce-scatter.8
  168.3 63.0 reduce-scatter.10
  269.0 20.4 reduce-scatter.12
  327.1 21.6 reduce-scatter.14
  386.4 21.7 reduce-scatter.16
where the time goes:
time: 417 us
  waiting for transfers between devices  254 us (61%)
  blocking collectives  113 us (27%)
  between operations  13.6 us (3%)
  matrix products  13.4 us (3%)
  other arithmetic  13.3 us (3%)
  local copies, waits for them, and re-layouts  9.42 us (2%)
    reduce_scatter x3, waiting for transfers between devices, scattered(): lax.psum_scatter(dest_terms(jnp.int32(0), vert_dev * lax.axis_size('row')...  189 us
    all_gather x3, blocking collectives, spread(): return lax.all_gather(weight, 'row', axis=0, tiled=True)  94.5 us
    reduce_scatter x3, waiting for transfers between devices, shards(): lax.psum_scatter(source_product.reshape(vert_dev * lax.axis_size('col'),...  64.3 us
    all_gather x3, blocking collectives, forward_terms(): gathered = lax.all_gather(frontier, 'col', axis=0, tiled=True)  18.7 us
    dot_general x3, matrix products, shards(): jnp.einsum('tgrj,tgrs->tjs', back_values, source_picked, preferred_elemen...  8.96 us
  transfers between devices with their start and end apart: 6, of which 6 were waited for; matrix products, arithmetic and copies ran while one was open for 1% of the time, Pallas kernels for 0%

commit v1 on v0

v1 whole, which is shorter than its diff:
```python
import jax
import jax.numpy as jnp
from jax import lax
from jax.sharding import PartitionSpec as P


def general_shards(paths_in, dep_in, levels, tile_src, pattern):
    vert_dev = paths_in.shape[0]
    tile_size = pattern.shape[-1]
    dest_tiles = tile_src.shape[2]
    band_slots = tile_src.shape[3]
    src_tiles = lax.axis_size("col") * vert_dev // tile_size
    per_source = dest_tiles * band_slots // src_tiles
    source_ids = tile_src[0, 0]
    tile_values = pattern[0, 0].astype(jnp.bfloat16)
    flat_ids = source_ids.reshape(-1)
    by_source = jnp.argsort(flat_ids, stable=True)
    back_values = tile_values.reshape(-1, tile_size, tile_size)[by_source]
    back_values = back_values.reshape(src_tiles, per_source, tile_size, tile_size)
    back_dest = (by_source // band_slots).reshape(src_tiles, per_source)

    def forward_terms(frontier):
        gathered = lax.all_gather(frontier, "col", axis=0, tiled=True)
        pieces = gathered.reshape(src_tiles, tile_size, gathered.shape[1])
        product = jnp.einsum(
            "ibrj,ibjs->irs", tile_values, pieces[source_ids], preferred_element_type=jnp.float32
        )
        terms = product.reshape(vert_dev * lax.axis_size("row"), product.shape[2])
        return lax.psum_scatter(terms, "row", scatter_dimension=0, tiled=True)

    def spread(weight):
        return lax.all_gather(weight, "row", axis=0, tiled=True)

    level_masks = [(levels == distance).astype(jnp.float32) for distance in range(4)]
    path_counts = [level_masks[0] * paths_in]
    for distance in (1, 2, 3):
        path_counts.append(
            level_masks[distance] * forward_terms(path_counts[-1].astype(jnp.bfloat16))
        )
    numerator = level_masks[3] * (1.0 + dep_in)
    spread_weight = spread((numerator / jnp.maximum(path_counts[3], 1.0)).astype(jnp.bfloat16))
    dependency = jnp.zeros(paths_in.shape, jnp.float32)
    for distance in (2, 1, 0):
        backward_pieces = spread_weight.reshape(dest_tiles, tile_size, spread_weight.shape[1])
        source_product = jnp.einsum(
            "tgrj,tgrs->tjs",
            back_values,
            backward_pieces[back_dest],
            preferred_element_type=jnp.float32,
        )
        source_product = source_product.reshape(
            vert_dev * lax.axis_size("col"), source_product.shape[2]
        )
        dependence = (
            level_masks[distance]
            * path_counts[distance]
            * lax.psum_scatter(source_product, "col", scatter_dimension=0, tiled=True)
        )
        dependency = dependency + dependence
        if distance > 0:
            weight = (
                level_masks[distance] * (1.0 + dependence) / jnp.maximum(path_counts[distance], 1.0)
            ).astype(jnp.bfloat16)
            spread_weight = spread(weight)
    return dependency


def partner(axis, bit):
    return [(i, i ^ bit) for i in range(lax.axis_size(axis))]


def swap(value, axis, bit):
    return lax.ppermute(value, axis, partner(axis, bit))


GROUP = 8
LAYERS = 4
STAGES = (("col", 1, 2), ("col", 2, 1), ("row", 1, 0))


def exchange(pieces):
    held = pieces
    for axis, bit, place in STAGES:
        keep, send = lax.index_in_dim(held, 0, place), lax.index_in_dim(held, 1, place)
        held = jnp.concatenate([keep, swap(send, axis, bit)], axis=place)
    return held


STEPS = 1625.0
LOWEST = 6.0


def coded(count):
    steps = jnp.clip((jnp.log2(count) + LOWEST) * STEPS + 1.5, 1.0, 65535.0)
    return jnp.where(count > 0.0, steps, 0.0).astype(jnp.int32).astype(jnp.uint16)


def decoded(code):
    steps = code.astype(jnp.int32).astype(jnp.float32)
    return jnp.where(steps > 0.0, jnp.exp2((steps - 1.0) * (1.0 / STEPS) - LOWEST), 0.0)


def split_shards(paths_in, dep_in, levels, tile_src, pattern):
    vert, sources = paths_in.shape
    share = sources // GROUP
    cols = lax.axis_size("col")
    tile = pattern.shape[-1]
    row, col = lax.axis_index("row"), lax.axis_index("col")
    layer, side = row >> 1, row & 1
    place = side * cols + col
    by_place = place ^ jnp.arange(GROUP)

    order = (((layer ^ jnp.arange(LAYERS)) << 1)[:, None] + (side ^ jnp.arange(2))[None, :]).reshape(-1)
    ids = tile_src[0, 0][order]
    slot = jnp.argmax(ids[:, None, :] == jnp.arange(cols)[None, :, None], axis=2)
    tiles = pattern[0, 0].reshape(-1, tile, tile).astype(jnp.bfloat16)
    own = tiles[order[:, None] * tile_src.shape[3] + slot]
    own = own.transpose(0, 2, 1, 3).reshape(LAYERS, 2, tile, cols * tile)
    flipped = jnp.flip(own, axis=1)

    by_x = swap(own, "col", 2)
    by_y = swap(flipped, "row", 1)
    by_core = swap(own, "col", 1)

    packed = levels.astype(jnp.float32) * 8.0 + jnp.where(
        levels == 0, paths_in, jnp.where(levels == 3, 1.0 + dep_in, 0.0)
    )
    pieces = packed.T.reshape(GROUP, share, vert)[by_place].reshape(2, 2, 2, share, vert)
    pieces = exchange(pieces).reshape(GROUP, share, vert)

    def by_vertex(values):
        return values.transpose(1, 0, 2).reshape(share, GROUP * vert)

    pieces = pieces.reshape(2, cols, share, vert)[:, col ^ jnp.arange(cols)]
    word = by_vertex(pieces.reshape(GROUP, share, vert))
    level = jnp.floor(word * 0.125)
    value = word - 8.0 * level
    masks = [(level == distance).astype(jnp.float32) for distance in range(4)]

    def placed(into, block, at_y, c):
        return lax.dynamic_update_slice(into, block[:, :, None], (0, at_y, c, 0, 0))

    cross_y = swap(by_x[:, :1], "row", 1)
    cross_x = swap(by_y[:, :1], "col", 2)
    empty = jnp.zeros((LAYERS, 2, cols, tile, cols * tile), jnp.bfloat16)
    near = placed(placed(empty, own, 0, col), by_core, 0, col ^ 1)
    near = placed(placed(near, by_x, 0, col ^ 2), swap(by_x, "col", 1), 0, col ^ 3)
    far = placed(placed(empty, by_y, 0, col), swap(by_y, "col", 1), 0, col ^ 1)
    far = placed(placed(far, cross_x, 0, col ^ 2), cross_y, 1, col ^ 2)
    far = placed(placed(far, swap(cross_x, "col", 1), 0, col ^ 3), swap(cross_y, "col", 1), 1, col ^ 3)
    span = GROUP * vert
    near, far = (half.reshape(LAYERS * span, cols * tile) for half in (near, far))

    def forward(front):
        front = front.astype(jnp.bfloat16)
        dims = (((1,), (1,)), ((), ()))
        return lax.dot_general(
            front[:, : cols * vert], near, dims, preferred_element_type=jnp.float32
        ) + lax.dot_general(front[:, cols * vert :], far, dims, preferred_element_type=jnp.float32)

    def backward(weights):
        dims = (((1,), (0,)), ((), ()))
        return jnp.concatenate(
            [
                lax.dot_general(weights, half, dims, preferred_element_type=jnp.float32)
                for half in (near, far)
            ],
            axis=1,
        )

    def across(value):
        return [swap(value[k], "row", 2 * k) for k in range(1, LAYERS)]

    counts = [masks[0] * value]
    for distance in (1, 2, 3):
        terms = forward(counts[-1])
        terms = [terms[:, k * span : (k + 1) * span] for k in range(LAYERS)]
        total = terms[0]
        for got in across([coded(t) for t in terms]):
            total = total + decoded(got)
        counts.append(masks[distance] * total)
    weight = (masks[3] * value / jnp.maximum(counts[3], 1.0)).astype(jnp.bfloat16)
    found = jnp.zeros_like(value)
    for distance in (2, 1, 0):
        gathered = jnp.concatenate([weight] + across([weight] * LAYERS), axis=1)
        back = backward(gathered)
        if distance > 0:
            delta = masks[distance] * counts[distance] * back
            found = found + delta
            weight = (
                masks[distance] * (1.0 + delta) / jnp.maximum(counts[distance], 1.0)
            ).astype(jnp.bfloat16)
        else:
            found = found + masks[0] * back

    found = found.reshape(share, 2, cols, vert).transpose(1, 2, 0, 3)[:, col ^ jnp.arange(cols)]
    home = exchange(found.reshape(2, 2, 2, share, vert)).reshape(GROUP, share, vert)[by_place]
    home = home.reshape(sources, vert).T
    return jnp.where(levels == 0, paths_in * home, home)


def solution(mesh):
    placed = (
        P(("row", "col"), None),
        P(("row", "col"), None),
        P(("row", "col"), None),
        P("row", "col", None, None),
        P("row", "col", None, None, None, None),
    )

    def shards(paths_in, dep_in, levels, tile_src, pattern):
        rows, cols = lax.axis_size("row"), lax.axis_size("col")
        fits = (
            rows == 2 * LAYERS
            and 2 * cols == GROUP
            and paths_in.shape[0] == pattern.shape[-1]
            and tile_src.shape[3] == cols
            and paths_in.shape[1] % GROUP == 0
        )
        chosen = split_shards if fits else general_shards
        return chosen(paths_in, dep_in, levels, tile_src, pattern)

    return jax.shard_map(
        shards, mesh=mesh, in_specs=placed, out_specs=P(("row", "col"), None), check_vma=False
    )
```

time: 417 us -> 186 us (0.45)
  waiting for transfers between devices: 254 us -> 63.2 us
  blocking collectives: 113 us -> 0 us
  starting transfers between devices: 0.21 us -> 38.7 us
  local copies, waits for them, and re-layouts: 9.42 us -> 39.1 us
  matrix products: 13.4 us -> 39 us
  between operations: 13.6 us -> 0.49 us
  other arithmetic: 13.3 us -> 4.62 us
    reduce_scatter x6 -> x0, waiting for transfers between devices: 253 us -> none  [the longest x3 189 us: scattered(): lax.psum_scatter(dest_terms(jnp.int32(0), vert_dev * lax.axis_size('row')...]
    all_gather x6 -> x0, blocking collectives: 113 us -> none  [the longest x3 94.5 us: spread(): return lax.all_gather(weight, 'row', axis=0, tiled=True)]
    ppermute x0 -> x33, waiting for transfers between devices: none -> 63.2 us  [swap(): return lax.ppermute(value, axis, partner(axis, bit))]
    ppermute x0 -> x33, starting transfers between devices: none -> 38.7 us  [swap(): return lax.ppermute(value, axis, partner(axis, bit))]
    dot_general x6 -> x12, matrix products: 13.4 us -> 39 us  [the longest x6 18 us: backward(): lax.dot_general(weights, half, dims, preferred_element_type=jnp.float32)]
    broadcast_in_dim x0 -> x12, local copies, waits for them, and re-layouts: none -> 18.3 us  [the longest x9 13.2 us: placed(): return lax.dynamic_update_slice(into, block[:, :, None], (0, at_y, c, 0, 0))]
    dynamic_update_slice x0 -> x10, local copies, waits for them, and re-layouts: none -> 10 us  [placed(): return lax.dynamic_update_slice(into, block[:, :, None], (0, at_y, c, 0, 0))]
    convert_element_type x7 -> x10, other arithmetic: 9.32 us -> 3.75 us  [the longest x1 1.83 us: split_shards(): tiles = pattern[0, 0].reshape(-1, tile, tile).astype(jnp.bfloat16)]
  transfers between devices with their start and end apart: 6 -> 33, of which waited for: 6 -> 21; matrix products, arithmetic and copies ran while one was open for 1% -> 15% of each run, Pallas kernels for 0% -> 0%
where the time goes in v1:
time: 186 us; the launch traced here: 185 us
  waiting for transfers between devices  63.2 us (34%)
  local copies, waits for them, and re-layouts  39.1 us (21%)
  matrix products  39 us (21%)
  starting transfers between devices  38.7 us (21%)
  other arithmetic  4.62 us (2%)
    ppermute x33, waiting for transfers between devices, swap(): return lax.ppermute(value, axis, partner(axis, bit))  63.2 us
    ppermute x33, starting transfers between devices, swap(): return lax.ppermute(value, axis, partner(axis, bit))  38.7 us
    dot_general x6, matrix products, backward(): lax.dot_general(weights, half, dims, preferred_element_type=jnp.float32)  18 us
    broadcast_in_dim x9, local copies, waits for them, and re-layouts, placed(): return lax.dynamic_update_slice(into, block[:, :, None], (0, at_y, c, 0, 0))  13.2 us
    dot_general x3, matrix products, forward(): lax.dot_general(front[:, :cols * vert], near, dims, preferred_element_typ...  10.5 us
    dot_general x3, matrix products, forward(): lax.dot_general(front[:, cols * vert:], far, dims, preferred_element_type...  10.5 us
    dynamic_update_slice x10, local copies, waits for them, and re-layouts, placed(): return lax.dynamic_update_slice(into, block[:, :, None], (0, at_y, c, 0, 0))  10 us
    broadcast_in_dim x2, local copies, waits for them, and re-layouts, split_shards(): empty = jnp.zeros((LAYERS, 2, cols, tile, cols * tile), jnp.bfloat16)  4.96 us
  transfers between devices with their start and end apart: 33, of which 21 were waited for; matrix products, arithmetic and copies ran while one was open for 15% of the time, Pallas kernels for 0%

profile of v1, /device:TPU:0, one launch (start us, length us, event | category | flops | bytes accessed | tf_op | source)
XLA Modules:
  0.0 185.1 jit_solution(6084049277739173682)
XLA Ops:
  2.4 1.8 convert_element_type.141
  5.8 3.1 %collective-permute-start.6 = (bf16[4,2,128,512]{2,3,1,0:T(8,128)(2,1)S(1)}, bf16[4,2,128,512]{2,3,1,0:T(8,128)(2,1)}, u32[]{:S(2)}, u32[]{:S(2)}) collective-permute-start(bf16[4,2,128,512]{2,3,1,0:T(8,128)(2,1)S(1)} %rev.4), channel_id=1, source_target_pairs={{0,4},{4,0},{8,12},{12,8},{16,20},{20,16},{24,28},{28,24},{1,5},{5... | collective-permute-start | bytes 3145736 | tf_op jit(solution)/shard_map/ppermute | solution.py:73
  8.8 1.5 collective-permute-start.4
  13.2 21.6 %collective-permute-done.1 = f32[2,1,2,32,128]{4,3,2,1,0:T(8,128)S(1)} collective-permute-done((f32[2,1,2,32,128]{4,3,2,1,0:T(8,128)S(1)}, f32[2,1,2,32,128]{4,3,2,1,0:T(8,128)S(1)}, u32[]{:S(2)}, u32[]{:S(2)}) %collective-permute-start.1) | collective-permute-done | bytes 65568 | tf_op jit(solution)/shard_map/ppermute | solution.py:73
  35.3 1.9 %slice.148 = bf16[4,1,128,512]{2,3,1,0:T(8,128)(2,1)} slice(bf16[4,2,128,512]{2,3,1,0:T(8,128)(2,1)} %collective-permute-done.6), slice={[0:4], [0:1], [0:128], [0:512]} | slice | bytes 1048576 | tf_op jit(solution)/shard_map/slice | solution.py:144
  37.2 1.6 collective-permute-start.8
  38.8 1.9 %slice.149 = bf16[4,1,128,512]{2,3,1,0:T(8,128)(2,1)} slice(bf16[4,2,128,512]{2,3,1,0:T(8,128)(2,1)} %collective-permute-done.4), slice={[0:4], [0:1], [0:128], [0:512]} | slice | bytes 1048576 | tf_op jit(solution)/shard_map/slice | solution.py:143
  40.7 1.5 collective-permute-start.9
  43.3 2.5 %broadcast_in_dim.66.clone.1 = bf16[4,2,4,128,512]{4,3,2,1,0:T(8,128)(2,1)} broadcast(bf16[]{:T(256)} %constant.84.clone.1), dimensions={} | broadcast | bytes 4194306 | tf_op jit(solution)/shard_map/broadcast_in_dim | solution.py:145
  47.5 2.6 %collective-permute-done.8 = bf16[4,1,128,512]{2,3,1,0:T(8,128)(2,1)} collective-permute-done((bf16[4,1,128,512]{2,3,1,0:T(8,128)(2,1)}, bf16[4,1,128,512]{2,3,1,0:T(8,128)(2,1)}, u32[]{:S(2)}, u32[]{:S(2)}) %collective-permute-start.8) | collective-permute-done | bytes 524320 | tf_op jit(solution)/shard_map/ppermute | solution.py:73
  50.1 2.9 %collective-permute-done.9 = bf16[4,1,128,512]{2,3,1,0:T(8,128)(2,1)} collective-permute-done((bf16[4,1,128,512]{2,3,1,0:T(8,128)(2,1)}, bf16[4,1,128,512]{2,3,1,0:T(8,128)(2,1)}, u32[]{:S(2)}, u32[]{:S(2)}) %collective-permute-start.9) | collective-permute-done | bytes 524320 | tf_op jit(solution)/shard_map/ppermute | solution.py:73
  57.2 2.4 %broadcast_in_dim.66.clone = bf16[4,2,4,128,512]{4,3,2,1,0:T(8,128)(2,1)} broadcast(bf16[]{:T(256)} %constant.84.clone.1), dimensions={} | broadcast | bytes 4194306 | tf_op jit(solution)/shard_map/broadcast_in_dim | solution.py:145
  65.6 1.5 copy.68
  67.1 2.0 %copy.71 = bf16[4,1,1,128,512]{4,3,2,1,0:T(8,128)(2,1)} copy(bf16[4,1,1,128,512]{3,4,0,2,1:T(8,128)(2,1)} %bitcast.25) | data formatting | bytes 1048576 | tf_op jit(solution)/shard_map/broadcast_in_dim | solution.py:141
  69.1 2.0 %copy.72 = bf16[4,1,1,128,512]{4,3,2,1,0:T(8,128)(2,1)} copy(bf16[4,1,1,128,512]{3,4,0,2,1:T(8,128)(2,1)} %bitcast.26) | data formatting | bytes 1048576 | tf_op jit(solution)/shard_map/broadcast_in_dim | solution.py:141
  71.2 1.7 copy.66
  77.3 3.5 %fusion.33 = f32[32,4096]{1,0:T(8,128)S(1)} fusion(bf16[4096,512]{1,0:T(8,128)(2,1)} %bitcast.27, bf16[32,1024]{1,0:T(8,128)(2,1)S(1)} %copy-done.2), kind=kOutput, calls=%fused_computation.92 | convolution fusion | flops 134217728 | bytes 4751360 | tf_op jit(solution)/shard_map/dot_general | solution.py:159
  81.9 3.5 %convolution_add_fusion.2 = f32[32,4096]{1,0:T(8,128)S(1)} fusion(f32[32,4096]{1,0:T(8,128)S(1)} %fusion.33, bf16[4096,512]{1,0:T(8,128)(2,1)} %bitcast.20, bf16[32,1024]{1,0:T(8,128)(2,1)S(1)} %copy-done.2), kind=kOutput, calls=%fused_computation.8 | convolution fusion | flops 134348800 | bytes 5275648 | tf_op jit(solution)/shard_map/dot_general | solution.py:157
  85.6 1.6 collective-permute-start.12
  87.3 2.6 %collective-permute-start.13 = (u16[32,1024]{1,0:T(8,128)(2,1)S(1)}, u16[32,1024]{1,0:T(8,128)(2,1)S(1)}, u32[]{:S(2)}, u32[]{:S(2)}) collective-permute-start(u16[32,1024]{1,0:T(8,128)(2,1)S(1)} %get-tuple-element.19), channel_id=1, source_target_pairs={{0,16},{4,20},{8,24},{12,28},{16,0},{20,4},{24,8},{28,12},{1,17},{... | collective-permute-start | bytes 196616 | tf_op jit(solution)/shard_map/ppermute | solution.py:73
  90.1 4.8 %collective-permute-done.13 = u16[32,1024]{1,0:T(8,128)(2,1)S(1)} collective-permute-done((u16[32,1024]{1,0:T(8,128)(2,1)S(1)}, u16[32,1024]{1,0:T(8,128)(2,1)S(1)}, u32[]{:S(2)}, u32[]{:S(2)}) %collective-permute-start.13) | collective-permute-done | bytes 65568 | tf_op jit(solution)/shard_map/ppermute | solution.py:73
  96.1 3.5 %fusion.30 = f32[32,4096]{1,0:T(8,128)S(1)} fusion(bf16[4096,512]{1,0:T(8,128)(2,1)} %bitcast.27, bf16[32,1024]{1,0:T(8,128)(2,1)S(1)} %get-tuple-element.9), kind=kOutput, calls=%fused_computation.89 | convolution fusion | flops 134217728 | bytes 4751360 | tf_op jit(solution)/shard_map/dot_general | solution.py:159
  99.6 3.5 %convolution_add_fusion.1 = f32[32,4096]{1,0:T(8,128)S(1)} fusion(f32[32,4096]{1,0:T(8,128)S(1)} %fusion.30, bf16[4096,512]{1,0:T(8,128)(2,1)} %bitcast.20, bf16[32,1024]{1,0:T(8,128)(2,1)S(1)} %get-tuple-element.9), kind=kOutput, calls=%fused_computation.7 | convolution fusion | flops 134348800 | bytes 5275648 | tf_op jit(solution)/shard_map/dot_general | solution.py:157
  104.6 1.7 collective-permute-start.16
  107.8 3.8 %collective-permute-done.16 = u16[32,1024]{1,0:T(8,128)(2,1)S(1)} collective-permute-done((u16[32,1024]{1,0:T(8,128)(2,1)S(1)}, u16[32,1024]{1,0:T(8,128)(2,1)S(1)}, u32[]{:S(2)}, u32[]{:S(2)}) %collective-permute-start.16) | collective-permute-done | bytes 65568 | tf_op jit(solution)/shard_map/ppermute | solution.py:73
  112.7 3.5 %fusion.27 = f32[32,4096]{1,0:T(8,128)S(1)} fusion(bf16[4096,512]{1,0:T(8,128)(2,1)} %bitcast.27, bf16[32,1024]{1,0:T(8,128)(2,1)S(1)} %get-tuple-element.7), kind=kOutput, calls=%fused_computation.86 | convolution fusion | flops 134217728 | bytes 4751360 | tf_op jit(solution)/shard_map/dot_general | solution.py:159
  116.2 3.5 %convolution_add_fusion = f32[32,4096]{1,0:T(8,128)S(1)} fusion(f32[32,4096]{1,0:T(8,128)S(1)} %fusion.27, bf16[4096,512]{1,0:T(8,128)(2,1)} %bitcast.20, bf16[32,1024]{1,0:T(8,128)(2,1)S(1)} %get-tuple-element.7), kind=kOutput, calls=%fused_computation.6 | convolution fusion | flops 134348800 | bytes 5275648 | tf_op jit(solution)/shard_map/dot_general | solution.py:157
  122.2 2.1 %collective-permute-start.20 = (u16[32,1024]{1,0:T(8,128)(2,1)S(1)}, u16[32,1024]{1,0:T(8,128)(2,1)S(1)}, u32[]{:S(2)}, u32[]{:S(2)}) collective-permute-start(u16[32,1024]{1,0:T(8,128)(2,1)S(1)} %get-tuple-element.12), channel_id=1, source_target_pairs={{0,24},{4,28},{8,16},{12,20},{16,8},{20,12},{24,0},{28,4},{1,25},{... | collective-permute-start | bytes 196616 | tf_op jit(solution)/shard_map/ppermute | solution.py:73
  125.1 1.7 collective-permute-done.19
  126.8 1.5 collective-permute-done.20
  128.6 2.8 %collective-permute-start.22 = (bf16[32,1024]{1,0:T(8,128)(2,1)S(1)}, bf16[32,1024]{1,0:T(8,128)(2,1)S(1)}, u32[]{:S(2)}, u32[]{:S(2)}) collective-permute-start(bf16[32,1024]{1,0:T(8,128)(2,1)S(1)} %fusion.13), channel_id=1, source_target_pairs={{0,16},{4,20},{8,24},{12,28},{16,0},{20,4},{24,8},{28,12},{1,17},{... | collective-permute-start | bytes 196616 | tf_op jit(solution)/shard_map/ppermute | solution.py:73
  131.5 1.5 collective-permute-start.23
  133.9 3.7 %collective-permute-done.23 = bf16[32,1024]{1,0:T(8,128)(2,1)S(1)} collective-permute-done((bf16[32,1024]{1,0:T(8,128)(2,1)S(1)}, bf16[32,1024]{1,0:T(8,128)(2,1)S(1)}, u32[]{:S(2)}, u32[]{:S(2)}) %collective-permute-start.23) | collective-permute-done | bytes 65568 | tf_op jit(solution)/shard_map/ppermute | solution.py:73
  137.5 3.0 %fusion.26 = f32[32,512]{1,0:T(8,128)S(1)} fusion(bf16[4096,512]{1,0:T(8,128)(2,1)} %bitcast.20, bf16[32,1024]{1,0:T(8,128)(2,1)S(1)} %collective-permute-done.23, bf16[32,1024]{1,0:T(8,128)(2,1)S(1)} %collective-permute-done.22, bf16[32,1024]{1,0:T(8,128)(2,1)S(1)} %collective-permute-done.21, bf16[32,1024]{1,0:T(8,128)(2,1)S(1)} %fusion.13), kind=kOutput, calls=%fused_computation.85 | convolution fusion | flops 135266304 | bytes 4521984 | tf_op jit(solution)/shard_map/dot_general | solution.py:165
  140.5 3.0 %fusion.25 = f32[32,512]{1,0:T(8,128)S(1)} fusion(bf16[4096,512]{1,0:T(8,128)(2,1)} %bitcast.27, bf16[32,1024]{1,0:T(8,128)(2,1)S(1)} %collective-permute-done.23, bf16[32,1024]{1,0:T(8,128)(2,1)S(1)} %collective-permute-done.22, bf16[32,1024]{1,0:T(8,128)(2,1)S(1)} %collective-permute-done.21, bf16[32,1024]{1,0:T(8,128)(2,1)S(1)} %fusion.13), kind=kOutput, calls=%fused_computation.84 | convolution fusion | flops 135266304 | bytes 4521984 | tf_op jit(solution)/shard_map/dot_general | solution.py:165
  143.7 2.1 %collective-permute-start.25 = (bf16[32,1024]{1,0:T(8,128)(2,1)S(1)}, bf16[32,1024]{1,0:T(8,128)(2,1)S(1)}, u32[]{:S(2)}, u32[]{:S(2)}) collective-permute-start(bf16[32,1024]{1,0:T(8,128)(2,1)S(1)} %divide_convert_fusion.1), channel_id=1, source_target_pairs={{0,16},{4,20},{8,24},{12,28},{16,0},{20,4},{24,8},{28,12},{1,17},{... | collective-permute-start | bytes 196616 | tf_op jit(solution)/shard_map/ppermute | solution.py:73
  145.8 2.3 %collective-permute-start.26 = (bf16[32,1024]{1,0:T(8,128)(2,1)S(1)}, bf16[32,1024]{1,0:T(8,128)(2,1)S(1)}, u32[]{:S(2)}, u32[]{:S(2)}) collective-permute-start(bf16[32,1024]{1,0:T(8,128)(2,1)S(1)} %divide_convert_fusion.1), channel_id=1, source_target_pairs={{0,24},{4,28},{8,16},{12,20},{16,8},{20,12},{24,0},{28,4},{1,25},{... | collective-permute-start | bytes 196616 | tf_op jit(solution)/shard_map/ppermute | solution.py:73
  148.9 2.9 %collective-permute-done.26 = bf16[32,1024]{1,0:T(8,128)(2,1)S(1)} collective-permute-done((bf16[32,1024]{1,0:T(8,128)(2,1)S(1)}, bf16[32,1024]{1,0:T(8,128)(2,1)S(1)}, u32[]{:S(2)}, u32[]{:S(2)}) %collective-permute-start.26) | collective-permute-done | bytes 65568 | tf_op jit(solution)/shard_map/ppermute | solution.py:73
  151.8 3.0 %fusion.24 = f32[32,512]{1,0:T(8,128)S(1)} fusion(bf16[4096,512]{1,0:T(8,128)(2,1)} %bitcast.20, bf16[32,1024]{1,0:T(8,128)(2,1)S(1)} %collective-permute-done.26, bf16[32,1024]{1,0:T(8,128)(2,1)S(1)} %collective-permute-done.25, bf16[32,1024]{1,0:T(8,128)(2,1)S(1)} %collective-permute-done.24, bf16[32,1024]{1,0:T(8,128)(2,1)S(1)} %divide_convert_fusion.1), kind=kOutput, calls=%fused_computation.83 | convolution fusion | flops 135266304 | bytes 4521984 | tf_op jit(solution)/shard_map/dot_general | solution.py:165
  154.8 3.0 %fusion.23 = f32[32,512]{1,0:T(8,128)S(1)} fusion(bf16[4096,512]{1,0:T(8,128)(2,1)} %bitcast.27, bf16[32,1024]{1,0:T(8,128)(2,1)S(1)} %collective-permute-done.26, bf16[32,1024]{1,0:T(8,128)(2,1)S(1)} %collective-permute-done.25, bf16[32,1024]{1,0:T(8,128)(2,1)S(1)} %collective-permute-done.24, bf16[32,1024]{1,0:T(8,128)(2,1)S(1)} %divide_convert_fusion.1), kind=kOutput, calls=%fused_computation.82 | convolution fusion | flops 135266304 | bytes 4521984 | tf_op jit(solution)/shard_map/dot_general | solution.py:165
  158.0 2.8 %collective-permute-start.28 = (bf16[32,1024]{1,0:T(8,128)(2,1)S(1)}, bf16[32,1024]{1,0:T(8,128)(2,1)S(1)}, u32[]{:S(2)}, u32[]{:S(2)}) collective-permute-start(bf16[32,1024]{1,0:T(8,128)(2,1)S(1)} %divide_convert_fusion), channel_id=1, source_target_pairs={{0,16},{4,20},{8,24},{12,28},{16,0},{20,4},{24,8},{28,12},{1,17},{... | collective-permute-start | bytes 196616 | tf_op jit(solution)/shard_map/ppermute | solution.py:73
  160.8 1.5 collective-permute-start.29
  163.2 3.7 %collective-permute-done.29 = bf16[32,1024]{1,0:T(8,128)(2,1)S(1)} collective-permute-done((bf16[32,1024]{1,0:T(8,128)(2,1)S(1)}, bf16[32,1024]{1,0:T(8,128)(2,1)S(1)}, u32[]{:S(2)}, u32[]{:S(2)}) %collective-permute-start.29) | collective-permute-done | bytes 65568 | tf_op jit(solution)/shard_map/ppermute | solution.py:73
  166.9 3.0 %fusion.22 = f32[32,512]{1,0:T(8,128)S(1)} fusion(bf16[4096,512]{1,0:T(8,128)(2,1)} %bitcast.20, bf16[32,1024]{1,0:T(8,128)(2,1)S(1)} %collective-permute-done.29, bf16[32,1024]{1,0:T(8,128)(2,1)S(1)} %collective-permute-done.28, bf16[32,1024]{1,0:T(8,128)(2,1)S(1)} %collective-permute-done.27, bf16[32,1024]{1,0:T(8,128)(2,1)S(1)} %divide_convert_fusion), kind=kOutput, calls=%fused_computation.81 | convolution fusion | flops 135266304 | bytes 4521984 | tf_op jit(solution)/shard_map/dot_general | solution.py:165
  169.9 3.0 %fusion.21 = f32[32,512]{1,0:T(8,128)S(1)} fusion(bf16[4096,512]{1,0:T(8,128)(2,1)} %bitcast.27, bf16[32,1024]{1,0:T(8,128)(2,1)S(1)} %collective-permute-done.29, bf16[32,1024]{1,0:T(8,128)(2,1)S(1)} %collective-permute-done.28, bf16[32,1024]{1,0:T(8,128)(2,1)S(1)} %collective-permute-done.27, bf16[32,1024]{1,0:T(8,128)(2,1)S(1)} %divide_convert_fusion), kind=kOutput, calls=%fused_computation.80 | convolution fusion | flops 135266304 | bytes 4521984 | tf_op jit(solution)/shard_map/dot_general | solution.py:165
  175.5 3.8 %collective-permute-done.31 = f32[2,1,2,32,128]{4,3,0,2,1:T(8,128)S(1)} collective-permute-done((f32[2,1,2,32,128]{4,3,0,2,1:T(8,128)S(1)}, f32[2,1,2,32,128]{4,3,0,2,1:T(8,128)S(1)}, u32[]{:S(2)}, u32[]{:S(2)}) %collective-permute-start.31) | collective-permute-done | bytes 65568 | tf_op jit(solution)/shard_map/ppermute | solution.py:73
  179.3 1.6 collective-permute-start.32
  180.9 2.7 %collective-permute-done.32 = f32[1,2,2,32,128]{4,3,0,2,1:T(8,128)S(1)} collective-permute-done((f32[1,2,2,32,128]{4,3,0,2,1:T(8,128)S(1)}, f32[1,2,2,32,128]{4,3,0,2,1:T(8,128)S(1)}, u32[]{:S(2)}, u32[]{:S(2)}) %collective-permute-start.32) | collective-permute-done | bytes 65568 | tf_op jit(solution)/shard_map/ppermute | solution.py:73
  (120 shorter events, 41.5 us)
Async XLA Ops:
  2.4 7.9 %copy-start.3 = (s32[128,256]{1,0:T(8,128)S(1)}, s32[128,256]{1,0:T(8,128)}, u32[]{:S(2)}) copy-start(s32[128,256]{1,0:T(8,128)} %param.7) | copy-start | bytes 393220
  2.4 8.0 %copy-start.4 = (f32[128,256]{1,0:T(8,128)S(1)}, f32[128,256]{1,0:T(8,128)}, u32[]{:S(2)}) copy-start(f32[128,256]{1,0:T(8,128)} %param.5) | copy-start | bytes 393220
  4.3 6.3 %copy-start.5 = (f32[128,256]{1,0:T(8,128)S(1)}, f32[128,256]{1,0:T(8,128)}, u32[]{:S(2)}) copy-start(f32[128,256]{1,0:T(8,128)} %param.6) | copy-start | bytes 393220
  5.8 29.5 %collective-permute-start.6 = (bf16[4,2,128,512]{2,3,1,0:T(8,128)(2,1)S(1)}, bf16[4,2,128,512]{2,3,1,0:T(8,128)(2,1)}, u32[]{:S(2)}, u32[]{:S(2)}) collective-permute-start(bf16[4,2,128,512]{2,3,1,0:T(8,128)(2,1)S(1)} %rev.4), channel_id=1, source_target_pairs={{0,4},{4,0},{8,12},{12,8},{16,20},{20,16},{24,28},{28,24},{1,5},{5... | collective-permute-start | bytes 3145736 | tf_op jit(solution)/shard_map/ppermute | solution.py:73
  8.8 30.0 %collective-permute-start.4 = (bf16[4,2,128,512]{2,3,1,0:T(8,128)(2,1)S(1)}, bf16[4,2,128,512]{2,3,1,0:T(8,128)(2,1)}, u32[]{:S(2)}, u32[]{:S(2)}) collective-permute-start(bf16[4,2,128,512]{2,3,1,0:T(8,128)(2,1)S(1)} %bitcast.96), channel_id=1, source_target_pairs={{0,2},{1,3},{2,0},{3,1},{4,6},{5,7},{6,4},{7,5},{8,10},{9,11},{10,... | collective-permute-start | bytes 3145736 | tf_op jit(solution)/shard_map/ppermute | solution.py:73
  11.3 1.3 collective-permute-start
  11.4 43.8 %collective-permute-start.3 = (bf16[4,2,128,512]{2,3,1,0:T(8,128)(2,1)S(1)}, bf16[4,2,128,512]{2,3,1,0:T(8,128)(2,1)S(1)}, u32[]{:S(2)}, u32[]{:S(2)}) collective-permute-start(bf16[4,2,128,512]{2,3,1,0:T(8,128)(2,1)S(1)} %bitcast.97), channel_id=1, source_target_pairs={{0,1},{1,0},{2,3},{3,2},{4,5},{5,4},{6,7},{7,6},{8,9},{9,8},{10,11... | collective-permute-start | bytes 3145736 | tf_op jit(solution)/shard_map/ppermute | solution.py:73
  12.6 22.2 %collective-permute-start.1 = (f32[2,1,2,32,128]{4,3,2,1,0:T(8,128)S(1)}, f32[2,1,2,32,128]{4,3,2,1,0:T(8,128)S(1)}, u32[]{:S(2)}, u32[]{:S(2)}) collective-permute-start(f32[2,1,2,32,128]{4,3,2,1,0:T(8,128)S(1)} %get-tuple-element.29), channel_id=1, source_target_pairs={{0,2},{1,3},{2,0},{3,1},{4,6},{5,7},{6,4},{7,5},{8,10},{9,11},{10,... | collective-permute-start | bytes 196616 | tf_op jit(solution)/shard_map/ppermute | solution.py:73
  34.9 7.3 %collective-permute-start.2 = (f32[1,2,2,32,128]{4,3,2,1,0:T(8,128)S(1)}, f32[1,2,2,32,128]{4,3,2,1,0:T(8,128)S(1)}, u32[]{:S(2)}, u32[]{:S(2)}) collective-permute-start(f32[1,2,2,32,128]{4,3,2,1,0:T(8,128)S(1)} %get-tuple-element.27), channel_id=1, source_target_pairs={{0,4},{4,0},{8,12},{12,8},{16,20},{20,16},{24,28},{28,24},{1,5},{5... | collective-permute-start | bytes 196616 | tf_op jit(solution)/shard_map/ppermute | solution.py:73
  37.2 12.9 %collective-permute-start.8 = (bf16[4,1,128,512]{2,3,1,0:T(8,128)(2,1)}, bf16[4,1,128,512]{2,3,1,0:T(8,128)(2,1)}, u32[]{:S(2)}, u32[]{:S(2)}) collective-permute-start(bf16[4,1,128,512]{2,3,1,0:T(8,128)(2,1)} %slice.148), channel_id=1, source_target_pairs={{0,2},{1,3},{2,0},{3,1},{4,6},{5,7},{6,4},{7,5},{8,10},{9,11},{10,... | collective-permute-start | bytes 1572872 | tf_op jit(solution)/shard_map/ppermute | solution.py:73
  40.7 12.4 %collective-permute-start.9 = (bf16[4,1,128,512]{2,3,1,0:T(8,128)(2,1)}, bf16[4,1,128,512]{2,3,1,0:T(8,128)(2,1)}, u32[]{:S(2)}, u32[]{:S(2)}) collective-permute-start(bf16[4,1,128,512]{2,3,1,0:T(8,128)(2,1)} %slice.149), channel_id=1, source_target_pairs={{0,4},{4,0},{8,12},{12,8},{16,20},{20,16},{24,28},{28,24},{1,5},{5... | collective-permute-start | bytes 1572872 | tf_op jit(solution)/shard_map/ppermute | solution.py:73
  42.2 23.4 %collective-permute-start.7 = (bf16[4,2,128,512]{2,3,1,0:T(8,128)(2,1)}, bf16[4,2,128,512]{2,3,1,0:T(8,128)(2,1)}, u32[]{:S(2)}, u32[]{:S(2)}) collective-permute-start(bf16[4,2,128,512]{2,3,1,0:T(8,128)(2,1)} %collective-permute-done.6), channel_id=1, source_target_pairs={{0,1},{1,0},{2,3},{3,2},{4,5},{5,4},{6,7},{7,6},{8,9},{9,8},{10,11... | collective-permute-start | bytes 3145736 | tf_op jit(solution)/shard_map/ppermute | solution.py:73
  42.2 29.0 %collective-permute-start.5 = (bf16[4,2,128,512]{2,3,1,0:T(8,128)(2,1)}, bf16[4,2,128,512]{2,3,1,0:T(8,128)(2,1)}, u32[]{:S(2)}, u32[]{:S(2)}) collective-permute-start(bf16[4,2,128,512]{2,3,1,0:T(8,128)(2,1)} %collective-permute-done.4), channel_id=1, source_target_pairs={{0,1},{1,0},{2,3},{3,2},{4,5},{5,4},{6,7},{7,6},{8,9},{9,8},{10,11... | collective-permute-start | bytes 3145736 | tf_op jit(solution)/shard_map/ppermute | solution.py:73
  50.1 17.0 %collective-permute-start.10 = (bf16[4,1,128,512]{2,3,1,0:T(8,128)(2,1)}, bf16[4,1,128,512]{2,3,1,0:T(8,128)(2,1)}, u32[]{:S(2)}, u32[]{:S(2)}) collective-permute-start(bf16[4,1,128,512]{2,3,1,0:T(8,128)(2,1)} %collective-permute-done.8), channel_id=1, source_target_pairs={{0,1},{1,0},{2,3},{3,2},{4,5},{5,4},{6,7},{7,6},{8,9},{9,8},{10,11... | collective-permute-start | bytes 1572872 | tf_op jit(solution)/shard_map/ppermute | solution.py:73
  53.1 16.1 %collective-permute-start.11 = (bf16[4,1,128,512]{2,3,1,0:T(8,128)(2,1)}, bf16[4,1,128,512]{2,3,1,0:T(8,128)(2,1)}, u32[]{:S(2)}, u32[]{:S(2)}) collective-permute-start(bf16[4,1,128,512]{2,3,1,0:T(8,128)(2,1)} %collective-permute-done.9), channel_id=1, source_target_pairs={{0,1},{1,0},{2,3},{3,2},{4,5},{5,4},{6,7},{7,6},{8,9},{9,8},{10,11... | collective-permute-start | bytes 1572872 | tf_op jit(solution)/shard_map/ppermute | solution.py:73
  72.8 2.8 %copy-start = (bf16[4,1,1,128,512]{4,3,2,1,0:T(8,128)(2,1)S(1)}, bf16[4,1,1,128,512]{4,3,2,1,0:T(8,128)(2,1)}, u32[]{:S(2)}) copy-start(bf16[4,1,1,128,512]{4,3,2,1,0:T(8,128)(2,1)} %copy.71) | copy-start | bytes 1572868
  72.8 3.6 %copy-start.1 = (bf16[4,1,1,128,512]{4,3,2,1,0:T(8,128)(2,1)S(1)}, bf16[4,1,1,128,512]{4,3,2,1,0:T(8,128)(2,1)}, u32[]{:S(2)}) copy-start(bf16[4,1,1,128,512]{4,3,2,1,0:T(8,128)(2,1)} %copy.72) | copy-start | bytes 1572868
  72.8 4.5 %copy-start.2 = (bf16[32,1024]{1,0:T(8,128)(2,1)S(1)}, bf16[32,1024]{1,0:T(8,128)(2,1)}, u32[]{:S(2)}) copy-start(bf16[32,1024]{1,0:T(8,128)(2,1)} %select_convert_fusion) | copy-start | bytes 196612
  85.6 4.5 %collective-permute-start.12 = (u16[32,1024]{1,0:T(8,128)(2,1)S(1)}, u16[32,1024]{1,0:T(8,128)(2,1)S(1)}, u32[]{:S(2)}, u32[]{:S(2)}) collective-permute-start(u16[32,1024]{1,0:T(8,128)(2,1)S(1)} %get-tuple-element.17), channel_id=1, source_target_pairs={{0,8},{4,12},{8,0},{12,4},{16,24},{20,28},{24,16},{28,20},{1,9},{5... | collective-permute-start | bytes 196616 | tf_op jit(solution)/shard_map/ppermute | solution.py:73
  87.3 7.7 %collective-permute-start.13 = (u16[32,1024]{1,0:T(8,128)(2,1)S(1)}, u16[32,1024]{1,0:T(8,128)(2,1)S(1)}, u32[]{:S(2)}, u32[]{:S(2)}) collective-permute-start(u16[32,1024]{1,0:T(8,128)(2,1)S(1)} %get-tuple-element.19), channel_id=1, source_target_pairs={{0,16},{4,20},{8,24},{12,28},{16,0},{20,4},{24,8},{28,12},{1,17},{... | collective-permute-start | bytes 196616 | tf_op jit(solution)/shard_map/ppermute | solution.py:73
  89.9 6.1 %collective-permute-start.14 = (u16[32,1024]{1,0:T(8,128)(2,1)S(1)}, u16[32,1024]{1,0:T(8,128)(2,1)S(1)}, u32[]{:S(2)}, u32[]{:S(2)}) collective-permute-start(u16[32,1024]{1,0:T(8,128)(2,1)S(1)} %get-tuple-element.18), channel_id=1, source_target_pairs={{0,24},{4,28},{8,16},{12,20},{16,8},{20,12},{24,0},{28,4},{1,25},{... | collective-permute-start | bytes 196616 | tf_op jit(solution)/shard_map/ppermute | solution.py:73
  103.3 4.5 %collective-permute-start.15 = (u16[32,1024]{1,0:T(8,128)(2,1)S(1)}, u16[32,1024]{1,0:T(8,128)(2,1)S(1)}, u32[]{:S(2)}, u32[]{:S(2)}) collective-permute-start(u16[32,1024]{1,0:T(8,128)(2,1)S(1)} %get-tuple-element.14), channel_id=1, source_target_pairs={{0,8},{4,12},{8,0},{12,4},{16,24},{20,28},{24,16},{28,20},{1,9},{5... | collective-permute-start | bytes 196616 | tf_op jit(solution)/shard_map/ppermute | solution.py:73
  104.6 6.9 %collective-permute-start.16 = (u16[32,1024]{1,0:T(8,128)(2,1)S(1)}, u16[32,1024]{1,0:T(8,128)(2,1)S(1)}, u32[]{:S(2)}, u32[]{:S(2)}) collective-permute-start(u16[32,1024]{1,0:T(8,128)(2,1)S(1)} %get-tuple-element.16), channel_id=1, source_target_pairs={{0,16},{4,20},{8,24},{12,28},{16,0},{20,4},{24,8},{28,12},{1,17},{... | collective-permute-start | bytes 196616 | tf_op jit(solution)/shard_map/ppermute | solution.py:73
  106.3 6.2 %collective-permute-start.17 = (u16[32,1024]{1,0:T(8,128)(2,1)S(1)}, u16[32,1024]{1,0:T(8,128)(2,1)S(1)}, u32[]{:S(2)}, u32[]{:S(2)}) collective-permute-start(u16[32,1024]{1,0:T(8,128)(2,1)S(1)} %get-tuple-element.15), channel_id=1, source_target_pairs={{0,24},{4,28},{8,16},{12,20},{16,8},{20,12},{24,0},{28,4},{1,25},{... | collective-permute-start | bytes 196616 | tf_op jit(solution)/shard_map/ppermute | solution.py:73
  119.9 5.2 %collective-permute-start.18 = (u16[32,1024]{1,0:T(8,128)(2,1)S(1)}, u16[32,1024]{1,0:T(8,128)(2,1)S(1)}, u32[]{:S(2)}, u32[]{:S(2)}) collective-permute-start(u16[32,1024]{1,0:T(8,128)(2,1)S(1)} %get-tuple-element.11), channel_id=1, source_target_pairs={{0,8},{4,12},{8,0},{12,4},{16,24},{20,28},{24,16},{28,20},{1,9},{5... | collective-permute-start | bytes 196616 | tf_op jit(solution)/shard_map/ppermute | solution.py:73
  120.9 5.9 %collective-permute-start.19 = (u16[32,1024]{1,0:T(8,128)(2,1)S(1)}, u16[32,1024]{1,0:T(8,128)(2,1)S(1)}, u32[]{:S(2)}, u32[]{:S(2)}) collective-permute-start(u16[32,1024]{1,0:T(8,128)(2,1)S(1)} %get-tuple-element.13), channel_id=1, source_target_pairs={{0,16},{4,20},{8,24},{12,28},{16,0},{20,4},{24,8},{28,12},{1,17},{... | collective-permute-start | bytes 196616 | tf_op jit(solution)/shard_map/ppermute | solution.py:73
  122.2 6.2 %collective-permute-start.20 = (u16[32,1024]{1,0:T(8,128)(2,1)S(1)}, u16[32,1024]{1,0:T(8,128)(2,1)S(1)}, u32[]{:S(2)}, u32[]{:S(2)}) collective-permute-start(u16[32,1024]{1,0:T(8,128)(2,1)S(1)} %get-tuple-element.12), channel_id=1, source_target_pairs={{0,24},{4,28},{8,16},{12,20},{16,8},{20,12},{24,0},{28,4},{1,25},{... | collective-permute-start | bytes 196616 | tf_op jit(solution)/shard_map/ppermute | solution.py:73
  128.6 4.5 %collective-permute-start.21 = (bf16[32,1024]{1,0:T(8,128)(2,1)S(1)}, bf16[32,1024]{1,0:T(8,128)(2,1)S(1)}, u32[]{:S(2)}, u32[]{:S(2)}) collective-permute-start(bf16[32,1024]{1,0:T(8,128)(2,1)S(1)} %fusion.13), channel_id=1, source_target_pairs={{0,8},{4,12},{8,0},{12,4},{16,24},{20,28},{24,16},{28,20},{1,9},{5... | collective-permute-start | bytes 196616 | tf_op jit(solution)/shard_map/ppermute | solution.py:73
  128.6 5.2 %collective-permute-start.22 = (bf16[32,1024]{1,0:T(8,128)(2,1)S(1)}, bf16[32,1024]{1,0:T(8,128)(2,1)S(1)}, u32[]{:S(2)}, u32[]{:S(2)}) collective-permute-start(bf16[32,1024]{1,0:T(8,128)(2,1)S(1)} %fusion.13), channel_id=1, source_target_pairs={{0,16},{4,20},{8,24},{12,28},{16,0},{20,4},{24,8},{28,12},{1,17},{... | collective-permute-start | bytes 196616 | tf_op jit(solution)/shard_map/ppermute | solution.py:73
  131.5 6.1 %collective-permute-start.23 = (bf16[32,1024]{1,0:T(8,128)(2,1)S(1)}, bf16[32,1024]{1,0:T(8,128)(2,1)S(1)}, u32[]{:S(2)}, u32[]{:S(2)}) collective-permute-start(bf16[32,1024]{1,0:T(8,128)(2,1)S(1)} %fusion.13), channel_id=1, source_target_pairs={{0,24},{4,28},{8,16},{12,20},{16,8},{20,12},{24,0},{28,4},{1,25},{... | collective-permute-start | bytes 196616 | tf_op jit(solution)/shard_map/ppermute | solution.py:73
  143.6 4.5 %collective-permute-start.24 = (bf16[32,1024]{1,0:T(8,128)(2,1)S(1)}, bf16[32,1024]{1,0:T(8,128)(2,1)S(1)}, u32[]{:S(2)}, u32[]{:S(2)}) collective-permute-start(bf16[32,1024]{1,0:T(8,128)(2,1)S(1)} %divide_convert_fusion.1), channel_id=1, source_target_pairs={{0,8},{4,12},{8,0},{12,4},{16,24},{20,28},{24,16},{28,20},{1,9},{5... | collective-permute-start | bytes 196616 | tf_op jit(solution)/shard_map/ppermute | solution.py:73
  143.7 5.2 %collective-permute-start.25 = (bf16[32,1024]{1,0:T(8,128)(2,1)S(1)}, bf16[32,1024]{1,0:T(8,128)(2,1)S(1)}, u32[]{:S(2)}, u32[]{:S(2)}) collective-permute-start(bf16[32,1024]{1,0:T(8,128)(2,1)S(1)} %divide_convert_fusion.1), channel_id=1, source_target_pairs={{0,16},{4,20},{8,24},{12,28},{16,0},{20,4},{24,8},{28,12},{1,17},{... | collective-permute-start | bytes 196616 | tf_op jit(solution)/shard_map/ppermute | solution.py:73
  145.8 6.1 %collective-permute-start.26 = (bf16[32,1024]{1,0:T(8,128)(2,1)S(1)}, bf16[32,1024]{1,0:T(8,128)(2,1)S(1)}, u32[]{:S(2)}, u32[]{:S(2)}) collective-permute-start(bf16[32,1024]{1,0:T(8,128)(2,1)S(1)} %divide_convert_fusion.1), channel_id=1, source_target_pairs={{0,24},{4,28},{8,16},{12,20},{16,8},{20,12},{24,0},{28,4},{1,25},{... | collective-permute-start | bytes 196616 | tf_op jit(solution)/shard_map/ppermute | solution.py:73
  157.9 4.5 %collective-permute-start.27 = (bf16[32,1024]{1,0:T(8,128)(2,1)S(1)}, bf16[32,1024]{1,0:T(8,128)(2,1)S(1)}, u32[]{:S(2)}, u32[]{:S(2)}) collective-permute-start(bf16[32,1024]{1,0:T(8,128)(2,1)S(1)} %divide_convert_fusion), channel_id=1, source_target_pairs={{0,8},{4,12},{8,0},{12,4},{16,24},{20,28},{24,16},{28,20},{1,9},{5... | collective-permute-start | bytes 196616 | tf_op jit(solution)/shard_map/ppermute | solution.py:73
  158.0 5.2 %collective-permute-start.28 = (bf16[32,1024]{1,0:T(8,128)(2,1)S(1)}, bf16[32,1024]{1,0:T(8,128)(2,1)S(1)}, u32[]{:S(2)}, u32[]{:S(2)}) collective-permute-start(bf16[32,1024]{1,0:T(8,128)(2,1)S(1)} %divide_convert_fusion), channel_id=1, source_target_pairs={{0,16},{4,20},{8,24},{12,28},{16,0},{20,4},{24,8},{28,12},{1,17},{... | collective-permute-start | bytes 196616 | tf_op jit(solution)/shard_map/ppermute | solution.py:73
  160.8 6.1 %collective-permute-start.29 = (bf16[32,1024]{1,0:T(8,128)(2,1)S(1)}, bf16[32,1024]{1,0:T(8,128)(2,1)S(1)}, u32[]{:S(2)}, u32[]{:S(2)}) collective-permute-start(bf16[32,1024]{1,0:T(8,128)(2,1)S(1)} %divide_convert_fusion), channel_id=1, source_target_pairs={{0,24},{4,28},{8,16},{12,20},{16,8},{20,12},{24,0},{28,4},{1,25},{... | collective-permute-start | bytes 196616 | tf_op jit(solution)/shard_map/ppermute | solution.py:73
  173.7 1.3 collective-permute-start.30
  175.0 4.3 %collective-permute-start.31 = (f32[2,1,2,32,128]{4,3,0,2,1:T(8,128)S(1)}, f32[2,1,2,32,128]{4,3,0,2,1:T(8,128)S(1)}, u32[]{:S(2)}, u32[]{:S(2)}) collective-permute-start(f32[2,1,2,32,128]{4,3,0,2,1:T(8,128)S(1)} %get-tuple-element.23), channel_id=1, source_target_pairs={{0,2},{1,3},{2,0},{3,1},{4,6},{5,7},{6,4},{7,5},{8,10},{9,11},{10,... | collective-permute-start | bytes 196616 | tf_op jit(solution)/shard_map/ppermute | solution.py:73
  179.3 4.3 %collective-permute-start.32 = (f32[1,2,2,32,128]{4,3,0,2,1:T(8,128)S(1)}, f32[1,2,2,32,128]{4,3,0,2,1:T(8,128)S(1)}, u32[]{:S(2)}, u32[]{:S(2)}) collective-permute-start(f32[1,2,2,32,128]{4,3,0,2,1:T(8,128)S(1)} %get-tuple-element.21), channel_id=1, source_target_pairs={{0,4},{4,0},{8,12},{12,8},{16,20},{20,16},{24,28},{28,24},{1,5},{5... | collective-permute-start | bytes 196616 | tf_op jit(solution)/shard_map/ppermute | solution.py:73

commit v2 on v0

v2 whole, which is shorter than its diff:
```python
import functools

import jax
import jax.numpy as jnp
from jax import lax
from jax.experimental import pallas as pl
from jax.experimental.pallas import tpu as pltpu
from jax.sharding import PartitionSpec as P


def general_shards(paths_in, dep_in, levels, tile_src, pattern):
    vert_dev = paths_in.shape[0]
    tile_size = pattern.shape[-1]
    dest_tiles = tile_src.shape[2]
    band_slots = tile_src.shape[3]
    src_tiles = lax.axis_size("col") * vert_dev // tile_size
    per_source = dest_tiles * band_slots // src_tiles
    source_ids = tile_src[0, 0]
    tile_values = pattern[0, 0].astype(jnp.bfloat16)
    flat_ids = source_ids.reshape(-1)
    by_source = jnp.argsort(flat_ids, stable=True)
    back_values = tile_values.reshape(-1, tile_size, tile_size)[by_source]
    back_values = back_values.reshape(src_tiles, per_source, tile_size, tile_size)
    back_dest = (by_source // band_slots).reshape(src_tiles, per_source)

    def forward_terms(frontier):
        gathered = lax.all_gather(frontier, "col", axis=0, tiled=True)
        pieces = gathered.reshape(src_tiles, tile_size, gathered.shape[1])
        product = jnp.einsum(
            "ibrj,ibjs->irs", tile_values, pieces[source_ids], preferred_element_type=jnp.float32
        )
        terms = product.reshape(vert_dev * lax.axis_size("row"), product.shape[2])
        return lax.psum_scatter(terms, "row", scatter_dimension=0, tiled=True)

    def spread(weight):
        return lax.all_gather(weight, "row", axis=0, tiled=True)

    level_masks = [(levels == distance).astype(jnp.float32) for distance in range(4)]
    path_counts = [level_masks[0] * paths_in]
    for distance in (1, 2, 3):
        path_counts.append(
            level_masks[distance] * forward_terms(path_counts[-1].astype(jnp.bfloat16))
        )
    numerator = level_masks[3] * (1.0 + dep_in)
    spread_weight = spread((numerator / jnp.maximum(path_counts[3], 1.0)).astype(jnp.bfloat16))
    dependency = jnp.zeros(paths_in.shape, jnp.float32)
    for distance in (2, 1, 0):
        backward_pieces = spread_weight.reshape(dest_tiles, tile_size, spread_weight.shape[1])
        source_product = jnp.einsum(
            "tgrj,tgrs->tjs",
            back_values,
            backward_pieces[back_dest],
            preferred_element_type=jnp.float32,
        )
        source_product = source_product.reshape(
            vert_dev * lax.axis_size("col"), source_product.shape[2]
        )
        dependence = (
            level_masks[distance]
            * path_counts[distance]
            * lax.psum_scatter(source_product, "col", scatter_dimension=0, tiled=True)
        )
        dependency = dependency + dependence
        if distance > 0:
            weight = (
                level_masks[distance] * (1.0 + dependence) / jnp.maximum(path_counts[distance], 1.0)
            ).astype(jnp.bfloat16)
            spread_weight = spread(weight)
    return dependency


def partner(axis, bit):
    return [(i, i ^ bit) for i in range(lax.axis_size(axis))]


def swap(value, axis, bit):
    return lax.ppermute(value, axis, partner(axis, bit))


def diagonal():
    cols = lax.axis_size("col")
    return [(i, i ^ cols ^ 2) for i in range(lax.axis_size("row") * cols)]


GROUP = 8
LAYERS = 4
LOWEST = 5
MANTISSA = 18
BYTE = 255


def coded(count):
    scaled = count * 2.0**LOWEST
    exponent = jnp.zeros_like(count)
    for bit in (32, 16, 8, 4, 2, 1):
        large = scaled >= 2.0**bit
        scaled = jnp.where(large, scaled * 2.0**-bit, scaled)
        exponent = exponent + jnp.where(large, float(bit), 0.0)
    mantissa = jnp.floor((scaled - 1.0) * 2.0**MANTISSA + 0.5)
    code = jnp.where(count > 0.0, exponent * 2.0**MANTISSA + mantissa, 0.0).astype(jnp.int32)
    *first, last = jnp.split(code, 4, axis=1)
    words = [part | (((last >> (8 * at)) & BYTE) << 24) for at, part in enumerate(first)]
    return jnp.concatenate(words, axis=1)


def decoded(words):
    words = jnp.split(words, 3, axis=1)
    last = sum(((word >> 24) & BYTE) << (8 * at) for at, word in enumerate(words))
    code = jnp.concatenate([word & (2**24 - 1) for word in words] + [last], axis=1)
    exponent = code >> MANTISSA
    mantissa = code & (2**MANTISSA - 1)
    count = mantissa.astype(jnp.float32) * 2.0 ** (-MANTISSA - LOWEST) + 2.0**-LOWEST
    for bit in (32, 16, 8, 4, 2, 1):
        count = jnp.where((exponent & bit) != 0, count * 2.0**bit, count)
    return jnp.where(code > 0, count, 0.0)


IN_VMEM = pl.BlockSpec(memory_space=pltpu.VMEM)
IN_SMEM = pl.BlockSpec(memory_space=pltpu.SMEM)


def pack_kernel(ids, pattern, *outs):
    cols = outs[0].shape[1]
    row = lax.axis_index("row")
    for y in range(2):
        for layer in range(LAYERS):
            i = row ^ (2 * layer + y)
            for t in range(cols):
                slot = jnp.int32(0)
                for e in range(1, cols):
                    slot = jnp.where(ids[e, i] == t, e, slot)
                outs[y][layer, t] = pattern[i * cols + slot].astype(jnp.float32).astype(jnp.bfloat16)


def packed_block(ids, pattern):
    cols, tile = ids.shape[0], pattern.shape[-1]
    half = jax.ShapeDtypeStruct((LAYERS, cols, tile, tile), jnp.bfloat16)
    return pl.pallas_call(
        pack_kernel,
        out_shape=[half] * 2,
        in_specs=[IN_SMEM, IN_VMEM],
        out_specs=[IN_VMEM] * 2,
        compiler_params=pltpu.CompilerParams(vmem_limit_bytes=8 * 1024 * 1024),
        name="pack",
    )(ids, pattern)


def inputs_kernel(paths_in, dep_in, levels, keep, send, words):
    level = levels[...]
    word = jnp.where(
        level == 0, -paths_in[...], jnp.where(level == 3, 1.0 + dep_in[...], 0.0)
    )
    word = jnp.where(level == 1, 0.5, jnp.where(level == 2, 0.25, word))
    words[...] = word.T
    share = keep.shape[-2]
    place = lax.axis_index("row") % 2 * lax.axis_size("col") + lax.axis_index("col")
    for out, core in ((keep, 0), (send, 1)):
        for at in range(GROUP // 2):
            rows = pl.multiple_of((place ^ (2 * at + core)) * share, share)
            out[at] = words[pl.ds(rows, share), :]


def packed_inputs(paths_in, dep_in, levels):
    vert, sources = paths_in.shape
    half = jax.ShapeDtypeStruct((GROUP // 2, sources // GROUP, vert), jnp.float32)
    return pl.pallas_call(
        inputs_kernel,
        out_shape=[half] * 2,
        in_specs=[IN_VMEM] * 3,
        out_specs=[IN_VMEM] * 2,
        scratch_shapes=[pltpu.VMEM((sources, vert), jnp.float32)],
        compiler_params=pltpu.CompilerParams(vmem_limit_bytes=4 * 1024 * 1024),
        name="inputs",
    )(paths_in, dep_in, levels)


def placed_kernel(*rest):
    pieces, word, front = rest[:-2], rest[-2], rest[-1]
    vert = pieces[0].shape[-1]
    col = lax.axis_index("col")
    for at in range(2 * len(pieces)):
        to = (at & 4) | ((at & 3) ^ col)
        piece = pieces[at // 2][at % 2]
        lanes = pl.ds(pl.multiple_of(to * vert, vert), vert)
        word[:, lanes] = piece
        front[:, lanes] = jnp.maximum(-piece, 0.0).astype(jnp.bfloat16)


def placed_inputs(pieces):
    _, share, vert = pieces[0].shape
    shape = (share, 2 * len(pieces) * vert)
    return pl.pallas_call(
        placed_kernel,
        out_shape=[jax.ShapeDtypeStruct(shape, kind) for kind in (jnp.float32, jnp.bfloat16)],
        in_specs=[IN_VMEM] * len(pieces),
        out_specs=[IN_VMEM] * 2,
        compiler_params=pltpu.CompilerParams(vmem_limit_bytes=4 * 1024 * 1024),
        name="placed",
    )(*pieces)


def rows_of(halves, layer):
    cols = halves[0].shape[1]
    return jnp.concatenate(
        [jnp.concatenate([half[layer, t] for t in range(cols)], axis=1) for half in halves], axis=0
    )


def first_kernel(base, front, *rest):
    outs = rest[-LAYERS:]
    start = rest[:LAYERS] if base else None
    halves = rest[LAYERS if base else 0 : -LAYERS]
    pairs = ((1, 2), (1, 3)) if base else tuple((at // 4, at % 4) for at in range(6))
    layers, cols, tile, _ = halves[0].shape
    wide = cols * tile
    col = lax.axis_index("col")
    for layer in range(layers):
        for flip in range(cols):
            terms = None
            for at, (side, c) in enumerate(pairs):
                if c == flip:
                    term = lax.dot_general(
                        front[:, side * wide : (side + 1) * wide],
                        rows_of(halves[2 * at : 2 * at + 2], layer),
                        (((1,), (1,)), ((), ())),
                        preferred_element_type=jnp.float32,
                    )
                    terms = term if terms is None else terms + term
            for y in range(2):
                lanes = pl.ds(pl.multiple_of((y * cols + (col ^ flip)) * tile, tile), tile)
                if terms is None:
                    outs[layer][:, lanes] = start[layer][:, lanes]
                    continue
                part = terms[:, y * tile : (y + 1) * tile]
                outs[layer][:, lanes] = part + start[layer][:, lanes] if base else part


def first_terms(front, base, halves):
    shape = jax.ShapeDtypeStruct(front.shape, jnp.float32)
    flops = 2 * front.shape[0] * len(halves) * halves[0].size
    return pl.pallas_call(
        functools.partial(first_kernel, bool(base)),
        out_shape=[shape] * LAYERS,
        in_specs=[IN_VMEM] * (1 + len(base) + len(halves)),
        out_specs=[IN_VMEM] * LAYERS,
        compiler_params=pltpu.CompilerParams(vmem_limit_bytes=12 * 1024 * 1024),
        cost_estimate=pl.CostEstimate(flops=flops, bytes_accessed=len(halves) * halves[0].size * 2, transcendentals=0),
        name="first",
    )(front, *base, *halves)


def assemble_kernel(count, *rest):
    blocks, outs = rest[:count], rest[count:]
    layers, cols, tile, _ = blocks[0].shape
    col = lax.axis_index("col")
    for layer in range(layers):
        for at, block in enumerate(blocks):
            side, flip, y = at // (2 * cols), at // 2 % cols, at % 2
            rows = pl.ds(pl.multiple_of((y * cols + (col ^ flip)) * tile, tile), tile)
            for t in range(cols):
                start = (side * cols + t) * tile
                outs[layer][rows, start : start + tile] = block[layer, t]


def assembled(near, far):
    layers, cols, tile, _ = near[0].shape
    span = 2 * cols * tile
    return pl.pallas_call(
        functools.partial(assemble_kernel, len(near + far)),
        out_shape=[jax.ShapeDtypeStruct((span, span), jnp.bfloat16)] * layers,
        in_specs=[IN_VMEM] * len(near + far),
        out_specs=[IN_VMEM] * layers,
        compiler_params=pltpu.CompilerParams(vmem_limit_bytes=20 * 1024 * 1024),
        cost_estimate=pl.CostEstimate(
            flops=0, bytes_accessed=4 * len(near + far) * near[0].size, transcendentals=0
        ),
        name="assemble",
    )(*near, *far)


def spread_kernel(found, keep, send):
    place = lax.axis_index("row") % 2 * lax.axis_size("col") + lax.axis_index("col")
    vert = keep.shape[-1]
    cols = lax.axis_size("col")
    for out, core in ((keep, 0), (send, 1)):
        for at in range(GROUP // 2):
            rel = 2 * at + core
            to = (rel & cols) | ((rel & (cols - 1)) ^ (place & (cols - 1)))
            out[at] = found[:, pl.ds(pl.multiple_of(to * vert, vert), vert)]


def spread_found(found):
    share, span = found.shape
    half = jax.ShapeDtypeStruct((GROUP // 2, share, span // GROUP), jnp.float32)
    return pl.pallas_call(
        spread_kernel,
        out_shape=[half] * 2,
        in_specs=[IN_VMEM],
        out_specs=[IN_VMEM] * 2,
        compiler_params=pltpu.CompilerParams(vmem_limit_bytes=4 * 1024 * 1024),
        name="spread",
    )(found)


def home_kernel(factor, *rest):
    pieces, out, words = rest[:-2], rest[-2], rest[-1]
    place = lax.axis_index("row") % 2 * lax.axis_size("col") + lax.axis_index("col")
    share = pieces[0].shape[-2]
    for at in range(2 * len(pieces)):
        rows = pl.multiple_of((place ^ at) * share, share)
        words[pl.ds(rows, share), :] = pieces[at // 2][at % 2]
    out[...] = words[...].T * factor[...]


def brought_home(factor, pieces):
    vert, sources = factor.shape
    return pl.pallas_call(
        home_kernel,
        out_shape=jax.ShapeDtypeStruct((vert, sources), jnp.float32),
        in_specs=[IN_VMEM] * (1 + len(pieces)),
        out_specs=IN_VMEM,
        scratch_shapes=[pltpu.VMEM((sources, vert), jnp.float32)],
        compiler_params=pltpu.CompilerParams(vmem_limit_bytes=4 * 1024 * 1024),
        name="home",
    )(factor, *pieces)


def traded(keep, send):
    got = swap(send, "col", 1)
    held = [jnp.stack([keep[at], got[at]]) for at in range(GROUP // 2)]
    from_y = swap(held[2], "row", 1)
    from_x = swap(held[1], "col", 2)
    from_d = lax.ppermute(held[3], ("row", "col"), diagonal())
    return [held[0], from_x, from_y, from_d]


def split_shards(paths_in, dep_in, levels, tile_src, pattern):
    vert, _ = paths_in.shape
    tile = pattern.shape[-1]

    own = packed_block(tile_src[0, 0].T, pattern[0, 0].reshape(-1, tile, tile))
    keep, send = packed_inputs(paths_in, dep_in, levels)
    pieces = traded(keep, send)
    by_y = [swap(own[1], "row", 1)]
    by_x = [swap(own[0], "col", 2)]
    by_core = [swap(half, "col", 1) for half in own]
    by_y.append(swap(own[0], "row", 1))
    by_x.append(swap(own[1], "col", 2))

    upper = jnp.where(levels == 0, paths_in, 1.0)[: vert // 2]
    lower = jnp.where(levels == 0, paths_in, 1.0)[vert // 2 :]
    upper, lower = lax.optimization_barrier((upper, lower))

    word, front = placed_inputs(pieces)
    masks = [word < 0.0, word == 0.5, word == 0.25, word >= 1.0]

    cross = [swap(by_y[0], "col", 2), swap(by_x[0], "row", 1)]
    crossed = [swap(by_x[0], "col", 1), swap(by_y[0], "col", 1)]
    crossed += [swap(by_x[1], "col", 1), swap(by_y[1], "col", 1)]
    near = list(own) + by_core + by_x + [crossed[0], crossed[2]]
    far = by_y + [crossed[1], crossed[3]]
    last = cross + [swap(half, "col", 1) for half in cross]
    first = first_terms(front, [], near + far)
    first = first_terms(front, first, last)
    whole = assembled(near, far + last)

    def forward(front, k):
        dims = (((1,), (1,)), ((), ()))
        return lax.dot_general(
            front.astype(jnp.bfloat16), whole[k], dims, preferred_element_type=jnp.float32
        )

    def across(value):
        return {k: swap(value(k), "row", 2 * k) for k in reversed(range(1, LAYERS))}

    counts = [None]
    for distance in (1, 2, 3):
        def terms(k):
            return first[k] if distance == 1 else forward(counts[-1], k)

        got = across(lambda k: coded(terms(k)))
        total = terms(0)
        for k in range(1, LAYERS):
            total = total + decoded(got[k])
        counts.append(jnp.where(masks[distance], total, 0.0))
    weight = (jnp.where(masks[3], word, 0.0) / jnp.maximum(counts[3], 1.0)).astype(jnp.bfloat16)
    found = jnp.zeros_like(word)
    for distance in (2, 1, 0):
        got = {0: weight} | across(lambda k: weight)
        back = sum(
            jnp.dot(got[k], whole[k], preferred_element_type=jnp.float32) for k in range(LAYERS)
        )
        if distance > 0:
            delta = counts[distance] * back
            found = found + delta
            weight = jnp.where(
                masks[distance], (1.0 + delta) / jnp.maximum(counts[distance], 1.0), 0.0
            ).astype(jnp.bfloat16)
        else:
            found = found + jnp.where(masks[0], back, 0.0)

    keep, send = spread_found(found)
    pieces = traded(keep, send)
    return brought_home(jnp.concatenate([upper, lower]), pieces)


def solution(mesh):
    placed = (
        P(("row", "col"), None),
        P(("row", "col"), None),
        P(("row", "col"), None),
        P("row", "col", None, None),
        P("row", "col", None, None, None, None),
    )

    def shards(paths_in, dep_in, levels, tile_src, pattern):
        rows, cols = lax.axis_size("row"), lax.axis_size("col")
        fits = (
            rows == 2 * LAYERS
            and 2 * cols == GROUP
            and paths_in.shape[0] == pattern.shape[-1]
            and tile_src.shape[3] == cols
            and paths_in.shape[1] % GROUP == 0
        )
        chosen = split_shards if fits else general_shards
        return chosen(paths_in, dep_in, levels, tile_src, pattern)

    return jax.shard_map(
        shards, mesh=mesh, in_specs=placed, out_specs=P(("row", "col"), None), check_vma=False
    )
```

time: 417 us -> 139 us (0.33)
  waiting for transfers between devices: 254 us -> 67.7 us
  blocking collectives: 113 us -> 0 us
  starting transfers between devices: 0.21 us -> 47.2 us
  between operations: 13.6 us -> 0.5 us
  other arithmetic: 13.3 us -> 1.47 us
  local copies, waits for them, and re-layouts: 9.42 us -> 2.32 us
  Pallas kernels: 0 us -> 6.49 us
    reduce_scatter x6 -> x0, waiting for transfers between devices: 253 us -> none  [the longest x3 189 us: scattered(): lax.psum_scatter(dest_terms(jnp.int32(0), vert_dev * lax.axis_size('row')...]
    all_gather x6 -> x0, blocking collectives: 113 us -> none  [the longest x3 94.5 us: spread(): return lax.all_gather(weight, 'row', axis=0, tiled=True)]
    ppermute x0 -> x40, waiting for transfers between devices: none -> 67.7 us  [the longest x38 64.2 us: swap(): return lax.ppermute(value, axis, partner(axis, bit))]
    ppermute x0 -> x40, starting transfers between devices: none -> 47.2 us  [the longest x38 43.4 us: swap(): return lax.ppermute(value, axis, partner(axis, bit))]
    gather x7 -> x0, local copies, waits for them, and re-layouts: 8.88 us -> none  [the longest x3 6.09 us: shards(): source_picked = backward_pieces[back_dest]]
    convert_element_type x7 -> x4, other arithmetic: 9.32 us -> 1.02 us  [the longest x2 0.53 us: coded(): jnp.where(count > 0.0, exponent * 2.0 ** MANTISSA + mantissa, 0.0)]
    pallas_call x0 -> x8, Pallas kernels: none -> 6.49 us  [the longest x2 2.62 us: first_terms(): pl.pallas_call(functools.partial(first_kernel, bool(base)), out_shape=[sh...]
    dot_general x6 -> x20, matrix products: 13.4 us -> 13.2 us  [the longest x8 7.52 us: forward(): lax.dot_general(front.astype(jnp.bfloat16), whole[k], dims, preferred_ele...]
  transfers between devices with their start and end apart: 6 -> 40, of which waited for: 6 -> 21; matrix products, arithmetic and copies ran while one was open for 1% -> 4% of each run, Pallas kernels for 0% -> 3%
where the time goes in v2:
time: 139 us
  waiting for transfers between devices  67.7 us (49%)
  starting transfers between devices  47.2 us (34%)
  matrix products  13.2 us (9%)
  Pallas kernels  6.49 us (5%)
  local copies, waits for them, and re-layouts  2.32 us (2%)
  other arithmetic  1.47 us (1%)
    ppermute x38, waiting for transfers between devices, swap(): return lax.ppermute(value, axis, partner(axis, bit))  64.2 us
    ppermute x38, starting transfers between devices, swap(): return lax.ppermute(value, axis, partner(axis, bit))  43.4 us
    dot_general x8, matrix products, forward(): lax.dot_general(front.astype(jnp.bfloat16), whole[k], dims, preferred_ele...  7.52 us
    dot_general x12, matrix products, split_shards(): jnp.dot(got[k], whole[k], preferred_element_type=jnp.float32)  5.65 us
    ppermute x2, starting transfers between devices, traded(): from_d = lax.ppermute(held[3], ('row', 'col'), diagonal())  3.73 us
    ppermute x2, waiting for transfers between devices, traded(): from_d = lax.ppermute(held[3], ('row', 'col'), diagonal())  3.43 us
  transfers between devices with their start and end apart: 40, of which 21 were waited for; matrix products, arithmetic and copies ran while one was open for 4% of the time, Pallas kernels for 3%

profile of v2, /device:TPU:0, one launch (start us, length us, event | category | flops | bytes accessed | tf_op | source)
XLA Modules:
  0.0 138.8 jit_solution(7165698895144969057)
XLA Ops:
  0.0 1.6 %copy-done = s32[1,1,8,4,128,128]{5,4,3,2,1,0:T(8,128)S(1)} copy-done((s32[1,1,8,4,128,128]{5,4,3,2,1,0:T(8,128)S(1)}, s32[1,1,8,4,128,128]{5,4,3,2,1,0:T(8,128)}, u32[]{:S(2)}) %copy-start) | copy-done | bytes 2097176
  3.0 3.0 %collective-permute-start.6 = (bf16[4,4,128,128]{3,2,1,0:T(8,128)(2,1)S(1)}, bf16[4,4,128,128]{3,2,1,0:T(8,128)(2,1)S(1)}, u32[]{:S(2)}, u32[]{:S(2)}) collective-permute-start(bf16[4,4,128,128]{3,2,1,0:T(8,128)(2,1)S(1)} %get-tuple-element.33.rest_0_), channel_id=1, source_target_pairs={{0,2},{1,3},{2,0},{3,1},{4,6},{5,7},{6,4},{7,5},{8,10},{9,11},{10,... | collective-permute-start | bytes 1572872 | tf_op jit(solution)/shard_map/ppermute | solution.py:77
  6.0 1.5 %collective-permute-start.11 = (bf16[4,4,128,128]{3,2,1,0:T(8,128)(2,1)S(1)}, bf16[4,4,128,128]{3,2,1,0:T(8,128)(2,1)S(1)}, u32[]{:S(2)}, u32[]{:S(2)}) collective-permute-start(bf16[4,4,128,128]{3,2,1,0:T(8,128)(2,1)S(1)} %get-tuple-element.33.rest_0_), channel_id=1, source_target_pairs={{0,4},{4,0},{8,12},{12,8},{16,20},{20,16},{24,28},{28,24},{1,5},{5... | collective-permute-start | bytes 1572872 | tf_op jit(solution)/shard_map/ppermute | solution.py:77
  8.4 1.2 collective-permute-done
  9.6 2.0 %collective-permute-start.1 = (f32[2,32,128]{2,1,0:T(8,128)S(1)}, f32[2,32,128]{2,1,0:T(8,128)S(1)}, u32[]{:S(2)}, u32[]{:S(2)}) collective-permute-start(f32[2,32,128]{2,1,0:T(8,128)S(1)} %pad_maximum_fusion.2), channel_id=1, source_target_pairs={{0,2},{1,3},{2,0},{3,1},{4,6},{5,7},{6,4},{7,5},{8,10},{9,11},{10,... | collective-permute-start | bytes 98312 | tf_op jit(solution)/shard_map/ppermute | solution.py:77
  11.6 18.3 %collective-permute-done.1.rest_1_ = f32[2,32,128]{2,1,0:T(8,128)S(1)} collective-permute-done((f32[2,32,128]{2,1,0:T(8,128)S(1)}, f32[2,32,128]{2,1,0:T(8,128)S(1)}, u32[]{:S(2)}, u32[]{:S(2)}) %collective-permute-start.1) | collective-permute-done | bytes 32800 | tf_op jit(solution)/shard_map/ppermute | solution.py:77
  29.9 1.8 %collective-permute-start.2 = (f32[2,32,128]{2,1,0:T(8,128)S(1)}, f32[2,32,128]{2,1,0:T(8,128)S(1)}, u32[]{:S(2)}, u32[]{:S(2)}) collective-permute-start(f32[2,32,128]{2,1,0:T(8,128)S(1)} %pad_maximum_fusion.3), channel_id=1, source_target_pairs={{0,4},{4,0},{8,12},{12,8},{16,20},{20,16},{24,28},{28,24},{1,5},{5... | collective-permute-start | bytes 98312 | tf_op jit(solution)/shard_map/ppermute | solution.py:77
  31.7 2.1 %collective-permute-done.2.rest_2_ = f32[2,32,128]{2,1,0:T(8,128)S(1)} collective-permute-done((f32[2,32,128]{2,1,0:T(8,128)S(1)}, f32[2,32,128]{2,1,0:T(8,128)S(1)}, u32[]{:S(2)}, u32[]{:S(2)}) %collective-permute-start.2) | collective-permute-done | bytes 32800 | tf_op jit(solution)/shard_map/ppermute | solution.py:77
  33.8 2.7 %collective-permute-start.3 = (f32[2,32,128]{2,1,0:T(8,128)S(1)}, f32[2,32,128]{2,1,0:T(8,128)S(1)}, u32[]{:S(2)}, u32[]{:S(2)}) collective-permute-start(f32[2,32,128]{2,1,0:T(8,128)S(1)} %pad_maximum_fusion.4), channel_id=1, source_target_pairs={{0,6},{1,7},{2,4},{3,5},{4,2},{5,3},{6,0},{7,1},{8,14},{9,15},{10,... | collective-permute-start | bytes 98312 | tf_op jit(solution)/shard_map/ppermute | solution.py:333
  36.5 2.1 %collective-permute-done.3.rest_3_ = f32[2,32,128]{2,1,0:T(8,128)S(1)} collective-permute-done((f32[2,32,128]{2,1,0:T(8,128)S(1)}, f32[2,32,128]{2,1,0:T(8,128)S(1)}, u32[]{:S(2)}, u32[]{:S(2)}) %collective-permute-start.3) | collective-permute-done | bytes 32800 | tf_op jit(solution)/shard_map/ppermute | solution.py:333
  39.2 1.7 %collective-permute-start.14 = (bf16[4,4,128,128]{3,2,1,0:T(8,128)(2,1)S(1)}, bf16[4,4,128,128]{3,2,1,0:T(8,128)(2,1)S(1)}, u32[]{:S(2)}, u32[]{:S(2)}) collective-permute-start(bf16[4,4,128,128]{3,2,1,0:T(8,128)(2,1)S(1)} %collective-permute-done.10.rest_8_), channel_id=1, source_target_pairs={{0,2},{1,3},{2,0},{3,1},{4,6},{5,7},{6,4},{7,5},{8,10},{9,11},{10,... | collective-permute-start | bytes 1572872 | tf_op jit(solution)/shard_map/ppermute | solution.py:77
  41.0 1.5 %collective-permute-start.15 = (bf16[4,4,128,128]{3,2,1,0:T(8,128)(2,1)S(1)}, bf16[4,4,128,128]{3,2,1,0:T(8,128)(2,1)S(1)}, u32[]{:S(2)}, u32[]{:S(2)}) collective-permute-start(bf16[4,4,128,128]{3,2,1,0:T(8,128)(2,1)S(1)} %collective-permute-done.6.rest_4_), channel_id=1, source_target_pairs={{0,4},{4,0},{8,12},{12,8},{16,20},{20,16},{24,28},{28,24},{1,5},{5... | collective-permute-start | bytes 1572872 | tf_op jit(solution)/shard_map/ppermute | solution.py:77
  43.1 10.4 %collective-permute-done.14.rest_4_.rest_12_ = bf16[4,4,128,128]{3,2,1,0:T(8,128)(2,1)S(1)} collective-permute-done((bf16[4,4,128,128]{3,2,1,0:T(8,128)(2,1)S(1)}, bf16[4,4,128,128]{3,2,1,0:T(8,128)(2,1)S(1)}, u32[]{:S(2)}, u32[]{:S(2)}) %collective-permute-start.14) | collective-permute-done | bytes 524320 | tf_op jit(solution)/shard_map/ppermute | solution.py:77
  53.5 1.5 %collective-permute-done.15.rest_5_.rest_13_ = bf16[4,4,128,128]{3,2,1,0:T(8,128)(2,1)S(1)} collective-permute-done((bf16[4,4,128,128]{3,2,1,0:T(8,128)(2,1)S(1)}, bf16[4,4,128,128]{3,2,1,0:T(8,128)(2,1)S(1)}, u32[]{:S(2)}, u32[]{:S(2)}) %collective-permute-start.15) | collective-permute-done | bytes 524320 | tf_op jit(solution)/shard_map/ppermute | solution.py:77
  55.1 1.9 %first.2 = (f32[32,1024]{1,0:T(8,128)S(1)}, f32[32,1024]{1,0:T(8,128)S(1)}, f32[32,1024]{1,0:T(8,128)S(1)}, f32[32,1024]{1,0:T(8,128)S(1)}) custom-call(bf16[32,1024]{1,0:T(8,128)(2,1)S(1)} %get-tuple-element.32.front, bf16[4,4,128,128]{3,2,1,0:T(8,128)(2,1)S(1)} %get-tuple-element.33.rest_0_, bf16[4,4,128,128]{3,2,1,0:T(8,128)(2,1)S(1)} %get-tuple-element.34.rest_1_, ...), custom_call_target="tpu_custom_call" | custom-call | flops 201326592 | bytes 6291456 | tf_op jit(solution)/shard_map/first/pallas_call | solution.py:241
  58.1 1.6 %collective-permute-start.18 = (s32[32,768]{1,0:T(8,128)S(1)}, s32[32,768]{1,0:T(8,128)S(1)}, u32[]{:S(2)}, u32[]{:S(2)}) collective-permute-start(s32[32,768]{1,0:T(8,128)S(1)} %pad_add_fusion.9), channel_id=1, source_target_pairs={{0,8},{4,12},{8,0},{12,4},{16,24},{20,28},{24,16},{28,20},{1,9},{5... | collective-permute-start | bytes 294920 | tf_op jit(solution)/shard_map/ppermute | solution.py:77
  59.8 2.7 %collective-permute-start.19 = (s32[32,768]{1,0:T(8,128)S(1)}, s32[32,768]{1,0:T(8,128)S(1)}, u32[]{:S(2)}, u32[]{:S(2)}) collective-permute-start(s32[32,768]{1,0:T(8,128)S(1)} %pad_add_fusion.10), channel_id=1, source_target_pairs={{0,16},{4,20},{8,24},{12,28},{16,0},{20,4},{24,8},{28,12},{1,17},{... | collective-permute-start | bytes 294920 | tf_op jit(solution)/shard_map/ppermute | solution.py:77
  63.0 2.2 %assemble.1 = (bf16[1024,1024]{1,0:T(8,128)(2,1)S(1)}, bf16[1024,1024]{1,0:T(8,128)(2,1)S(1)}, bf16[1024,1024]{1,0:T(8,128)(2,1)S(1)}, bf16[1024,1024]{1,0:T(8,128)(2,1)S(1)}) custom-call(bf16[4,4,128,128]{3,2,1,0:T(8,128)(2,1)S(1)} %get-tuple-element.33.rest_0_, bf16[4,4,128,128]{3,2,1,0:T(8,128)(2,1)S(1)} %get-tuple-element.34.rest_1_, ...), custom_call_target="tpu_custom_call" | custom-call | bytes 16777216 | tf_op jit(solution)/shard_map/assemble/pallas_call | solution.py:268
  65.2 5.4 %collective-permute-done.19 = s32[32,768]{1,0:T(8,128)S(1)} collective-permute-done((s32[32,768]{1,0:T(8,128)S(1)}, s32[32,768]{1,0:T(8,128)S(1)}, u32[]{:S(2)}, u32[]{:S(2)}) %collective-permute-start.19) | collective-permute-done | bytes 98336 | tf_op jit(solution)/shard_map/ppermute | solution.py:77
  71.0 0.9 fusion.54
  72.0 2.1 %collective-permute-start.21 = (s32[32,768]{1,0:T(8,128)S(1)}, s32[32,768]{1,0:T(8,128)S(1)}, u32[]{:S(2)}, u32[]{:S(2)}) collective-permute-start(s32[32,768]{1,0:T(8,128)S(1)} %pad_add_fusion.12), channel_id=1, source_target_pairs={{0,8},{4,12},{8,0},{12,4},{16,24},{20,28},{24,16},{28,20},{1,9},{5... | collective-permute-start | bytes 294920 | tf_op jit(solution)/shard_map/ppermute | solution.py:77
  75.0 1.3 collective-permute-start.22
  77.2 1.4 %collective-permute-start.23 = (s32[32,768]{1,0:T(8,128)S(1)}, s32[32,768]{1,0:T(8,128)S(1)}, u32[]{:S(2)}, u32[]{:S(2)}) collective-permute-start(s32[32,768]{1,0:T(8,128)S(1)} %pad_add_fusion.14), channel_id=1, source_target_pairs={{0,24},{4,28},{8,16},{12,20},{16,8},{20,12},{24,0},{28,4},{1,25},{... | collective-permute-start | bytes 294920 | tf_op jit(solution)/shard_map/ppermute | solution.py:77
  78.6 6.2 %collective-permute-done.22 = s32[32,768]{1,0:T(8,128)S(1)} collective-permute-done((s32[32,768]{1,0:T(8,128)S(1)}, s32[32,768]{1,0:T(8,128)S(1)}, u32[]{:S(2)}, u32[]{:S(2)}) %collective-permute-start.22) | collective-permute-done | bytes 98336 | tf_op jit(solution)/shard_map/ppermute | solution.py:77
  84.8 1.0 fusion.156
  87.6 0.9 fusion.99
  88.6 1.8 %collective-permute-start.24 = (s32[32,768]{1,0:T(8,128)S(1)}, s32[32,768]{1,0:T(8,128)S(1)}, u32[]{:S(2)}, u32[]{:S(2)}) collective-permute-start(s32[32,768]{1,0:T(8,128)S(1)} %pad_add_fusion.15), channel_id=1, source_target_pairs={{0,8},{4,12},{8,0},{12,4},{16,24},{20,28},{24,16},{28,20},{1,9},{5... | collective-permute-start | bytes 294920 | tf_op jit(solution)/shard_map/ppermute | solution.py:77
  90.4 1.1 collective-permute-start.25
  91.5 1.7 %collective-permute-start.26 = (s32[32,768]{1,0:T(8,128)S(1)}, s32[32,768]{1,0:T(8,128)S(1)}, u32[]{:S(2)}, u32[]{:S(2)}) collective-permute-start(s32[32,768]{1,0:T(8,128)S(1)} %pad_add_fusion.17), channel_id=1, source_target_pairs={{0,24},{4,28},{8,16},{12,20},{16,8},{20,12},{24,0},{28,4},{1,25},{... | collective-permute-start | bytes 294920 | tf_op jit(solution)/shard_map/ppermute | solution.py:77
  93.2 1.1 collective-permute-done.24
  94.3 6.1 %collective-permute-done.25 = s32[32,768]{1,0:T(8,128)S(1)} collective-permute-done((s32[32,768]{1,0:T(8,128)S(1)}, s32[32,768]{1,0:T(8,128)S(1)}, u32[]{:S(2)}, u32[]{:S(2)}) %collective-permute-start.25) | collective-permute-done | bytes 98336 | tf_op jit(solution)/shard_map/ppermute | solution.py:77
  100.5 1.2 fusion.18
  101.7 1.6 %collective-permute-start.27 = (bf16[32,1024]{1,0:T(8,128)(2,1)S(1)}, bf16[32,1024]{1,0:T(8,128)(2,1)S(1)}, u32[]{:S(2)}, u32[]{:S(2)}) collective-permute-start(bf16[32,1024]{1,0:T(8,128)(2,1)S(1)} %fusion.18), channel_id=1, source_target_pairs={{0,8},{4,12},{8,0},{12,4},{16,24},{20,28},{24,16},{28,20},{1,9},{5... | collective-permute-start | bytes 196616 | tf_op jit(solution)/shard_map/ppermute | solution.py:77
  103.3 1.2 collective-permute-start.28
  104.5 1.7 %collective-permute-start.29 = (bf16[32,1024]{1,0:T(8,128)(2,1)S(1)}, bf16[32,1024]{1,0:T(8,128)(2,1)S(1)}, u32[]{:S(2)}, u32[]{:S(2)}) collective-permute-start(bf16[32,1024]{1,0:T(8,128)(2,1)S(1)} %fusion.18), channel_id=1, source_target_pairs={{0,24},{4,28},{8,16},{12,20},{16,8},{20,12},{24,0},{28,4},{1,25},{... | collective-permute-start | bytes 196616 | tf_op jit(solution)/shard_map/ppermute | solution.py:77
  107.1 2.8 %collective-permute-done.28 = bf16[32,1024]{1,0:T(8,128)(2,1)S(1)} collective-permute-done((bf16[32,1024]{1,0:T(8,128)(2,1)S(1)}, bf16[32,1024]{1,0:T(8,128)(2,1)S(1)}, u32[]{:S(2)}, u32[]{:S(2)}) %collective-permute-start.28) | collective-permute-done | bytes 65568 | tf_op jit(solution)/shard_map/ppermute | solution.py:77
  111.7 1.2 collective-permute-start.30
  112.9 2.2 %collective-permute-start.31 = (bf16[32,1024]{1,0:T(8,128)(2,1)S(1)}, bf16[32,1024]{1,0:T(8,128)(2,1)S(1)}, u32[]{:S(2)}, u32[]{:S(2)}) collective-permute-start(bf16[32,1024]{1,0:T(8,128)(2,1)S(1)} %get-tuple-element.135), channel_id=1, source_target_pairs={{0,16},{4,20},{8,24},{12,28},{16,0},{20,4},{24,8},{28,12},{1,17},{... | collective-permute-start | bytes 196616 | tf_op jit(solution)/shard_map/ppermute | solution.py:77
  115.1 1.1 collective-permute-start.32
  116.7 2.7 %collective-permute-done.31 = bf16[32,1024]{1,0:T(8,128)(2,1)S(1)} collective-permute-done((bf16[32,1024]{1,0:T(8,128)(2,1)S(1)}, bf16[32,1024]{1,0:T(8,128)(2,1)S(1)}, u32[]{:S(2)}, u32[]{:S(2)}) %collective-permute-start.31) | collective-permute-done | bytes 65568 | tf_op jit(solution)/shard_map/ppermute | solution.py:77
  119.8 1.4 collective-permute-done.32
  122.2 1.7 %collective-permute-start.34 = (bf16[32,1024]{1,0:T(8,128)(2,1)S(1)}, bf16[32,1024]{1,0:T(8,128)(2,1)S(1)}, u32[]{:S(2)}, u32[]{:S(2)}) collective-permute-start(bf16[32,1024]{1,0:T(8,128)(2,1)S(1)} %select_convert_fusion), channel_id=1, source_target_pairs={{0,16},{4,20},{8,24},{12,28},{16,0},{20,4},{24,8},{28,12},{1,17},{... | collective-permute-start | bytes 196616 | tf_op jit(solution)/shard_map/ppermute | solution.py:77
  124.0 2.7 %collective-permute-start.35 = (bf16[32,1024]{1,0:T(8,128)(2,1)S(1)}, bf16[32,1024]{1,0:T(8,128)(2,1)S(1)}, u32[]{:S(2)}, u32[]{:S(2)}) collective-permute-start(bf16[32,1024]{1,0:T(8,128)(2,1)S(1)} %select_convert_fusion), channel_id=1, source_target_pairs={{0,24},{4,28},{8,16},{12,20},{16,8},{20,12},{24,0},{28,4},{1,25},{... | collective-permute-start | bytes 196616 | tf_op jit(solution)/shard_map/ppermute | solution.py:77
  127.9 2.1 %collective-permute-done.35 = bf16[32,1024]{1,0:T(8,128)(2,1)S(1)} collective-permute-done((bf16[32,1024]{1,0:T(8,128)(2,1)S(1)}, bf16[32,1024]{1,0:T(8,128)(2,1)S(1)}, u32[]{:S(2)}, u32[]{:S(2)}) %collective-permute-start.35) | collective-permute-done | bytes 65568 | tf_op jit(solution)/shard_map/ppermute | solution.py:77
  131.1 1.2 collective-permute-done.36
  132.4 1.0 collective-permute-start.39
  134.1 1.9 %collective-permute-start.37 = (f32[2,32,128]{2,1,0:T(8,128)S(1)}, f32[2,32,128]{2,1,0:T(8,128)S(1)}, u32[]{:S(2)}, u32[]{:S(2)}) collective-permute-start(f32[2,32,128]{2,1,0:T(8,128)S(1)} %pad_maximum_fusion.6), channel_id=1, source_target_pairs={{0,2},{1,3},{2,0},{3,1},{4,6},{5,7},{6,4},{7,5},{8,10},{9,11},{10,... | collective-permute-start | bytes 98312 | tf_op jit(solution)/shard_map/ppermute | solution.py:77
  135.9 1.3 collective-permute-done.39.rest_3_
  (117 shorter events, 18.5 us)
Async XLA Ops:
  0.0 1.6 %copy-start = (s32[1,1,8,4,128,128]{5,4,3,2,1,0:T(8,128)S(1)}, s32[1,1,8,4,128,128]{5,4,3,2,1,0:T(8,128)}, u32[]{:S(2)}) copy-start(s32[1,1,8,4,128,128]{5,4,3,2,1,0:T(8,128)} %param.9) | copy-start | bytes 6291460
  1.6 0.7 copy-start.4
  2.3 5.9 %copy-start.1 = (f32[128,256]{1,0:T(8,128)S(1)}, f32[128,256]{1,0:T(8,128)}, u32[]{:S(2)}) copy-start(f32[128,256]{1,0:T(8,128)} %paths_in.1) | copy-start | bytes 393220
  2.3 5.9 %copy-start.2 = (s32[128,256]{1,0:T(8,128)S(1)}, s32[128,256]{1,0:T(8,128)}, u32[]{:S(2)}) copy-start(s32[128,256]{1,0:T(8,128)} %levels.1) | copy-start | bytes 393220
  2.3 5.9 %copy-start.3 = (f32[128,256]{1,0:T(8,128)S(1)}, f32[128,256]{1,0:T(8,128)}, u32[]{:S(2)}) copy-start(f32[128,256]{1,0:T(8,128)} %dep_in.1) | copy-start | bytes 393220
  3.0 36.1 %collective-permute-start.6 = (bf16[4,4,128,128]{3,2,1,0:T(8,128)(2,1)S(1)}, bf16[4,4,128,128]{3,2,1,0:T(8,128)(2,1)S(1)}, u32[]{:S(2)}, u32[]{:S(2)}) collective-permute-start(bf16[4,4,128,128]{3,2,1,0:T(8,128)(2,1)S(1)} %get-tuple-element.33.rest_0_), channel_id=1, source_target_pairs={{0,2},{1,3},{2,0},{3,1},{4,6},{5,7},{6,4},{7,5},{8,10},{9,11},{10,... | collective-permute-start | bytes 1572872 | tf_op jit(solution)/shard_map/ppermute | solution.py:77
  6.0 33.2 %collective-permute-start.11 = (bf16[4,4,128,128]{3,2,1,0:T(8,128)(2,1)S(1)}, bf16[4,4,128,128]{3,2,1,0:T(8,128)(2,1)S(1)}, u32[]{:S(2)}, u32[]{:S(2)}) collective-permute-start(bf16[4,4,128,128]{3,2,1,0:T(8,128)(2,1)S(1)} %get-tuple-element.33.rest_0_), channel_id=1, source_target_pairs={{0,4},{4,0},{8,12},{12,8},{16,20},{20,16},{24,28},{28,24},{1,5},{5... | collective-permute-start | bytes 1572872 | tf_op jit(solution)/shard_map/ppermute | solution.py:77
  7.6 31.1 %collective-permute-start.10 = (bf16[4,4,128,128]{3,2,1,0:T(8,128)(2,1)S(1)}, bf16[4,4,128,128]{3,2,1,0:T(8,128)(2,1)S(1)}, u32[]{:S(2)}, u32[]{:S(2)}) collective-permute-start(bf16[4,4,128,128]{3,2,1,0:T(8,128)(2,1)S(1)} %get-tuple-element.34.rest_1_), channel_id=1, source_target_pairs={{0,4},{4,0},{8,12},{12,8},{16,20},{20,16},{24,28},{28,24},{1,5},{5... | collective-permute-start | bytes 1572872 | tf_op jit(solution)/shard_map/ppermute | solution.py:77
  8.1 32.9 %collective-permute-start.7 = (bf16[4,4,128,128]{3,2,1,0:T(8,128)(2,1)S(1)}, bf16[4,4,128,128]{3,2,1,0:T(8,128)(2,1)S(1)}, u32[]{:S(2)}, u32[]{:S(2)}) collective-permute-start(bf16[4,4,128,128]{3,2,1,0:T(8,128)(2,1)S(1)} %get-tuple-element.34.rest_1_), channel_id=1, source_target_pairs={{0,2},{1,3},{2,0},{3,1},{4,6},{5,7},{6,4},{7,5},{8,10},{9,11},{10,... | collective-permute-start | bytes 1572872 | tf_op jit(solution)/shard_map/ppermute | solution.py:77
  8.3 1.3 collective-permute-start
  9.6 20.3 %collective-permute-start.1 = (f32[2,32,128]{2,1,0:T(8,128)S(1)}, f32[2,32,128]{2,1,0:T(8,128)S(1)}, u32[]{:S(2)}, u32[]{:S(2)}) collective-permute-start(f32[2,32,128]{2,1,0:T(8,128)S(1)} %pad_maximum_fusion.2), channel_id=1, source_target_pairs={{0,2},{1,3},{2,0},{3,1},{4,6},{5,7},{6,4},{7,5},{8,10},{9,11},{10,... | collective-permute-start | bytes 98312 | tf_op jit(solution)/shard_map/ppermute | solution.py:77
  29.9 3.9 %collective-permute-start.2 = (f32[2,32,128]{2,1,0:T(8,128)S(1)}, f32[2,32,128]{2,1,0:T(8,128)S(1)}, u32[]{:S(2)}, u32[]{:S(2)}) collective-permute-start(f32[2,32,128]{2,1,0:T(8,128)S(1)} %pad_maximum_fusion.3), channel_id=1, source_target_pairs={{0,4},{4,0},{8,12},{12,8},{16,20},{20,16},{24,28},{28,24},{1,5},{5... | collective-permute-start | bytes 98312 | tf_op jit(solution)/shard_map/ppermute | solution.py:77
  33.8 4.8 %collective-permute-start.3 = (f32[2,32,128]{2,1,0:T(8,128)S(1)}, f32[2,32,128]{2,1,0:T(8,128)S(1)}, u32[]{:S(2)}, u32[]{:S(2)}) collective-permute-start(f32[2,32,128]{2,1,0:T(8,128)S(1)} %pad_maximum_fusion.4), channel_id=1, source_target_pairs={{0,6},{1,7},{2,4},{3,5},{4,2},{5,3},{6,0},{7,1},{8,14},{9,15},{10,... | collective-permute-start | bytes 98312 | tf_op jit(solution)/shard_map/ppermute | solution.py:333
  38.6 3.9 %collective-permute-start.4 = (bf16[4,4,128,128]{3,2,1,0:T(8,128)(2,1)S(1)}, bf16[4,4,128,128]{3,2,1,0:T(8,128)(2,1)S(1)}, u32[]{:S(2)}, u32[]{:S(2)}) collective-permute-start(bf16[4,4,128,128]{3,2,1,0:T(8,128)(2,1)S(1)} %get-tuple-element.33.rest_0_), channel_id=1, source_target_pairs={{0,1},{1,0},{2,3},{3,2},{4,5},{5,4},{6,7},{7,6},{8,9},{9,8},{10,11... | collective-permute-start | bytes 1572872 | tf_op jit(solution)/shard_map/ppermute | solution.py:77
  38.6 3.9 %collective-permute-start.5 = (bf16[4,4,128,128]{3,2,1,0:T(8,128)(2,1)S(1)}, bf16[4,4,128,128]{3,2,1,0:T(8,128)(2,1)S(1)}, u32[]{:S(2)}, u32[]{:S(2)}) collective-permute-start(bf16[4,4,128,128]{3,2,1,0:T(8,128)(2,1)S(1)} %get-tuple-element.34.rest_1_), channel_id=1, source_target_pairs={{0,1},{1,0},{2,3},{3,2},{4,5},{5,4},{6,7},{7,6},{8,9},{9,8},{10,11... | collective-permute-start | bytes 1572872 | tf_op jit(solution)/shard_map/ppermute | solution.py:77
  39.2 3.9 %collective-permute-start.12 = (bf16[4,4,128,128]{3,2,1,0:T(8,128)(2,1)S(1)}, bf16[4,4,128,128]{3,2,1,0:T(8,128)(2,1)S(1)}, u32[]{:S(2)}, u32[]{:S(2)}) collective-permute-start(bf16[4,4,128,128]{3,2,1,0:T(8,128)(2,1)S(1)} %collective-permute-done.10.rest_8_), channel_id=1, source_target_pairs={{0,1},{1,0},{2,3},{3,2},{4,5},{5,4},{6,7},{7,6},{8,9},{9,8},{10,11... | collective-permute-start | bytes 1572872 | tf_op jit(solution)/shard_map/ppermute | solution.py:77
  39.2 14.3 %collective-permute-start.14 = (bf16[4,4,128,128]{3,2,1,0:T(8,128)(2,1)S(1)}, bf16[4,4,128,128]{3,2,1,0:T(8,128)(2,1)S(1)}, u32[]{:S(2)}, u32[]{:S(2)}) collective-permute-start(bf16[4,4,128,128]{3,2,1,0:T(8,128)(2,1)S(1)} %collective-permute-done.10.rest_8_), channel_id=1, source_target_pairs={{0,2},{1,3},{2,0},{3,1},{4,6},{5,7},{6,4},{7,5},{8,10},{9,11},{10,... | collective-permute-start | bytes 1572872 | tf_op jit(solution)/shard_map/ppermute | solution.py:77
  41.0 14.0 %collective-permute-start.15 = (bf16[4,4,128,128]{3,2,1,0:T(8,128)(2,1)S(1)}, bf16[4,4,128,128]{3,2,1,0:T(8,128)(2,1)S(1)}, u32[]{:S(2)}, u32[]{:S(2)}) collective-permute-start(bf16[4,4,128,128]{3,2,1,0:T(8,128)(2,1)S(1)} %collective-permute-done.6.rest_4_), channel_id=1, source_target_pairs={{0,4},{4,0},{8,12},{12,8},{16,20},{20,16},{24,28},{28,24},{1,5},{5... | collective-permute-start | bytes 1572872 | tf_op jit(solution)/shard_map/ppermute | solution.py:77
  42.5 12.5 %collective-permute-start.8 = (bf16[4,4,128,128]{3,2,1,0:T(8,128)(2,1)S(1)}, bf16[4,4,128,128]{3,2,1,0:T(8,128)(2,1)S(1)}, u32[]{:S(2)}, u32[]{:S(2)}) collective-permute-start(bf16[4,4,128,128]{3,2,1,0:T(8,128)(2,1)S(1)} %collective-permute-done.6.rest_4_), channel_id=1, source_target_pairs={{0,1},{1,0},{2,3},{3,2},{4,5},{5,4},{6,7},{7,6},{8,9},{9,8},{10,11... | collective-permute-start | bytes 1572872 | tf_op jit(solution)/shard_map/ppermute | solution.py:77
  42.5 12.5 %collective-permute-start.13 = (bf16[4,4,128,128]{3,2,1,0:T(8,128)(2,1)S(1)}, bf16[4,4,128,128]{3,2,1,0:T(8,128)(2,1)S(1)}, u32[]{:S(2)}, u32[]{:S(2)}) collective-permute-start(bf16[4,4,128,128]{3,2,1,0:T(8,128)(2,1)S(1)} %collective-permute-done.11.rest_9_), channel_id=1, source_target_pairs={{0,1},{1,0},{2,3},{3,2},{4,5},{5,4},{6,7},{7,6},{8,9},{9,8},{10,11... | collective-permute-start | bytes 1572872 | tf_op jit(solution)/shard_map/ppermute | solution.py:77
  43.0 12.0 %collective-permute-start.9 = (bf16[4,4,128,128]{3,2,1,0:T(8,128)(2,1)S(1)}, bf16[4,4,128,128]{3,2,1,0:T(8,128)(2,1)S(1)}, u32[]{:S(2)}, u32[]{:S(2)}) collective-permute-start(bf16[4,4,128,128]{3,2,1,0:T(8,128)(2,1)S(1)} %collective-permute-done.7.rest_5_), channel_id=1, source_target_pairs={{0,1},{1,0},{2,3},{3,2},{4,5},{5,4},{6,7},{7,6},{8,9},{9,8},{10,11... | collective-permute-start | bytes 1572872 | tf_op jit(solution)/shard_map/ppermute | solution.py:77
  53.5 3.5 %collective-permute-start.16 = (bf16[4,4,128,128]{3,2,1,0:T(8,128)(2,1)S(1)}, bf16[4,4,128,128]{3,2,1,0:T(8,128)(2,1)S(1)}, u32[]{:S(2)}, u32[]{:S(2)}) collective-permute-start(bf16[4,4,128,128]{3,2,1,0:T(8,128)(2,1)S(1)} %collective-permute-done.14.rest_4_.rest_12_), channel_id=1, source_target_pairs={{0,1},{1,0},{2,3},{3,2},{4,5},{5,4},{6,7},{7,6},{8,9},{9,8},{10,11... | collective-permute-start | bytes 1572872 | tf_op jit(solution)/shard_map/ppermute | solution.py:77
  55.0 2.0 %collective-permute-start.17 = (bf16[4,4,128,128]{3,2,1,0:T(8,128)(2,1)S(1)}, bf16[4,4,128,128]{3,2,1,0:T(8,128)(2,1)S(1)}, u32[]{:S(2)}, u32[]{:S(2)}) collective-permute-start(bf16[4,4,128,128]{3,2,1,0:T(8,128)(2,1)S(1)} %collective-permute-done.15.rest_5_.rest_13_), channel_id=1, source_target_pairs={{0,1},{1,0},{2,3},{3,2},{4,5},{5,4},{6,7},{7,6},{8,9},{9,8},{10,11... | collective-permute-start | bytes 1572872 | tf_op jit(solution)/shard_map/ppermute | solution.py:77
  58.1 7.0 %collective-permute-start.18 = (s32[32,768]{1,0:T(8,128)S(1)}, s32[32,768]{1,0:T(8,128)S(1)}, u32[]{:S(2)}, u32[]{:S(2)}) collective-permute-start(s32[32,768]{1,0:T(8,128)S(1)} %pad_add_fusion.9), channel_id=1, source_target_pairs={{0,8},{4,12},{8,0},{12,4},{16,24},{20,28},{24,16},{28,20},{1,9},{5... | collective-permute-start | bytes 294920 | tf_op jit(solution)/shard_map/ppermute | solution.py:77
  59.8 10.7 %collective-permute-start.19 = (s32[32,768]{1,0:T(8,128)S(1)}, s32[32,768]{1,0:T(8,128)S(1)}, u32[]{:S(2)}, u32[]{:S(2)}) collective-permute-start(s32[32,768]{1,0:T(8,128)S(1)} %pad_add_fusion.10), channel_id=1, source_target_pairs={{0,16},{4,20},{8,24},{12,28},{16,0},{20,4},{24,8},{28,12},{1,17},{... | collective-permute-start | bytes 294920 | tf_op jit(solution)/shard_map/ppermute | solution.py:77
  62.7 7.9 %collective-permute-start.20 = (s32[32,768]{1,0:T(8,128)S(1)}, s32[32,768]{1,0:T(8,128)S(1)}, u32[]{:S(2)}, u32[]{:S(2)}) collective-permute-start(s32[32,768]{1,0:T(8,128)S(1)} %pad_add_fusion.11), channel_id=1, source_target_pairs={{0,24},{4,28},{8,16},{12,20},{16,8},{20,12},{24,0},{28,4},{1,25},{... | collective-permute-start | bytes 294920 | tf_op jit(solution)/shard_map/ppermute | solution.py:77
  72.0 6.6 %collective-permute-start.21 = (s32[32,768]{1,0:T(8,128)S(1)}, s32[32,768]{1,0:T(8,128)S(1)}, u32[]{:S(2)}, u32[]{:S(2)}) collective-permute-start(s32[32,768]{1,0:T(8,128)S(1)} %pad_add_fusion.12), channel_id=1, source_target_pairs={{0,8},{4,12},{8,0},{12,4},{16,24},{20,28},{24,16},{28,20},{1,9},{5... | collective-permute-start | bytes 294920 | tf_op jit(solution)/shard_map/ppermute | solution.py:77
  75.0 9.8 %collective-permute-start.22 = (s32[32,768]{1,0:T(8,128)S(1)}, s32[32,768]{1,0:T(8,128)S(1)}, u32[]{:S(2)}, u32[]{:S(2)}) collective-permute-start(s32[32,768]{1,0:T(8,128)S(1)} %pad_add_fusion.13), channel_id=1, source_target_pairs={{0,16},{4,20},{8,24},{12,28},{16,0},{20,4},{24,8},{28,12},{1,17},{... | collective-permute-start | bytes 294920 | tf_op jit(solution)/shard_map/ppermute | solution.py:77
  77.2 7.6 %collective-permute-start.23 = (s32[32,768]{1,0:T(8,128)S(1)}, s32[32,768]{1,0:T(8,128)S(1)}, u32[]{:S(2)}, u32[]{:S(2)}) collective-permute-start(s32[32,768]{1,0:T(8,128)S(1)} %pad_add_fusion.14), channel_id=1, source_target_pairs={{0,24},{4,28},{8,16},{12,20},{16,8},{20,12},{24,0},{28,4},{1,25},{... | collective-permute-start | bytes 294920 | tf_op jit(solution)/shard_map/ppermute | solution.py:77
  88.6 5.7 %collective-permute-start.24 = (s32[32,768]{1,0:T(8,128)S(1)}, s32[32,768]{1,0:T(8,128)S(1)}, u32[]{:S(2)}, u32[]{:S(2)}) collective-permute-start(s32[32,768]{1,0:T(8,128)S(1)} %pad_add_fusion.15), channel_id=1, source_target_pairs={{0,8},{4,12},{8,0},{12,4},{16,24},{20,28},{24,16},{28,20},{1,9},{5... | collective-permute-start | bytes 294920 | tf_op jit(solution)/shard_map/ppermute | solution.py:77
  90.4 10.0 %collective-permute-start.25 = (s32[32,768]{1,0:T(8,128)S(1)}, s32[32,768]{1,0:T(8,128)S(1)}, u32[]{:S(2)}, u32[]{:S(2)}) collective-permute-start(s32[32,768]{1,0:T(8,128)S(1)} %pad_add_fusion.16), channel_id=1, source_target_pairs={{0,16},{4,20},{8,24},{12,28},{16,0},{20,4},{24,8},{28,12},{1,17},{... | collective-permute-start | bytes 294920 | tf_op jit(solution)/shard_map/ppermute | solution.py:77
  91.5 8.9 %collective-permute-start.26 = (s32[32,768]{1,0:T(8,128)S(1)}, s32[32,768]{1,0:T(8,128)S(1)}, u32[]{:S(2)}, u32[]{:S(2)}) collective-permute-start(s32[32,768]{1,0:T(8,128)S(1)} %pad_add_fusion.17), channel_id=1, source_target_pairs={{0,24},{4,28},{8,16},{12,20},{16,8},{20,12},{24,0},{28,4},{1,25},{... | collective-permute-start | bytes 294920 | tf_op jit(solution)/shard_map/ppermute | solution.py:77
  101.7 5.0 %collective-permute-start.27 = (bf16[32,1024]{1,0:T(8,128)(2,1)S(1)}, bf16[32,1024]{1,0:T(8,128)(2,1)S(1)}, u32[]{:S(2)}, u32[]{:S(2)}) collective-permute-start(bf16[32,1024]{1,0:T(8,128)(2,1)S(1)} %fusion.18), channel_id=1, source_target_pairs={{0,8},{4,12},{8,0},{12,4},{16,24},{20,28},{24,16},{28,20},{1,9},{5... | collective-permute-start | bytes 196616 | tf_op jit(solution)/shard_map/ppermute | solution.py:77
  103.3 6.6 %collective-permute-start.28 = (bf16[32,1024]{1,0:T(8,128)(2,1)S(1)}, bf16[32,1024]{1,0:T(8,128)(2,1)S(1)}, u32[]{:S(2)}, u32[]{:S(2)}) collective-permute-start(bf16[32,1024]{1,0:T(8,128)(2,1)S(1)} %fusion.18), channel_id=1, source_target_pairs={{0,16},{4,20},{8,24},{12,28},{16,0},{20,4},{24,8},{28,12},{1,17},{... | collective-permute-start | bytes 196616 | tf_op jit(solution)/shard_map/ppermute | solution.py:77
  104.5 6.2 %collective-permute-start.29 = (bf16[32,1024]{1,0:T(8,128)(2,1)S(1)}, bf16[32,1024]{1,0:T(8,128)(2,1)S(1)}, u32[]{:S(2)}, u32[]{:S(2)}) collective-permute-start(bf16[32,1024]{1,0:T(8,128)(2,1)S(1)} %fusion.18), channel_id=1, source_target_pairs={{0,24},{4,28},{8,16},{12,20},{16,8},{20,12},{24,0},{28,4},{1,25},{... | collective-permute-start | bytes 196616 | tf_op jit(solution)/shard_map/ppermute | solution.py:77
  111.7 4.5 %collective-permute-start.30 = (bf16[32,1024]{1,0:T(8,128)(2,1)S(1)}, bf16[32,1024]{1,0:T(8,128)(2,1)S(1)}, u32[]{:S(2)}, u32[]{:S(2)}) collective-permute-start(bf16[32,1024]{1,0:T(8,128)(2,1)S(1)} %get-tuple-element.135), channel_id=1, source_target_pairs={{0,8},{4,12},{8,0},{12,4},{16,24},{20,28},{24,16},{28,20},{1,9},{5... | collective-permute-start | bytes 196616 | tf_op jit(solution)/shard_map/ppermute | solution.py:77
  112.9 6.4 %collective-permute-start.31 = (bf16[32,1024]{1,0:T(8,128)(2,1)S(1)}, bf16[32,1024]{1,0:T(8,128)(2,1)S(1)}, u32[]{:S(2)}, u32[]{:S(2)}) collective-permute-start(bf16[32,1024]{1,0:T(8,128)(2,1)S(1)} %get-tuple-element.135), channel_id=1, source_target_pairs={{0,16},{4,20},{8,24},{12,28},{16,0},{20,4},{24,8},{28,12},{1,17},{... | collective-permute-start | bytes 196616 | tf_op jit(solution)/shard_map/ppermute | solution.py:77
  115.1 6.1 %collective-permute-start.32 = (bf16[32,1024]{1,0:T(8,128)(2,1)S(1)}, bf16[32,1024]{1,0:T(8,128)(2,1)S(1)}, u32[]{:S(2)}, u32[]{:S(2)}) collective-permute-start(bf16[32,1024]{1,0:T(8,128)(2,1)S(1)} %get-tuple-element.135), channel_id=1, source_target_pairs={{0,24},{4,28},{8,16},{12,20},{16,8},{20,12},{24,0},{28,4},{1,25},{... | collective-permute-start | bytes 196616 | tf_op jit(solution)/shard_map/ppermute | solution.py:77
  122.1 4.5 %collective-permute-start.33 = (bf16[32,1024]{1,0:T(8,128)(2,1)S(1)}, bf16[32,1024]{1,0:T(8,128)(2,1)S(1)}, u32[]{:S(2)}, u32[]{:S(2)}) collective-permute-start(bf16[32,1024]{1,0:T(8,128)(2,1)S(1)} %select_convert_fusion), channel_id=1, source_target_pairs={{0,8},{4,12},{8,0},{12,4},{16,24},{20,28},{24,16},{28,20},{1,9},{5... | collective-permute-start | bytes 196616 | tf_op jit(solution)/shard_map/ppermute | solution.py:77
  122.2 5.2 %collective-permute-start.34 = (bf16[32,1024]{1,0:T(8,128)(2,1)S(1)}, bf16[32,1024]{1,0:T(8,128)(2,1)S(1)}, u32[]{:S(2)}, u32[]{:S(2)}) collective-permute-start(bf16[32,1024]{1,0:T(8,128)(2,1)S(1)} %select_convert_fusion), channel_id=1, source_target_pairs={{0,16},{4,20},{8,24},{12,28},{16,0},{20,4},{24,8},{28,12},{1,17},{... | collective-permute-start | bytes 196616 | tf_op jit(solution)/shard_map/ppermute | solution.py:77
  124.0 6.1 %collective-permute-start.35 = (bf16[32,1024]{1,0:T(8,128)(2,1)S(1)}, bf16[32,1024]{1,0:T(8,128)(2,1)S(1)}, u32[]{:S(2)}, u32[]{:S(2)}) collective-permute-start(bf16[32,1024]{1,0:T(8,128)(2,1)S(1)} %select_convert_fusion), channel_id=1, source_target_pairs={{0,24},{4,28},{8,16},{12,20},{16,8},{20,12},{24,0},{28,4},{1,25},{... | collective-permute-start | bytes 196616 | tf_op jit(solution)/shard_map/ppermute | solution.py:77
  131.0 1.3 collective-permute-start.36
  132.4 4.9 %collective-permute-start.39 = (f32[2,32,128]{2,1,0:T(8,128)S(1)}, f32[2,32,128]{2,1,0:T(8,128)S(1)}, u32[]{:S(2)}, u32[]{:S(2)}) collective-permute-start(f32[2,32,128]{2,1,0:T(8,128)S(1)} %pad_maximum_fusion.8), channel_id=1, source_target_pairs={{0,6},{1,7},{2,4},{3,5},{4,2},{5,3},{6,0},{7,1},{8,14},{9,15},{10,... | collective-permute-start | bytes 98312 | tf_op jit(solution)/shard_map/ppermute | solution.py:333
  133.4 4.2 %collective-permute-start.38 = (f32[2,32,128]{2,1,0:T(8,128)S(1)}, f32[2,32,128]{2,1,0:T(8,128)S(1)}, u32[]{:S(2)}, u32[]{:S(2)}) collective-permute-start(f32[2,32,128]{2,1,0:T(8,128)S(1)} %pad_maximum_fusion.7), channel_id=1, source_target_pairs={{0,4},{4,0},{8,12},{12,8},{16,20},{20,16},{24,28},{28,24},{1,5},{5... | collective-permute-start | bytes 98312 | tf_op jit(solution)/shard_map/ppermute | solution.py:77
  134.1 3.9 %collective-permute-start.37 = (f32[2,32,128]{2,1,0:T(8,128)S(1)}, f32[2,32,128]{2,1,0:T(8,128)S(1)}, u32[]{:S(2)}, u32[]{:S(2)}) collective-permute-start(f32[2,32,128]{2,1,0:T(8,128)S(1)} %pad_maximum_fusion.6), channel_id=1, source_target_pairs={{0,2},{1,3},{2,0},{3,1},{4,6},{5,7},{6,4},{7,5},{8,10},{9,11},{10,... | collective-permute-start | bytes 98312 | tf_op jit(solution)/shard_map/ppermute | solution.py:77

commit v3 on v2

--- a/solution.py
+++ b/solution.py
@@ -122,24 +122,30 @@
 def pack_kernel(ids, pattern, *outs):
     cols = outs[0].shape[1]
     row = lax.axis_index("row")
-    for y in range(2):
-        for layer in range(LAYERS):
+    for layer in reversed(range(LAYERS)):
+        for y in range(2):
             i = row ^ (2 * layer + y)
             for t in range(cols):
                 slot = jnp.int32(0)
                 for e in range(1, cols):
                     slot = jnp.where(ids[e, i] == t, e, slot)
-                outs[y][layer, t] = pattern[i * cols + slot].astype(jnp.float32).astype(jnp.bfloat16)
+                tile = pattern[i * cols + slot].astype(jnp.float32).astype(jnp.bfloat16)
+                if layer:
+                    outs[y][layer - 1, t] = tile
+                else:
+                    outs[2][y, t] = tile
+                    outs[3][1 - y, t] = tile
 
 
 def packed_block(ids, pattern):
     cols, tile = ids.shape[0], pattern.shape[-1]
-    half = jax.ShapeDtypeStruct((LAYERS, cols, tile, tile), jnp.bfloat16)
+    other = jax.ShapeDtypeStruct((LAYERS - 1, cols, tile, tile), jnp.bfloat16)
+    own = jax.ShapeDtypeStruct((2, cols, tile, tile), jnp.bfloat16)
     return pl.pallas_call(
         pack_kernel,
-        out_shape=[half] * 2,
+        out_shape=[other, other, own, own],
         in_specs=[IN_SMEM, IN_VMEM],
-        out_specs=[IN_VMEM] * 2,
+        out_specs=[IN_VMEM] * 4,
         compiler_params=pltpu.CompilerParams(vmem_limit_bytes=8 * 1024 * 1024),
         name="pack",
     )(ids, pattern)
@@ -207,14 +213,15 @@
 
 
 def first_kernel(base, front, *rest):
-    outs = rest[-LAYERS:]
-    start = rest[:LAYERS] if base else None
-    halves = rest[LAYERS if base else 0 : -LAYERS]
+    count = LAYERS - 1
+    outs = rest[-count:]
+    start = rest[:count] if base else None
+    halves = rest[count if base else 0 : -count]
     pairs = ((1, 2), (1, 3)) if base else tuple((at // 4, at % 4) for at in range(6))
     layers, cols, tile, _ = halves[0].shape
     wide = cols * tile
     col = lax.axis_index("col")
-    for layer in range(layers):
+    for layer in reversed(range(layers)):
         for flip in range(cols):
             terms = None
             for at, (side, c) in enumerate(pairs):
@@ -237,45 +244,50 @@
 
 def first_terms(front, base, halves):
     shape = jax.ShapeDtypeStruct(front.shape, jnp.float32)
-    flops = 2 * front.shape[0] * len(halves) * halves[0].size
+    count = LAYERS - 1
+    size = len(halves) * halves[0].size
     return pl.pallas_call(
         functools.partial(first_kernel, bool(base)),
-        out_shape=[shape] * LAYERS,
+        out_shape=[shape] * count,
         in_specs=[IN_VMEM] * (1 + len(base) + len(halves)),
-        out_specs=[IN_VMEM] * LAYERS,
+        out_specs=[IN_VMEM] * count,
         compiler_params=pltpu.CompilerParams(vmem_limit_bytes=12 * 1024 * 1024),
-        cost_estimate=pl.CostEstimate(flops=flops, bytes_accessed=len(halves) * halves[0].size * 2, transcendentals=0),
+        cost_estimate=pl.CostEstimate(
+            flops=2 * front.shape[0] * size, bytes_accessed=2 * size, transcendentals=0
+        ),
         name="first",
     )(front, *base, *halves)
 
 
-def assemble_kernel(count, *rest):
+def assemble_kernel(parts, count, *rest):
     blocks, outs = rest[:count], rest[count:]
-    layers, cols, tile, _ = blocks[0].shape
+    _, cols, tile, _ = blocks[0].shape
     col = lax.axis_index("col")
-    for layer in range(layers):
-        for at, block in enumerate(blocks):
+    for layer, out in enumerate(outs):
+        for at in range(count * 2 // parts):
             side, flip, y = at // (2 * cols), at // 2 % cols, at % 2
+            block, lead = (blocks[at], layer) if parts == 2 else (blocks[at // 2], y)
             rows = pl.ds(pl.multiple_of((y * cols + (col ^ flip)) * tile, tile), tile)
             for t in range(cols):
                 start = (side * cols + t) * tile
-                outs[layer][rows, start : start + tile] = block[layer, t]
-
-
-def assembled(near, far):
-    layers, cols, tile, _ = near[0].shape
+                out[rows, start : start + tile] = block[lead, t]
+
+
+def assembled(blocks, parts):
+    lead, cols, tile, _ = blocks[0].shape
     span = 2 * cols * tile
-    return pl.pallas_call(
-        functools.partial(assemble_kernel, len(near + far)),
+    layers = lead if parts == 2 else 1
+    return pl.pallas_call(
+        functools.partial(assemble_kernel, parts, len(blocks)),
         out_shape=[jax.ShapeDtypeStruct((span, span), jnp.bfloat16)] * layers,
-        in_specs=[IN_VMEM] * len(near + far),
+        in_specs=[IN_VMEM] * len(blocks),
         out_specs=[IN_VMEM] * layers,
-        compiler_params=pltpu.CompilerParams(vmem_limit_bytes=20 * 1024 * 1024),
+        compiler_params=pltpu.CompilerParams(vmem_limit_bytes=16 * 1024 * 1024),
         cost_estimate=pl.CostEstimate(
-            flops=0, bytes_accessed=4 * len(near + far) * near[0].size, transcendentals=0
+            flops=0, bytes_accessed=4 * len(blocks) * blocks[0].size, transcendentals=0
         ),
         name="assemble",
-    )(*near, *far)
+    )(*blocks)
 
 
 def spread_kernel(found, keep, send):
@@ -338,7 +350,7 @@
     vert, _ = paths_in.shape
     tile = pattern.shape[-1]
 
-    own = packed_block(tile_src[0, 0].T, pattern[0, 0].reshape(-1, tile, tile))
+    *own, same, flipped = packed_block(tile_src[0, 0].T, pattern[0, 0].reshape(-1, tile, tile))
     keep, send = packed_inputs(paths_in, dep_in, levels)
     pieces = traded(keep, send)
     by_y = [swap(own[1], "row", 1)]
@@ -355,6 +367,9 @@
     masks = [word < 0.0, word == 0.5, word == 0.25, word >= 1.0]
 
     cross = [swap(by_y[0], "col", 2), swap(by_x[0], "row", 1)]
+    same_y = swap(flipped, "row", 1)
+    same_x = swap(same, "col", 2)
+    same_d = lax.ppermute(flipped, ("row", "col"), diagonal())
     crossed = [swap(by_x[0], "col", 1), swap(by_y[0], "col", 1)]
     crossed += [swap(by_x[1], "col", 1), swap(by_y[1], "col", 1)]
     near = list(own) + by_core + by_x + [crossed[0], crossed[2]]
@@ -362,7 +377,12 @@
     last = cross + [swap(half, "col", 1) for half in cross]
     first = first_terms(front, [], near + far)
     first = first_terms(front, first, last)
-    whole = assembled(near, far + last)
+    blocks = [
+        part
+        for block in (same, same_x, same_y, same_d)
+        for part in (block, swap(block, "col", 1))
+    ]
+    whole = assembled(blocks, 1) + assembled(near + far + last, 2)
 
     def forward(front, k):
         dims = (((1,), (1,)), ((), ()))
@@ -376,10 +396,10 @@
     counts = [None]
     for distance in (1, 2, 3):
         def terms(k):
-            return first[k] if distance == 1 else forward(counts[-1], k)
+            return forward(counts[-1], k) if distance > 1 else first[k - 1]
 
         got = across(lambda k: coded(terms(k)))
-        total = terms(0)
+        total = forward(front if distance == 1 else counts[-1], 0)
         for k in range(1, LAYERS):
             total = total + decoded(got[k])
         counts.append(jnp.where(masks[distance], total, 0.0))

time: 139 us -> 145 us (1.043)
  local copies, waits for them, and re-layouts: 2.32 us -> 5.03 us
  waiting for transfers between devices: 67.7 us -> 69.6 us
    ppermute x0 -> x1, waiting for transfers between devices: none -> 10.8 us  [split_shards(): same_d = lax.ppermute(flipped, ('row', 'col'), diagonal())]
    ppermute x38 -> x44, waiting for transfers between devices: 64.2 us -> 57.6 us  [swap(): return lax.ppermute(value, axis, partner(axis, bit))]
    ppermute x0 -> x1, starting transfers between devices: none -> 2.98 us  [split_shards(): same_d = lax.ppermute(flipped, ('row', 'col'), diagonal())]
    unnamed x10 -> x14, local copies, waits for them, and re-layouts: 2.28 us -> 5 us
    ppermute x2, waiting for transfers between devices: 3.43 us -> 1.22 us  [traded(): from_d = lax.ppermute(held[3], ('row', 'col'), diagonal())]
    ppermute x38 -> x44, starting transfers between devices: 43.4 us -> 41.6 us  [swap(): return lax.ppermute(value, axis, partner(axis, bit))]
    dot_general x8 -> x9, matrix products: 7.52 us -> 8.36 us  [forward(): lax.dot_general(front.astype(jnp.bfloat16), whole[k], dims, preferred_ele...]
    pallas_call x2 -> x3, Pallas kernels: 2.9 us -> 2.9 us  [the longest x2 2.18 us: assembled(): pl.pallas_call(functools.partial(assemble_kernel, parts, len(blocks)), ou...]
  transfers between devices with their start and end apart: 40 -> 47, of which waited for: 21 -> 25; matrix products, arithmetic and copies ran while one was open for 4% -> 4% of each run, Pallas kernels for 3% -> 3%
where the time goes in v3:
time: 145 us; the launch traced here: 144 us
  waiting for transfers between devices  69.6 us (48%)
  starting transfers between devices  48.1 us (33%)
  matrix products  14.1 us (10%)
  Pallas kernels  5.9 us (4%)
  local copies, waits for them, and re-layouts  5.03 us (3%)
    ppermute x44, waiting for transfers between devices, swap(): return lax.ppermute(value, axis, partner(axis, bit))  57.6 us
    ppermute x44, starting transfers between devices, swap(): return lax.ppermute(value, axis, partner(axis, bit))  41.6 us
    ppermute x1, waiting for transfers between devices, split_shards(): same_d = lax.ppermute(flipped, ('row', 'col'), diagonal())  10.8 us
    dot_general x9, matrix products, forward(): lax.dot_general(front.astype(jnp.bfloat16), whole[k], dims, preferred_ele...  8.36 us
    dot_general x12, matrix products, split_shards(): jnp.dot(got[k], whole[k], preferred_element_type=jnp.float32)  5.7 us
    unnamed x14, local copies, waits for them, and re-layouts  5 us
    ppermute x2, starting transfers between devices, traded(): from_d = lax.ppermute(held[3], ('row', 'col'), diagonal())  3.59 us
    ppermute x1, starting transfers between devices, split_shards(): same_d = lax.ppermute(flipped, ('row', 'col'), diagonal())  2.98 us
  transfers between devices with their start and end apart: 47, of which 25 were waited for; matrix products, arithmetic and copies ran while one was open for 4% of the time, Pallas kernels for 3%

profile of v3, /device:TPU:0, one launch (start us, length us, event | category | flops | bytes accessed | tf_op | source)
XLA Modules:
  0.0 144.4 jit_solution(8652363470562791662)
XLA Ops:
  3.4 1.6 %copy-done = s32[1,1,8,4,128,128]{5,4,3,2,1,0:T(8,128)S(1)} copy-done((s32[1,1,8,4,128,128]{5,4,3,2,1,0:T(8,128)S(1)}, s32[1,1,8,4,128,128]{5,4,3,2,1,0:T(8,128)}, u32[]{:S(2)}) %copy-start) | copy-done | bytes 2097176
  6.4 2.6 %collective-permute-start.5 = (bf16[2,4,128,128]{3,2,1,0:T(8,128)(2,1)S(1)}, bf16[2,4,128,128]{3,2,1,0:T(8,128)(2,1)S(1)}, u32[]{:S(2)}, u32[]{:S(2)}) collective-permute-start(bf16[2,4,128,128]{3,2,1,0:T(8,128)(2,1)S(1)} %get-tuple-element.32.rest_0_), channel_id=1, source_target_pairs={{0,2},{1,3},{2,0},{3,1},{4,6},{5,7},{6,4},{7,5},{8,10},{9,11},{10,... | collective-permute-start | bytes 786440 | tf_op jit(solution)/shard_map/ppermute | solution.py:77
  9.1 2.0 %collective-permute-start.2 = (f32[2,32,128]{2,1,0:T(8,128)S(1)}, f32[2,32,128]{2,1,0:T(8,128)S(1)}, u32[]{:S(2)}, u32[]{:S(2)}) collective-permute-start(f32[2,32,128]{2,1,0:T(8,128)S(1)} %pad_maximum_fusion.3), channel_id=1, source_target_pairs={{0,4},{4,0},{8,12},{12,8},{16,20},{20,16},{24,28},{28,24},{1,5},{5... | collective-permute-start | bytes 98312 | tf_op jit(solution)/shard_map/ppermute | solution.py:77
  11.1 1.4 collective-permute-start.3
  12.7 4.2 %collective-permute-done.1.rest_1_ = f32[2,32,128]{2,1,0:T(8,128)S(1)} collective-permute-done((f32[2,32,128]{2,1,0:T(8,128)S(1)}, f32[2,32,128]{2,1,0:T(8,128)S(1)}, u32[]{:S(2)}, u32[]{:S(2)}) %collective-permute-start.1) | collective-permute-done | bytes 32800 | tf_op jit(solution)/shard_map/ppermute | solution.py:77
  16.8 3.0 %collective-permute-start.9 = (bf16[2,4,128,128]{3,2,1,0:T(8,128)(2,1)S(1)}, bf16[2,4,128,128]{3,2,1,0:T(8,128)(2,1)S(1)}, u32[]{:S(2)}, u32[]{:S(2)}) collective-permute-start(bf16[2,4,128,128]{3,2,1,0:T(8,128)(2,1)S(1)} %get-tuple-element.33), channel_id=1, source_target_pairs={{0,6},{1,7},{2,4},{3,5},{4,2},{5,3},{6,0},{7,1},{8,14},{9,15},{10,... | collective-permute-start | bytes 786440 | tf_op jit(solution)/shard_map/ppermute | solution.py:372
  20.3 1.6 %collective-permute-start.17 = (bf16[3,4,128,128]{3,2,1,0:T(8,128)(2,1)S(1)}, bf16[3,4,128,128]{3,2,1,0:T(8,128)(2,1)S(1)}, u32[]{:S(2)}, u32[]{:S(2)}) collective-permute-start(bf16[3,4,128,128]{3,2,1,0:T(8,128)(2,1)S(1)} %get-tuple-element.35.rest_1_), channel_id=1, source_target_pairs={{0,4},{4,0},{8,12},{12,8},{16,20},{20,16},{24,28},{28,24},{1,5},{5... | collective-permute-start | bytes 1179656 | tf_op jit(solution)/shard_map/ppermute | solution.py:77
  21.9 10.8 %collective-permute-done.9.rest_6_ = bf16[2,4,128,128]{3,2,1,0:T(8,128)(2,1)S(1)} collective-permute-done((bf16[2,4,128,128]{3,2,1,0:T(8,128)(2,1)S(1)}, bf16[2,4,128,128]{3,2,1,0:T(8,128)(2,1)S(1)}, u32[]{:S(2)}, u32[]{:S(2)}) %collective-permute-start.9) | collective-permute-done | bytes 262176 | tf_op jit(solution)/shard_map/ppermute | solution.py:372
  32.7 1.5 %collective-permute-start.14 = (bf16[3,4,128,128]{3,2,1,0:T(8,128)(2,1)S(1)}, bf16[3,4,128,128]{3,2,1,0:T(8,128)(2,1)S(1)}, u32[]{:S(2)}, u32[]{:S(2)}) collective-permute-start(bf16[3,4,128,128]{3,2,1,0:T(8,128)(2,1)S(1)} %get-tuple-element.35.rest_1_), channel_id=1, source_target_pairs={{0,2},{1,3},{2,0},{3,1},{4,6},{5,7},{6,4},{7,5},{8,10},{9,11},{10,... | collective-permute-start | bytes 1179656 | tf_op jit(solution)/shard_map/ppermute | solution.py:77
  35.6 7.4 %collective-permute-done.17.rest_8_ = bf16[3,4,128,128]{3,2,1,0:T(8,128)(2,1)S(1)} collective-permute-done((bf16[3,4,128,128]{3,2,1,0:T(8,128)(2,1)S(1)}, bf16[3,4,128,128]{3,2,1,0:T(8,128)(2,1)S(1)}, u32[]{:S(2)}, u32[]{:S(2)}) %collective-permute-start.17) | collective-permute-done | bytes 393248 | tf_op jit(solution)/shard_map/ppermute | solution.py:77
  43.5 5.8 %collective-permute-done.18.rest_9_ = bf16[3,4,128,128]{3,2,1,0:T(8,128)(2,1)S(1)} collective-permute-done((bf16[3,4,128,128]{3,2,1,0:T(8,128)(2,1)S(1)}, bf16[3,4,128,128]{3,2,1,0:T(8,128)(2,1)S(1)}, u32[]{:S(2)}, u32[]{:S(2)}) %collective-permute-start.18) | collective-permute-done | bytes 393248 | tf_op jit(solution)/shard_map/ppermute | solution.py:77
  51.0 1.0 collective-permute-done.10.rest_7_
  52.9 5.5 %collective-permute-done.21.rest_3_.rest_12_ = bf16[3,4,128,128]{3,2,1,0:T(8,128)(2,1)S(1)} collective-permute-done((bf16[3,4,128,128]{3,2,1,0:T(8,128)(2,1)S(1)}, bf16[3,4,128,128]{3,2,1,0:T(8,128)(2,1)S(1)}, u32[]{:S(2)}, u32[]{:S(2)}) %collective-permute-start.21) | collective-permute-done | bytes 393248 | tf_op jit(solution)/shard_map/ppermute | solution.py:77
  59.6 1.5 %first.2 = (f32[32,1024]{1,0:T(8,128)S(1)}, f32[32,1024]{1,0:T(8,128)S(1)}, f32[32,1024]{1,0:T(8,128)S(1)}) custom-call(bf16[32,1024]{1,0:T(8,128)(2,1)S(1)} %get-tuple-element.31.front, bf16[3,4,128,128]{3,2,1,0:T(8,128)(2,1)S(1)} %get-tuple-element.34.rest_0_, bf16[3,4,128,128]{3,2,1,0:T(8,128)(2,1)S(1)} %get-tuple-element.35.rest_1_, ...), custom_call_target="tpu_custom_call" | custom-call | flops 150994944 | bytes 4718592 | tf_op jit(solution)/shard_map/first/pallas_call | solution.py:249
  62.1 1.6 %collective-permute-start.25 = (s32[32,768]{1,0:T(8,128)S(1)}, s32[32,768]{1,0:T(8,128)S(1)}, u32[]{:S(2)}, u32[]{:S(2)}) collective-permute-start(s32[32,768]{1,0:T(8,128)S(1)} %pad_add_fusion.9), channel_id=1, source_target_pairs={{0,8},{4,12},{8,0},{12,4},{16,24},{20,28},{24,16},{28,20},{1,9},{5... | collective-permute-start | bytes 294920 | tf_op jit(solution)/shard_map/ppermute | solution.py:77
  63.8 2.7 %collective-permute-start.26 = (s32[32,768]{1,0:T(8,128)S(1)}, s32[32,768]{1,0:T(8,128)S(1)}, u32[]{:S(2)}, u32[]{:S(2)}) collective-permute-start(s32[32,768]{1,0:T(8,128)S(1)} %pad_add_fusion.10), channel_id=1, source_target_pairs={{0,16},{4,20},{8,24},{12,28},{16,0},{20,4},{24,8},{28,12},{1,17},{... | collective-permute-start | bytes 294920 | tf_op jit(solution)/shard_map/ppermute | solution.py:77
  66.9 1.6 %assemble.3 = (bf16[1024,1024]{1,0:T(8,128)(2,1)S(1)}, bf16[1024,1024]{1,0:T(8,128)(2,1)S(1)}, bf16[1024,1024]{1,0:T(8,128)(2,1)S(1)}) custom-call(bf16[3,4,128,128]{3,2,1,0:T(8,128)(2,1)S(1)} %get-tuple-element.34.rest_0_, bf16[3,4,128,128]{3,2,1,0:T(8,128)(2,1)S(1)} %get-tuple-element.35.rest_1_, ...), custom_call_target="tpu_custom_call" | custom-call | bytes 12582912 | tf_op jit(solution)/shard_map/assemble/pallas_call | solution.py:280
  68.6 5.8 %collective-permute-done.26 = s32[32,768]{1,0:T(8,128)S(1)} collective-permute-done((s32[32,768]{1,0:T(8,128)S(1)}, s32[32,768]{1,0:T(8,128)S(1)}, u32[]{:S(2)}, u32[]{:S(2)}) %collective-permute-start.26) | collective-permute-done | bytes 98336 | tf_op jit(solution)/shard_map/ppermute | solution.py:77
  74.4 1.0 fusion.153
  76.4 1.9 %collective-permute-start.28 = (s32[32,768]{1,0:T(8,128)S(1)}, s32[32,768]{1,0:T(8,128)S(1)}, u32[]{:S(2)}, u32[]{:S(2)}) collective-permute-start(s32[32,768]{1,0:T(8,128)S(1)} %pad_add_fusion.12), channel_id=1, source_target_pairs={{0,8},{4,12},{8,0},{12,4},{16,24},{20,28},{24,16},{28,20},{1,9},{5... | collective-permute-start | bytes 294920 | tf_op jit(solution)/shard_map/ppermute | solution.py:77
  79.2 1.5 %collective-permute-start.29 = (s32[32,768]{1,0:T(8,128)S(1)}, s32[32,768]{1,0:T(8,128)S(1)}, u32[]{:S(2)}, u32[]{:S(2)}) collective-permute-start(s32[32,768]{1,0:T(8,128)S(1)} %pad_add_fusion.13), channel_id=1, source_target_pairs={{0,16},{4,20},{8,24},{12,28},{16,0},{20,4},{24,8},{28,12},{1,17},{... | collective-permute-start | bytes 294920 | tf_op jit(solution)/shard_map/ppermute | solution.py:77
  81.6 1.2 collective-permute-start.30
  82.9 6.1 %collective-permute-done.29 = s32[32,768]{1,0:T(8,128)S(1)} collective-permute-done((s32[32,768]{1,0:T(8,128)S(1)}, s32[32,768]{1,0:T(8,128)S(1)}, u32[]{:S(2)}, u32[]{:S(2)}) %collective-permute-start.29) | collective-permute-done | bytes 98336 | tf_op jit(solution)/shard_map/ppermute | solution.py:77
  89.0 1.0 fusion.154
  92.8 1.7 %collective-permute-start.31 = (s32[32,768]{1,0:T(8,128)S(1)}, s32[32,768]{1,0:T(8,128)S(1)}, u32[]{:S(2)}, u32[]{:S(2)}) collective-permute-start(s32[32,768]{1,0:T(8,128)S(1)} %pad_add_fusion.15), channel_id=1, source_target_pairs={{0,8},{4,12},{8,0},{12,4},{16,24},{20,28},{24,16},{28,20},{1,9},{5... | collective-permute-start | bytes 294920 | tf_op jit(solution)/shard_map/ppermute | solution.py:77
  94.5 1.4 collective-permute-start.32
  95.9 1.5 %collective-permute-start.33 = (s32[32,768]{1,0:T(8,128)S(1)}, s32[32,768]{1,0:T(8,128)S(1)}, u32[]{:S(2)}, u32[]{:S(2)}) collective-permute-start(s32[32,768]{1,0:T(8,128)S(1)} %pad_add_fusion.17), channel_id=1, source_target_pairs={{0,24},{4,28},{8,16},{12,20},{16,8},{20,12},{24,0},{28,4},{1,25},{... | collective-permute-start | bytes 294920 | tf_op jit(solution)/shard_map/ppermute | solution.py:77
  97.4 0.9 collective-permute-done.31
  98.4 5.8 %collective-permute-done.32 = s32[32,768]{1,0:T(8,128)S(1)} collective-permute-done((s32[32,768]{1,0:T(8,128)S(1)}, s32[32,768]{1,0:T(8,128)S(1)}, u32[]{:S(2)}, u32[]{:S(2)}) %collective-permute-start.32) | collective-permute-done | bytes 98336 | tf_op jit(solution)/shard_map/ppermute | solution.py:77
  104.4 1.0 fusion.21
  105.5 1.6 %collective-permute-start.34 = (bf16[32,1024]{1,0:T(8,128)(2,1)S(1)}, bf16[32,1024]{1,0:T(8,128)(2,1)S(1)}, u32[]{:S(2)}, u32[]{:S(2)}) collective-permute-start(bf16[32,1024]{1,0:T(8,128)(2,1)S(1)} %fusion.21), channel_id=1, source_target_pairs={{0,8},{4,12},{8,0},{12,4},{16,24},{20,28},{24,16},{28,20},{1,9},{5... | collective-permute-start | bytes 196616 | tf_op jit(solution)/shard_map/ppermute | solution.py:77
  107.1 1.0 collective-permute-start.35
  108.2 1.8 %collective-permute-start.36 = (bf16[32,1024]{1,0:T(8,128)(2,1)S(1)}, bf16[32,1024]{1,0:T(8,128)(2,1)S(1)}, u32[]{:S(2)}, u32[]{:S(2)}) collective-permute-start(bf16[32,1024]{1,0:T(8,128)(2,1)S(1)} %fusion.21), channel_id=1, source_target_pairs={{0,24},{4,28},{8,16},{12,20},{16,8},{20,12},{24,0},{28,4},{1,25},{... | collective-permute-start | bytes 196616 | tf_op jit(solution)/shard_map/ppermute | solution.py:77
  111.0 2.7 %collective-permute-done.35 = bf16[32,1024]{1,0:T(8,128)(2,1)S(1)} collective-permute-done((bf16[32,1024]{1,0:T(8,128)(2,1)S(1)}, bf16[32,1024]{1,0:T(8,128)(2,1)S(1)}, u32[]{:S(2)}, u32[]{:S(2)}) %collective-permute-start.35) | collective-permute-done | bytes 65568 | tf_op jit(solution)/shard_map/ppermute | solution.py:77
  115.4 1.3 collective-permute-start.37
  116.7 2.1 %collective-permute-start.38 = (bf16[32,1024]{1,0:T(8,128)(2,1)S(1)}, bf16[32,1024]{1,0:T(8,128)(2,1)S(1)}, u32[]{:S(2)}, u32[]{:S(2)}) collective-permute-start(bf16[32,1024]{1,0:T(8,128)(2,1)S(1)} %get-tuple-element.134), channel_id=1, source_target_pairs={{0,16},{4,20},{8,24},{12,28},{16,0},{20,4},{24,8},{28,12},{1,17},{... | collective-permute-start | bytes 196616 | tf_op jit(solution)/shard_map/ppermute | solution.py:77
  118.8 1.1 collective-permute-start.39
  120.4 2.7 %collective-permute-done.38 = bf16[32,1024]{1,0:T(8,128)(2,1)S(1)} collective-permute-done((bf16[32,1024]{1,0:T(8,128)(2,1)S(1)}, bf16[32,1024]{1,0:T(8,128)(2,1)S(1)}, u32[]{:S(2)}, u32[]{:S(2)}) %collective-permute-start.38) | collective-permute-done | bytes 65568 | tf_op jit(solution)/shard_map/ppermute | solution.py:77
  123.5 1.4 collective-permute-done.39
  125.9 1.7 %collective-permute-start.41 = (bf16[32,1024]{1,0:T(8,128)(2,1)S(1)}, bf16[32,1024]{1,0:T(8,128)(2,1)S(1)}, u32[]{:S(2)}, u32[]{:S(2)}) collective-permute-start(bf16[32,1024]{1,0:T(8,128)(2,1)S(1)} %get-tuple-element.136), channel_id=1, source_target_pairs={{0,16},{4,20},{8,24},{12,28},{16,0},{20,4},{24,8},{28,12},{1,17},{... | collective-permute-start | bytes 196616 | tf_op jit(solution)/shard_map/ppermute | solution.py:77
  127.6 2.7 %collective-permute-start.42 = (bf16[32,1024]{1,0:T(8,128)(2,1)S(1)}, bf16[32,1024]{1,0:T(8,128)(2,1)S(1)}, u32[]{:S(2)}, u32[]{:S(2)}) collective-permute-start(bf16[32,1024]{1,0:T(8,128)(2,1)S(1)} %get-tuple-element.136), channel_id=1, source_target_pairs={{0,24},{4,28},{8,16},{12,20},{16,8},{20,12},{24,0},{28,4},{1,25},{... | collective-permute-start | bytes 196616 | tf_op jit(solution)/shard_map/ppermute | solution.py:77
  131.6 2.1 %collective-permute-done.42 = bf16[32,1024]{1,0:T(8,128)(2,1)S(1)} collective-permute-done((bf16[32,1024]{1,0:T(8,128)(2,1)S(1)}, bf16[32,1024]{1,0:T(8,128)(2,1)S(1)}, u32[]{:S(2)}, u32[]{:S(2)}) %collective-permute-start.42) | collective-permute-done | bytes 65568 | tf_op jit(solution)/shard_map/ppermute | solution.py:77
  134.8 1.2 collective-permute-done.43
  136.1 2.2 %collective-permute-start.46 = (f32[2,32,128]{2,1,0:T(8,128)S(1)}, f32[2,32,128]{2,1,0:T(8,128)S(1)}, u32[]{:S(2)}, u32[]{:S(2)}) collective-permute-start(f32[2,32,128]{2,1,0:T(8,128)S(1)} %pad_maximum_fusion.8), channel_id=1, source_target_pairs={{0,6},{1,7},{2,4},{3,5},{4,2},{5,3},{6,0},{7,1},{8,14},{9,15},{10,... | collective-permute-start | bytes 98312 | tf_op jit(solution)/shard_map/ppermute | solution.py:345
  138.2 1.5 %collective-permute-start.45 = (f32[2,32,128]{2,1,0:T(8,128)S(1)}, f32[2,32,128]{2,1,0:T(8,128)S(1)}, u32[]{:S(2)}, u32[]{:S(2)}) collective-permute-start(f32[2,32,128]{2,1,0:T(8,128)S(1)} %pad_maximum_fusion.7), channel_id=1, source_target_pairs={{0,4},{4,0},{8,12},{12,8},{16,20},{20,16},{24,28},{28,24},{1,5},{5... | collective-permute-start | bytes 98312 | tf_op jit(solution)/shard_map/ppermute | solution.py:77
  139.7 1.2 collective-permute-done.46.rest_3_
  141.0 1.2 collective-permute-done.45.rest_2_
  142.1 1.5 %collective-permute-done.44.rest_1_ = f32[2,32,128]{2,1,0:T(8,128)S(1)} collective-permute-done((f32[2,32,128]{2,1,0:T(8,128)S(1)}, f32[2,32,128]{2,1,0:T(8,128)S(1)}, u32[]{:S(2)}, u32[]{:S(2)}) %collective-permute-start.44) | collective-permute-done | bytes 32800 | tf_op jit(solution)/shard_map/ppermute | solution.py:77
  (135 shorter events, 26.0 us)
Async XLA Ops:
  2.8 6.1 %collective-permute-start = (f32[4,32,128]{2,1,0:T(8,128)S(1)}, f32[4,32,128]{2,1,0:T(8,128)S(1)}, u32[]{:S(2)}, u32[]{:S(2)}) collective-permute-start(f32[4,32,128]{2,1,0:T(8,128)S(1)} %get-tuple-element.29), channel_id=1, source_target_pairs={{0,1},{1,0},{2,3},{3,2},{4,5},{5,4},{6,7},{7,6},{8,9},{9,8},{10,11... | collective-permute-start | bytes 196616 | tf_op jit(solution)/shard_map/ppermute | solution.py:77
  6.4 13.9 %collective-permute-start.5 = (bf16[2,4,128,128]{3,2,1,0:T(8,128)(2,1)S(1)}, bf16[2,4,128,128]{3,2,1,0:T(8,128)(2,1)S(1)}, u32[]{:S(2)}, u32[]{:S(2)}) collective-permute-start(bf16[2,4,128,128]{3,2,1,0:T(8,128)(2,1)S(1)} %get-tuple-element.32.rest_0_), channel_id=1, source_target_pairs={{0,2},{1,3},{2,0},{3,1},{4,6},{5,7},{6,4},{7,5},{8,10},{9,11},{10,... | collective-permute-start | bytes 786440 | tf_op jit(solution)/shard_map/ppermute | solution.py:77
  9.0 7.8 %collective-permute-start.1 = (f32[2,32,128]{2,1,0:T(8,128)S(1)}, f32[2,32,128]{2,1,0:T(8,128)S(1)}, u32[]{:S(2)}, u32[]{:S(2)}) collective-permute-start(f32[2,32,128]{2,1,0:T(8,128)S(1)} %pad_maximum_fusion.2), channel_id=1, source_target_pairs={{0,2},{1,3},{2,0},{3,1},{4,6},{5,7},{6,4},{7,5},{8,10},{9,11},{10,... | collective-permute-start | bytes 98312 | tf_op jit(solution)/shard_map/ppermute | solution.py:77
  9.1 10.7 %collective-permute-start.2 = (f32[2,32,128]{2,1,0:T(8,128)S(1)}, f32[2,32,128]{2,1,0:T(8,128)S(1)}, u32[]{:S(2)}, u32[]{:S(2)}) collective-permute-start(f32[2,32,128]{2,1,0:T(8,128)S(1)} %pad_maximum_fusion.3), channel_id=1, source_target_pairs={{0,4},{4,0},{8,12},{12,8},{16,20},{20,16},{24,28},{28,24},{1,5},{5... | collective-permute-start | bytes 98312 | tf_op jit(solution)/shard_map/ppermute | solution.py:77
  11.1 9.2 %collective-permute-start.3 = (f32[2,32,128]{2,1,0:T(8,128)S(1)}, f32[2,32,128]{2,1,0:T(8,128)S(1)}, u32[]{:S(2)}, u32[]{:S(2)}) collective-permute-start(f32[2,32,128]{2,1,0:T(8,128)S(1)} %pad_maximum_fusion.4), channel_id=1, source_target_pairs={{0,6},{1,7},{2,4},{3,5},{4,2},{5,3},{6,0},{7,1},{8,14},{9,15},{10,... | collective-permute-start | bytes 98312 | tf_op jit(solution)/shard_map/ppermute | solution.py:345
  12.6 22.5 %collective-permute-start.13 = (bf16[3,4,128,128]{3,2,1,0:T(8,128)(2,1)S(1)}, bf16[3,4,128,128]{3,2,1,0:T(8,128)(2,1)S(1)}, u32[]{:S(2)}, u32[]{:S(2)}) collective-permute-start(bf16[3,4,128,128]{3,2,1,0:T(8,128)(2,1)S(1)} %get-tuple-element.34.rest_0_), channel_id=1, source_target_pairs={{0,2},{1,3},{2,0},{3,1},{4,6},{5,7},{6,4},{7,5},{8,10},{9,11},{10,... | collective-permute-start | bytes 1179656 | tf_op jit(solution)/shard_map/ppermute | solution.py:77
  16.8 15.9 %collective-permute-start.9 = (bf16[2,4,128,128]{3,2,1,0:T(8,128)(2,1)S(1)}, bf16[2,4,128,128]{3,2,1,0:T(8,128)(2,1)S(1)}, u32[]{:S(2)}, u32[]{:S(2)}) collective-permute-start(bf16[2,4,128,128]{3,2,1,0:T(8,128)(2,1)S(1)} %get-tuple-element.33), channel_id=1, source_target_pairs={{0,6},{1,7},{2,4},{3,5},{4,2},{5,3},{6,0},{7,1},{8,14},{9,15},{10,... | collective-permute-start | bytes 786440 | tf_op jit(solution)/shard_map/ppermute | solution.py:372
  19.8 14.8 %collective-permute-start.7 = (bf16[2,4,128,128]{3,2,1,0:T(8,128)(2,1)S(1)}, bf16[2,4,128,128]{3,2,1,0:T(8,128)(2,1)S(1)}, u32[]{:S(2)}, u32[]{:S(2)}) collective-permute-start(bf16[2,4,128,128]{3,2,1,0:T(8,128)(2,1)S(1)} %get-tuple-element.33), channel_id=1, source_target_pairs={{0,4},{4,0},{8,12},{12,8},{16,20},{20,16},{24,28},{28,24},{1,5},{5... | collective-permute-start | bytes 786440 | tf_op jit(solution)/shard_map/ppermute | solution.py:77
  20.3 14.8 %collective-permute-start.4 = (bf16[2,4,128,128]{3,2,1,0:T(8,128)(2,1)S(1)}, bf16[2,4,128,128]{3,2,1,0:T(8,128)(2,1)S(1)}, u32[]{:S(2)}, u32[]{:S(2)}) collective-permute-start(bf16[2,4,128,128]{3,2,1,0:T(8,128)(2,1)S(1)} %get-tuple-element.32.rest_0_), channel_id=1, source_target_pairs={{0,1},{1,0},{2,3},{3,2},{4,5},{5,4},{6,7},{7,6},{8,9},{9,8},{10,11... | collective-permute-start | bytes 786440 | tf_op jit(solution)/shard_map/ppermute | solution.py:77
  20.3 22.7 %collective-permute-start.17 = (bf16[3,4,128,128]{3,2,1,0:T(8,128)(2,1)S(1)}, bf16[3,4,128,128]{3,2,1,0:T(8,128)(2,1)S(1)}, u32[]{:S(2)}, u32[]{:S(2)}) collective-permute-start(bf16[3,4,128,128]{3,2,1,0:T(8,128)(2,1)S(1)} %get-tuple-element.35.rest_1_), channel_id=1, source_target_pairs={{0,4},{4,0},{8,12},{12,8},{16,20},{20,16},{24,28},{28,24},{1,5},{5... | collective-permute-start | bytes 1179656 | tf_op jit(solution)/shard_map/ppermute | solution.py:77
  32.7 10.6 %collective-permute-start.14 = (bf16[3,4,128,128]{3,2,1,0:T(8,128)(2,1)S(1)}, bf16[3,4,128,128]{3,2,1,0:T(8,128)(2,1)S(1)}, u32[]{:S(2)}, u32[]{:S(2)}) collective-permute-start(bf16[3,4,128,128]{3,2,1,0:T(8,128)(2,1)S(1)} %get-tuple-element.35.rest_1_), channel_id=1, source_target_pairs={{0,2},{1,3},{2,0},{3,1},{4,6},{5,7},{6,4},{7,5},{8,10},{9,11},{10,... | collective-permute-start | bytes 1179656 | tf_op jit(solution)/shard_map/ppermute | solution.py:77
  34.6 14.8 %collective-permute-start.18 = (bf16[3,4,128,128]{3,2,1,0:T(8,128)(2,1)S(1)}, bf16[3,4,128,128]{3,2,1,0:T(8,128)(2,1)S(1)}, u32[]{:S(2)}, u32[]{:S(2)}) collective-permute-start(bf16[3,4,128,128]{3,2,1,0:T(8,128)(2,1)S(1)} %get-tuple-element.34.rest_0_), channel_id=1, source_target_pairs={{0,4},{4,0},{8,12},{12,8},{16,20},{20,16},{24,28},{28,24},{1,5},{5... | collective-permute-start | bytes 1179656 | tf_op jit(solution)/shard_map/ppermute | solution.py:77
  35.1 14.8 %collective-permute-start.11 = (bf16[3,4,128,128]{3,2,1,0:T(8,128)(2,1)S(1)}, bf16[3,4,128,128]{3,2,1,0:T(8,128)(2,1)S(1)}, u32[]{:S(2)}, u32[]{:S(2)}) collective-permute-start(bf16[3,4,128,128]{3,2,1,0:T(8,128)(2,1)S(1)} %get-tuple-element.34.rest_0_), channel_id=1, source_target_pairs={{0,1},{1,0},{2,3},{3,2},{4,5},{5,4},{6,7},{7,6},{8,9},{9,8},{10,11... | collective-permute-start | bytes 1179656 | tf_op jit(solution)/shard_map/ppermute | solution.py:77
  35.1 15.3 %collective-permute-start.12 = (bf16[3,4,128,128]{3,2,1,0:T(8,128)(2,1)S(1)}, bf16[3,4,128,128]{3,2,1,0:T(8,128)(2,1)S(1)}, u32[]{:S(2)}, u32[]{:S(2)}) collective-permute-start(bf16[3,4,128,128]{3,2,1,0:T(8,128)(2,1)S(1)} %get-tuple-element.35.rest_1_), channel_id=1, source_target_pairs={{0,1},{1,0},{2,3},{3,2},{4,5},{5,4},{6,7},{7,6},{8,9},{9,8},{10,11... | collective-permute-start | bytes 1179656 | tf_op jit(solution)/shard_map/ppermute | solution.py:77
  43.0 7.4 %collective-permute-start.6 = (bf16[2,4,128,128]{3,2,1,0:T(8,128)(2,1)S(1)}, bf16[2,4,128,128]{3,2,1,0:T(8,128)(2,1)S(1)}, u32[]{:S(2)}, u32[]{:S(2)}) collective-permute-start(bf16[2,4,128,128]{3,2,1,0:T(8,128)(2,1)S(1)} %collective-permute-done.5.rest_2_), channel_id=1, source_target_pairs={{0,1},{1,0},{2,3},{3,2},{4,5},{5,4},{6,7},{7,6},{8,9},{9,8},{10,11... | collective-permute-start | bytes 786440 | tf_op jit(solution)/shard_map/ppermute | solution.py:77
  43.3 9.2 %collective-permute-start.15 = (bf16[3,4,128,128]{3,2,1,0:T(8,128)(2,1)S(1)}, bf16[3,4,128,128]{3,2,1,0:T(8,128)(2,1)S(1)}, u32[]{:S(2)}, u32[]{:S(2)}) collective-permute-start(bf16[3,4,128,128]{3,2,1,0:T(8,128)(2,1)S(1)} %collective-permute-done.13.rest_4_), channel_id=1, source_target_pairs={{0,1},{1,0},{2,3},{3,2},{4,5},{5,4},{6,7},{7,6},{8,9},{9,8},{10,11... | collective-permute-start | bytes 1179656 | tf_op jit(solution)/shard_map/ppermute | solution.py:77
  49.4 9.1 %collective-permute-start.21 = (bf16[3,4,128,128]{3,2,1,0:T(8,128)(2,1)S(1)}, bf16[3,4,128,128]{3,2,1,0:T(8,128)(2,1)S(1)}, u32[]{:S(2)}, u32[]{:S(2)}) collective-permute-start(bf16[3,4,128,128]{3,2,1,0:T(8,128)(2,1)S(1)} %collective-permute-done.17.rest_8_), channel_id=1, source_target_pairs={{0,2},{1,3},{2,0},{3,1},{4,6},{5,7},{6,4},{7,5},{8,10},{9,11},{10,... | collective-permute-start | bytes 1179656 | tf_op jit(solution)/shard_map/ppermute | solution.py:77
  49.9 8.8 %collective-permute-start.22 = (bf16[3,4,128,128]{3,2,1,0:T(8,128)(2,1)S(1)}, bf16[3,4,128,128]{3,2,1,0:T(8,128)(2,1)S(1)}, u32[]{:S(2)}, u32[]{:S(2)}) collective-permute-start(bf16[3,4,128,128]{3,2,1,0:T(8,128)(2,1)S(1)} %collective-permute-done.13.rest_4_), channel_id=1, source_target_pairs={{0,4},{4,0},{8,12},{12,8},{16,20},{20,16},{24,28},{28,24},{1,5},{5... | collective-permute-start | bytes 1179656 | tf_op jit(solution)/shard_map/ppermute | solution.py:77
  50.4 1.5 %collective-permute-start.10 = (bf16[2,4,128,128]{3,2,1,0:T(8,128)(2,1)S(1)}, bf16[2,4,128,128]{3,2,1,0:T(8,128)(2,1)S(1)}, u32[]{:S(2)}, u32[]{:S(2)}) collective-permute-start(bf16[2,4,128,128]{3,2,1,0:T(8,128)(2,1)S(1)} %collective-permute-done.9.rest_6_), channel_id=1, source_target_pairs={{0,1},{1,0},{2,3},{3,2},{4,5},{5,4},{6,7},{7,6},{8,9},{9,8},{10,11... | collective-permute-start | bytes 786440 | tf_op jit(solution)/shard_map/ppermute | solution.py:77
  50.5 1.9 %collective-permute-start.8 = (bf16[2,4,128,128]{3,2,1,0:T(8,128)(2,1)S(1)}, bf16[2,4,128,128]{3,2,1,0:T(8,128)(2,1)S(1)}, u32[]{:S(2)}, u32[]{:S(2)}) collective-permute-start(bf16[2,4,128,128]{3,2,1,0:T(8,128)(2,1)S(1)} %collective-permute-done.7.rest_4_), channel_id=1, source_target_pairs={{0,1},{1,0},{2,3},{3,2},{4,5},{5,4},{6,7},{7,6},{8,9},{9,8},{10,11... | collective-permute-start | bytes 786440 | tf_op jit(solution)/shard_map/ppermute | solution.py:77
  52.0 7.6 %collective-permute-start.19 = (bf16[3,4,128,128]{3,2,1,0:T(8,128)(2,1)S(1)}, bf16[3,4,128,128]{3,2,1,0:T(8,128)(2,1)S(1)}, u32[]{:S(2)}, u32[]{:S(2)}) collective-permute-start(bf16[3,4,128,128]{3,2,1,0:T(8,128)(2,1)S(1)} %collective-permute-done.17.rest_8_), channel_id=1, source_target_pairs={{0,1},{1,0},{2,3},{3,2},{4,5},{5,4},{6,7},{7,6},{8,9},{9,8},{10,11... | collective-permute-start | bytes 1179656 | tf_op jit(solution)/shard_map/ppermute | solution.py:77
  52.4 7.2 %collective-permute-start.16 = (bf16[3,4,128,128]{3,2,1,0:T(8,128)(2,1)S(1)}, bf16[3,4,128,128]{3,2,1,0:T(8,128)(2,1)S(1)}, u32[]{:S(2)}, u32[]{:S(2)}) collective-permute-start(bf16[3,4,128,128]{3,2,1,0:T(8,128)(2,1)S(1)} %collective-permute-done.14.rest_5_), channel_id=1, source_target_pairs={{0,1},{1,0},{2,3},{3,2},{4,5},{5,4},{6,7},{7,6},{8,9},{9,8},{10,11... | collective-permute-start | bytes 1179656 | tf_op jit(solution)/shard_map/ppermute | solution.py:77
  52.5 7.1 %collective-permute-start.20 = (bf16[3,4,128,128]{3,2,1,0:T(8,128)(2,1)S(1)}, bf16[3,4,128,128]{3,2,1,0:T(8,128)(2,1)S(1)}, u32[]{:S(2)}, u32[]{:S(2)}) collective-permute-start(bf16[3,4,128,128]{3,2,1,0:T(8,128)(2,1)S(1)} %collective-permute-done.18.rest_9_), channel_id=1, source_target_pairs={{0,1},{1,0},{2,3},{3,2},{4,5},{5,4},{6,7},{7,6},{8,9},{9,8},{10,11... | collective-permute-start | bytes 1179656 | tf_op jit(solution)/shard_map/ppermute | solution.py:77
  58.4 2.7 %collective-permute-start.23 = (bf16[3,4,128,128]{3,2,1,0:T(8,128)(2,1)S(1)}, bf16[3,4,128,128]{3,2,1,0:T(8,128)(2,1)S(1)}, u32[]{:S(2)}, u32[]{:S(2)}) collective-permute-start(bf16[3,4,128,128]{3,2,1,0:T(8,128)(2,1)S(1)} %collective-permute-done.21.rest_3_.rest_12_), channel_id=1, source_target_pairs={{0,1},{1,0},{2,3},{3,2},{4,5},{5,4},{6,7},{7,6},{8,9},{9,8},{10,11... | collective-permute-start | bytes 1179656 | tf_op jit(solution)/shard_map/ppermute | solution.py:77
  58.7 2.4 %collective-permute-start.24 = (bf16[3,4,128,128]{3,2,1,0:T(8,128)(2,1)S(1)}, bf16[3,4,128,128]{3,2,1,0:T(8,128)(2,1)S(1)}, u32[]{:S(2)}, u32[]{:S(2)}) collective-permute-start(bf16[3,4,128,128]{3,2,1,0:T(8,128)(2,1)S(1)} %collective-permute-done.22.rest_4_.rest_13_), channel_id=1, source_target_pairs={{0,1},{1,0},{2,3},{3,2},{4,5},{5,4},{6,7},{7,6},{8,9},{9,8},{10,11... | collective-permute-start | bytes 1179656 | tf_op jit(solution)/shard_map/ppermute | solution.py:77
  62.1 6.5 %collective-permute-start.25 = (s32[32,768]{1,0:T(8,128)S(1)}, s32[32,768]{1,0:T(8,128)S(1)}, u32[]{:S(2)}, u32[]{:S(2)}) collective-permute-start(s32[32,768]{1,0:T(8,128)S(1)} %pad_add_fusion.9), channel_id=1, source_target_pairs={{0,8},{4,12},{8,0},{12,4},{16,24},{20,28},{24,16},{28,20},{1,9},{5... | collective-permute-start | bytes 294920 | tf_op jit(solution)/shard_map/ppermute | solution.py:77
  63.8 10.6 %collective-permute-start.26 = (s32[32,768]{1,0:T(8,128)S(1)}, s32[32,768]{1,0:T(8,128)S(1)}, u32[]{:S(2)}, u32[]{:S(2)}) collective-permute-start(s32[32,768]{1,0:T(8,128)S(1)} %pad_add_fusion.10), channel_id=1, source_target_pairs={{0,16},{4,20},{8,24},{12,28},{16,0},{20,4},{24,8},{28,12},{1,17},{... | collective-permute-start | bytes 294920 | tf_op jit(solution)/shard_map/ppermute | solution.py:77
  66.6 7.8 %collective-permute-start.27 = (s32[32,768]{1,0:T(8,128)S(1)}, s32[32,768]{1,0:T(8,128)S(1)}, u32[]{:S(2)}, u32[]{:S(2)}) collective-permute-start(s32[32,768]{1,0:T(8,128)S(1)} %pad_add_fusion.11), channel_id=1, source_target_pairs={{0,24},{4,28},{8,16},{12,20},{16,8},{20,12},{24,0},{28,4},{1,25},{... | collective-permute-start | bytes 294920 | tf_op jit(solution)/shard_map/ppermute | solution.py:77
  76.4 6.5 %collective-permute-start.28 = (s32[32,768]{1,0:T(8,128)S(1)}, s32[32,768]{1,0:T(8,128)S(1)}, u32[]{:S(2)}, u32[]{:S(2)}) collective-permute-start(s32[32,768]{1,0:T(8,128)S(1)} %pad_add_fusion.12), channel_id=1, source_target_pairs={{0,8},{4,12},{8,0},{12,4},{16,24},{20,28},{24,16},{28,20},{1,9},{5... | collective-permute-start | bytes 294920 | tf_op jit(solution)/shard_map/ppermute | solution.py:77
  79.2 9.7 %collective-permute-start.29 = (s32[32,768]{1,0:T(8,128)S(1)}, s32[32,768]{1,0:T(8,128)S(1)}, u32[]{:S(2)}, u32[]{:S(2)}) collective-permute-start(s32[32,768]{1,0:T(8,128)S(1)} %pad_add_fusion.13), channel_id=1, source_target_pairs={{0,16},{4,20},{8,24},{12,28},{16,0},{20,4},{24,8},{28,12},{1,17},{... | collective-permute-start | bytes 294920 | tf_op jit(solution)/shard_map/ppermute | solution.py:77
  81.6 7.3 %collective-permute-start.30 = (s32[32,768]{1,0:T(8,128)S(1)}, s32[32,768]{1,0:T(8,128)S(1)}, u32[]{:S(2)}, u32[]{:S(2)}) collective-permute-start(s32[32,768]{1,0:T(8,128)S(1)} %pad_add_fusion.14), channel_id=1, source_target_pairs={{0,24},{4,28},{8,16},{12,20},{16,8},{20,12},{24,0},{28,4},{1,25},{... | collective-permute-start | bytes 294920 | tf_op jit(solution)/shard_map/ppermute | solution.py:77
  92.8 5.6 %collective-permute-start.31 = (s32[32,768]{1,0:T(8,128)S(1)}, s32[32,768]{1,0:T(8,128)S(1)}, u32[]{:S(2)}, u32[]{:S(2)}) collective-permute-start(s32[32,768]{1,0:T(8,128)S(1)} %pad_add_fusion.15), channel_id=1, source_target_pairs={{0,8},{4,12},{8,0},{12,4},{16,24},{20,28},{24,16},{28,20},{1,9},{5... | collective-permute-start | bytes 294920 | tf_op jit(solution)/shard_map/ppermute | solution.py:77
  94.5 9.7 %collective-permute-start.32 = (s32[32,768]{1,0:T(8,128)S(1)}, s32[32,768]{1,0:T(8,128)S(1)}, u32[]{:S(2)}, u32[]{:S(2)}) collective-permute-start(s32[32,768]{1,0:T(8,128)S(1)} %pad_add_fusion.16), channel_id=1, source_target_pairs={{0,16},{4,20},{8,24},{12,28},{16,0},{20,4},{24,8},{28,12},{1,17},{... | collective-permute-start | bytes 294920 | tf_op jit(solution)/shard_map/ppermute | solution.py:77
  95.9 8.3 %collective-permute-start.33 = (s32[32,768]{1,0:T(8,128)S(1)}, s32[32,768]{1,0:T(8,128)S(1)}, u32[]{:S(2)}, u32[]{:S(2)}) collective-permute-start(s32[32,768]{1,0:T(8,128)S(1)} %pad_add_fusion.17), channel_id=1, source_target_pairs={{0,24},{4,28},{8,16},{12,20},{16,8},{20,12},{24,0},{28,4},{1,25},{... | collective-permute-start | bytes 294920 | tf_op jit(solution)/shard_map/ppermute | solution.py:77
  104.2 2.9 %copy-start.2 = (f32[128,256]{1,0:T(8,128)S(1)}, f32[128,256]{1,0:T(8,128)}, u32[]{:S(2)}) copy-start(f32[128,256]{1,0:T(8,128)} %paths_in.1) | copy-start | bytes 393220
  105.5 5.0 %collective-permute-start.34 = (bf16[32,1024]{1,0:T(8,128)(2,1)S(1)}, bf16[32,1024]{1,0:T(8,128)(2,1)S(1)}, u32[]{:S(2)}, u32[]{:S(2)}) collective-permute-start(bf16[32,1024]{1,0:T(8,128)(2,1)S(1)} %fusion.21), channel_id=1, source_target_pairs={{0,8},{4,12},{8,0},{12,4},{16,24},{20,28},{24,16},{28,20},{1,9},{5... | collective-permute-start | bytes 196616 | tf_op jit(solution)/shard_map/ppermute | solution.py:77
  107.1 6.5 %collective-permute-start.35 = (bf16[32,1024]{1,0:T(8,128)(2,1)S(1)}, bf16[32,1024]{1,0:T(8,128)(2,1)S(1)}, u32[]{:S(2)}, u32[]{:S(2)}) collective-permute-start(bf16[32,1024]{1,0:T(8,128)(2,1)S(1)} %fusion.21), channel_id=1, source_target_pairs={{0,16},{4,20},{8,24},{12,28},{16,0},{20,4},{24,8},{28,12},{1,17},{... | collective-permute-start | bytes 196616 | tf_op jit(solution)/shard_map/ppermute | solution.py:77
  108.2 6.2 %collective-permute-start.36 = (bf16[32,1024]{1,0:T(8,128)(2,1)S(1)}, bf16[32,1024]{1,0:T(8,128)(2,1)S(1)}, u32[]{:S(2)}, u32[]{:S(2)}) collective-permute-start(bf16[32,1024]{1,0:T(8,128)(2,1)S(1)} %fusion.21), channel_id=1, source_target_pairs={{0,24},{4,28},{8,16},{12,20},{16,8},{20,12},{24,0},{28,4},{1,25},{... | collective-permute-start | bytes 196616 | tf_op jit(solution)/shard_map/ppermute | solution.py:77
  115.4 4.5 %collective-permute-start.37 = (bf16[32,1024]{1,0:T(8,128)(2,1)S(1)}, bf16[32,1024]{1,0:T(8,128)(2,1)S(1)}, u32[]{:S(2)}, u32[]{:S(2)}) collective-permute-start(bf16[32,1024]{1,0:T(8,128)(2,1)S(1)} %get-tuple-element.134), channel_id=1, source_target_pairs={{0,8},{4,12},{8,0},{12,4},{16,24},{20,28},{24,16},{28,20},{1,9},{5... | collective-permute-start | bytes 196616 | tf_op jit(solution)/shard_map/ppermute | solution.py:77
  116.7 6.3 %collective-permute-start.38 = (bf16[32,1024]{1,0:T(8,128)(2,1)S(1)}, bf16[32,1024]{1,0:T(8,128)(2,1)S(1)}, u32[]{:S(2)}, u32[]{:S(2)}) collective-permute-start(bf16[32,1024]{1,0:T(8,128)(2,1)S(1)} %get-tuple-element.134), channel_id=1, source_target_pairs={{0,16},{4,20},{8,24},{12,28},{16,0},{20,4},{24,8},{28,12},{1,17},{... | collective-permute-start | bytes 196616 | tf_op jit(solution)/shard_map/ppermute | solution.py:77
  118.8 6.1 %collective-permute-start.39 = (bf16[32,1024]{1,0:T(8,128)(2,1)S(1)}, bf16[32,1024]{1,0:T(8,128)(2,1)S(1)}, u32[]{:S(2)}, u32[]{:S(2)}) collective-permute-start(bf16[32,1024]{1,0:T(8,128)(2,1)S(1)} %get-tuple-element.134), channel_id=1, source_target_pairs={{0,24},{4,28},{8,16},{12,20},{16,8},{20,12},{24,0},{28,4},{1,25},{... | collective-permute-start | bytes 196616 | tf_op jit(solution)/shard_map/ppermute | solution.py:77
  125.8 4.5 %collective-permute-start.40 = (bf16[32,1024]{1,0:T(8,128)(2,1)S(1)}, bf16[32,1024]{1,0:T(8,128)(2,1)S(1)}, u32[]{:S(2)}, u32[]{:S(2)}) collective-permute-start(bf16[32,1024]{1,0:T(8,128)(2,1)S(1)} %get-tuple-element.136), channel_id=1, source_target_pairs={{0,8},{4,12},{8,0},{12,4},{16,24},{20,28},{24,16},{28,20},{1,9},{5... | collective-permute-start | bytes 196616 | tf_op jit(solution)/shard_map/ppermute | solution.py:77
  125.9 5.2 %collective-permute-start.41 = (bf16[32,1024]{1,0:T(8,128)(2,1)S(1)}, bf16[32,1024]{1,0:T(8,128)(2,1)S(1)}, u32[]{:S(2)}, u32[]{:S(2)}) collective-permute-start(bf16[32,1024]{1,0:T(8,128)(2,1)S(1)} %get-tuple-element.136), channel_id=1, source_target_pairs={{0,16},{4,20},{8,24},{12,28},{16,0},{20,4},{24,8},{28,12},{1,17},{... | collective-permute-start | bytes 196616 | tf_op jit(solution)/shard_map/ppermute | solution.py:77
  127.6 6.1 %collective-permute-start.42 = (bf16[32,1024]{1,0:T(8,128)(2,1)S(1)}, bf16[32,1024]{1,0:T(8,128)(2,1)S(1)}, u32[]{:S(2)}, u32[]{:S(2)}) collective-permute-start(bf16[32,1024]{1,0:T(8,128)(2,1)S(1)} %get-tuple-element.136), channel_id=1, source_target_pairs={{0,24},{4,28},{8,16},{12,20},{16,8},{20,12},{24,0},{28,4},{1,25},{... | collective-permute-start | bytes 196616 | tf_op jit(solution)/shard_map/ppermute | solution.py:77
  134.7 1.3 collective-permute-start.43
  136.1 4.9 %collective-permute-start.46 = (f32[2,32,128]{2,1,0:T(8,128)S(1)}, f32[2,32,128]{2,1,0:T(8,128)S(1)}, u32[]{:S(2)}, u32[]{:S(2)}) collective-permute-start(f32[2,32,128]{2,1,0:T(8,128)S(1)} %pad_maximum_fusion.8), channel_id=1, source_target_pairs={{0,6},{1,7},{2,4},{3,5},{4,2},{5,3},{6,0},{7,1},{8,14},{9,15},{10,... | collective-permute-start | bytes 98312 | tf_op jit(solution)/shard_map/ppermute | solution.py:345
  138.2 3.9 %collective-permute-start.45 = (f32[2,32,128]{2,1,0:T(8,128)S(1)}, f32[2,32,128]{2,1,0:T(8,128)S(1)}, u32[]{:S(2)}, u32[]{:S(2)}) collective-permute-start(f32[2,32,128]{2,1,0:T(8,128)S(1)} %pad_maximum_fusion.7), channel_id=1, source_target_pairs={{0,4},{4,0},{8,12},{12,8},{16,20},{20,16},{24,28},{28,24},{1,5},{5... | collective-permute-start | bytes 98312 | tf_op jit(solution)/shard_map/ppermute | solution.py:77
  139.7 3.9 %collective-permute-start.44 = (f32[2,32,128]{2,1,0:T(8,128)S(1)}, f32[2,32,128]{2,1,0:T(8,128)S(1)}, u32[]{:S(2)}, u32[]{:S(2)}) collective-permute-start(f32[2,32,128]{2,1,0:T(8,128)S(1)} %pad_maximum_fusion.6), channel_id=1, source_target_pairs={{0,2},{1,3},{2,0},{3,1},{4,6},{5,7},{6,4},{7,5},{8,10},{9,11},{10,... | collective-permute-start | bytes 98312 | tf_op jit(solution)/shard_map/ppermute | solution.py:77
  (6 other events, 7.7 us)

commit v4 on v3

--- a/solution.py
+++ b/solution.py
@@ -290,6 +290,88 @@
     )(*blocks)
 
 
+def lead_kernel(mask, own, *rest):
+    got, word, whole, count, front, words = rest[:-5], rest[-5], rest[-4], rest[-3], rest[-2], rest[-1]
+    total = own[...]
+    for message in got:
+        total = total + decoded(message[...])
+    total = jnp.where(mask(word[...]), total, 0.0)
+    count[...] = total
+    front[...] = total.astype(jnp.bfloat16)
+    words[...] = coded(across_terms(front[...], whole[...]))
+
+
+def across_terms(front, whole):
+    return lax.dot_general(
+        front, whole, (((1,), (1,)), ((), ())), preferred_element_type=jnp.float32
+    )
+
+
+def message_kernel(front, whole, words):
+    words[...] = coded(across_terms(front[...], whole[...]))
+
+
+def vmem_call(kernel, outs, args, flops):
+    moved = sum(x.size * x.dtype.itemsize for x in (*outs, *args))
+    return pl.pallas_call(
+        kernel,
+        out_shape=outs,
+        in_specs=[IN_VMEM] * len(args),
+        out_specs=[IN_VMEM] * len(outs),
+        compiler_params=pltpu.CompilerParams(vmem_limit_bytes=8 * 1024 * 1024),
+        cost_estimate=pl.CostEstimate(flops=flops, bytes_accessed=moved, transcendentals=0),
+    )(*args)
+
+
+def level_terms(mask, own, got, word, whole):
+    share, span = own.shape
+    outs = [
+        jax.ShapeDtypeStruct((share, span), jnp.float32),
+        jax.ShapeDtypeStruct((share, span), jnp.bfloat16),
+        jax.ShapeDtypeStruct((share, span // 4 * 3), jnp.int32),
+    ]
+    flops = 2 * share * whole.size
+    return vmem_call(functools.partial(lead_kernel, mask), outs, [own, *got, word, whole], flops)
+
+
+def message(front, whole):
+    share, span = front.shape
+    outs = [jax.ShapeDtypeStruct((share, span // 4 * 3), jnp.int32)]
+    return vmem_call(message_kernel, outs, [front, whole], 2 * share * whole.size)[0]
+
+
+def back_kernel(mask, last, part, weight, whole, *rest):
+    out = rest[-1]
+    back = part[...] + jnp.dot(weight[...], whole[...], preferred_element_type=jnp.float32)
+    if last:
+        found, word = rest[0], rest[1]
+        out[...] = found[...] + jnp.where(mask(word[...]), back, 0.0)
+        return
+    count, found, word, grown = rest[0], rest[1], rest[2], rest[3]
+    delta = count[...] * back
+    grown[...] = found[...] + delta
+    new = jnp.where(mask(word[...]), (1.0 + delta) / jnp.maximum(count[...], 1.0), 0.0)
+    out[...] = new.astype(jnp.bfloat16)
+
+
+def back_terms(mask, part, weight, whole, count, found, word):
+    last = count is None
+    outs = [jax.ShapeDtypeStruct(found.shape, jnp.float32)]
+    if not last:
+        outs.append(jax.ShapeDtypeStruct(found.shape, jnp.bfloat16))
+    args = [part, weight, whole] + ([] if last else [count]) + [found, word]
+    flops = 2 * found.shape[0] * whole.size
+    return vmem_call(functools.partial(back_kernel, mask, last), outs, args, flops)
+
+
+MASKS = (
+    lambda word: word < 0.0,
+    lambda word: word == 0.5,
+    lambda word: word == 0.25,
+    lambda word: word >= 1.0,
+)
+
+
 def spread_kernel(found, keep, send):
     place = lax.axis_index("row") % 2 * lax.axis_size("col") + lax.axis_index("col")
     vert = keep.shape[-1]
@@ -364,8 +446,6 @@
     upper, lower = lax.optimization_barrier((upper, lower))
 
     word, front = placed_inputs(pieces)
-    masks = [word < 0.0, word == 0.5, word == 0.25, word >= 1.0]
-
     cross = [swap(by_y[0], "col", 2), swap(by_x[0], "row", 1)]
     same_y = swap(flipped, "row", 1)
     same_x = swap(same, "col", 2)
@@ -384,40 +464,33 @@
     ]
     whole = assembled(blocks, 1) + assembled(near + far + last, 2)
 
-    def forward(front, k):
-        dims = (((1,), (1,)), ((), ()))
-        return lax.dot_general(
-            front.astype(jnp.bfloat16), whole[k], dims, preferred_element_type=jnp.float32
-        )
-
     def across(value):
-        return {k: swap(value(k), "row", 2 * k) for k in reversed(range(1, LAYERS))}
-
-    counts = [None]
-    for distance in (1, 2, 3):
-        def terms(k):
-            return forward(counts[-1], k) if distance > 1 else first[k - 1]
-
-        got = across(lambda k: coded(terms(k)))
-        total = forward(front if distance == 1 else counts[-1], 0)
-        for k in range(1, LAYERS):
-            total = total + decoded(got[k])
-        counts.append(jnp.where(masks[distance], total, 0.0))
-    weight = (jnp.where(masks[3], word, 0.0) / jnp.maximum(counts[3], 1.0)).astype(jnp.bfloat16)
+        got = {}
+        for k in reversed(range(1, LAYERS)):
+            got[k] = swap(value(k), "row", 2 * k)
+        return got
+
+    got = across(lambda k: coded(first[k - 1]))
+    counts = []
+    for distance in (1, 2):
+        own = across_terms(front, whole[0])
+        got = [got[k] for k in range(1, LAYERS)]
+        count, front, words = level_terms(MASKS[distance], own, got, word, whole[-1])
+        counts.append(count)
+        got = across(lambda k: words if k == LAYERS - 1 else message(front, whole[k]))
+    total = across_terms(front, whole[0])
+    for k in range(1, LAYERS):
+        total = total + decoded(got[k])
+    weight = jnp.where(MASKS[3](word), word / jnp.maximum(total, 1.0), 0.0).astype(jnp.bfloat16)
     found = jnp.zeros_like(word)
     for distance in (2, 1, 0):
-        got = {0: weight} | across(lambda k: weight)
-        back = sum(
-            jnp.dot(got[k], whole[k], preferred_element_type=jnp.float32) for k in range(LAYERS)
-        )
-        if distance > 0:
-            delta = counts[distance] * back
-            found = found + delta
-            weight = jnp.where(
-                masks[distance], (1.0 + delta) / jnp.maximum(counts[distance], 1.0), 0.0
-            ).astype(jnp.bfloat16)
-        else:
-            found = found + jnp.where(masks[0], back, 0.0)
+        got = across(lambda k: weight)
+        part = jnp.dot(weight, whole[0], preferred_element_type=jnp.float32)
+        for k in (1, 2):
+            part = part + jnp.dot(got[k], whole[k], preferred_element_type=jnp.float32)
+        count = counts[distance - 1] if distance else None
+        found, *weight = back_terms(MASKS[distance], part, got[3], whole[3], count, found, word)
+        weight = weight[0] if weight else None
 
     keep, send = spread_found(found)
     pieces = traded(keep, send)

time: 145 us -> 142 us (0.979)
  matrix products: 14.1 us -> 6.81 us
  Pallas kernels: 5.9 us -> 12.8 us
  waiting for transfers between devices: 69.6 us -> 67.1 us
    dot_general x21 -> x12, matrix products: 14.1 us -> 6.81 us  [the longest x6 2.81 us: split_shards(): part = part + jnp.dot(got[k], whole[k], preferred_element_type=jnp.float32)]
    pallas_call x0 -> x9, Pallas kernels: none -> 6.86 us  [vmem_call(): pl.pallas_call(kernel, out_shape=outs, in_specs=[IN_VMEM] * len(args), ou...]
    ppermute x44, waiting for transfers between devices: 57.6 us -> 55.9 us  [swap(): return lax.ppermute(value, axis, partner(axis, bit))]
    ppermute x2, starting transfers between devices: 3.59 us -> 5.04 us  [traded(): from_d = lax.ppermute(held[3], ('row', 'col'), diagonal())]
  transfers between devices with their start and end apart: 47 -> 47, of which waited for: 25 -> 24; matrix products, arithmetic and copies ran while one was open for 4% -> 4% of each run, Pallas kernels for 3% -> 4%
where the time goes in v4:
time: 142 us
  waiting for transfers between devices  67.1 us (47%)
  starting transfers between devices  49.4 us (35%)
  Pallas kernels  12.8 us (9%)
  matrix products  6.81 us (5%)
  local copies, waits for them, and re-layouts  5.04 us (4%)
    ppermute x44, waiting for transfers between devices, swap(): return lax.ppermute(value, axis, partner(axis, bit))  55.9 us
    ppermute x44, starting transfers between devices, swap(): return lax.ppermute(value, axis, partner(axis, bit))  41.4 us
    ppermute x1, waiting for transfers between devices, split_shards(): same_d = lax.ppermute(flipped, ('row', 'col'), diagonal())  10.8 us
    pallas_call x9, Pallas kernels, vmem_call(): pl.pallas_call(kernel, out_shape=outs, in_specs=[IN_VMEM] * len(args), ou...  6.86 us
    ppermute x2, starting transfers between devices, traded(): from_d = lax.ppermute(held[3], ('row', 'col'), diagonal())  5.04 us
    unnamed x14, local copies, waits for them, and re-layouts  5 us
    ppermute x1, starting transfers between devices, split_shards(): same_d = lax.ppermute(flipped, ('row', 'col'), diagonal())  2.98 us
  transfers between devices with their start and end apart: 47, of which 24 were waited for; matrix products, arithmetic and copies ran while one was open for 4% of the time, Pallas kernels for 4%

profile of v4, /device:TPU:0, one launch (start us, length us, event | category | flops | bytes accessed | tf_op | source)
XLA Modules:
  0.0 142.2 jit_solution(15049521928036009637)
XLA Ops:
  0.0 0.9 copy-done.1
  0.9 0.9 copy-done.3
  1.8 0.9 copy-done.5
  3.4 1.6 %copy-done = s32[1,1,8,4,128,128]{5,4,3,2,1,0:T(8,128)S(1)} copy-done((s32[1,1,8,4,128,128]{5,4,3,2,1,0:T(8,128)S(1)}, s32[1,1,8,4,128,128]{5,4,3,2,1,0:T(8,128)}, u32[]{:S(2)}) %copy-start) | copy-done | bytes 2097176
  6.4 2.6 %collective-permute-start.5 = (bf16[2,4,128,128]{3,2,1,0:T(8,128)(2,1)S(1)}, bf16[2,4,128,128]{3,2,1,0:T(8,128)(2,1)S(1)}, u32[]{:S(2)}, u32[]{:S(2)}) collective-permute-start(bf16[2,4,128,128]{3,2,1,0:T(8,128)(2,1)S(1)} %get-tuple-element.42.rest_0_), channel_id=1, source_target_pairs={{0,2},{1,3},{2,0},{3,1},{4,6},{5,7},{6,4},{7,5},{8,10},{9,11},{10,... | collective-permute-start | bytes 786440 | tf_op jit(solution)/shard_map/ppermute | solution.py:77
  9.1 2.0 %collective-permute-start.2 = (f32[2,32,128]{2,1,0:T(8,128)S(1)}, f32[2,32,128]{2,1,0:T(8,128)S(1)}, u32[]{:S(2)}, u32[]{:S(2)}) collective-permute-start(f32[2,32,128]{2,1,0:T(8,128)S(1)} %pad_maximum_fusion.3), channel_id=1, source_target_pairs={{0,4},{4,0},{8,12},{12,8},{16,20},{20,16},{24,28},{28,24},{1,5},{5... | collective-permute-start | bytes 98312 | tf_op jit(solution)/shard_map/ppermute | solution.py:77
  11.1 1.4 %collective-permute-start.3 = (f32[2,32,128]{2,1,0:T(8,128)S(1)}, f32[2,32,128]{2,1,0:T(8,128)S(1)}, u32[]{:S(2)}, u32[]{:S(2)}) collective-permute-start(f32[2,32,128]{2,1,0:T(8,128)S(1)} %pad_maximum_fusion.4), channel_id=1, source_target_pairs={{0,6},{1,7},{2,4},{3,5},{4,2},{5,3},{6,0},{7,1},{8,14},{9,15},{10,... | collective-permute-start | bytes 98312 | tf_op jit(solution)/shard_map/ppermute | solution.py:427
  12.7 4.2 %collective-permute-done.1.rest_1_ = f32[2,32,128]{2,1,0:T(8,128)S(1)} collective-permute-done((f32[2,32,128]{2,1,0:T(8,128)S(1)}, f32[2,32,128]{2,1,0:T(8,128)S(1)}, u32[]{:S(2)}, u32[]{:S(2)}) %collective-permute-start.1) | collective-permute-done | bytes 32800 | tf_op jit(solution)/shard_map/ppermute | solution.py:77
  16.8 3.0 %collective-permute-start.9 = (bf16[2,4,128,128]{3,2,1,0:T(8,128)(2,1)S(1)}, bf16[2,4,128,128]{3,2,1,0:T(8,128)(2,1)S(1)}, u32[]{:S(2)}, u32[]{:S(2)}) collective-permute-start(bf16[2,4,128,128]{3,2,1,0:T(8,128)(2,1)S(1)} %get-tuple-element.43), channel_id=1, source_target_pairs={{0,6},{1,7},{2,4},{3,5},{4,2},{5,3},{6,0},{7,1},{8,14},{9,15},{10,... | collective-permute-start | bytes 786440 | tf_op jit(solution)/shard_map/ppermute | solution.py:452
  20.3 1.6 %collective-permute-start.17 = (bf16[3,4,128,128]{3,2,1,0:T(8,128)(2,1)S(1)}, bf16[3,4,128,128]{3,2,1,0:T(8,128)(2,1)S(1)}, u32[]{:S(2)}, u32[]{:S(2)}) collective-permute-start(bf16[3,4,128,128]{3,2,1,0:T(8,128)(2,1)S(1)} %get-tuple-element.45.rest_1_), channel_id=1, source_target_pairs={{0,4},{4,0},{8,12},{12,8},{16,20},{20,16},{24,28},{28,24},{1,5},{5... | collective-permute-start | bytes 1179656 | tf_op jit(solution)/shard_map/ppermute | solution.py:77
  21.9 10.8 %collective-permute-done.9.rest_6_ = bf16[2,4,128,128]{3,2,1,0:T(8,128)(2,1)S(1)} collective-permute-done((bf16[2,4,128,128]{3,2,1,0:T(8,128)(2,1)S(1)}, bf16[2,4,128,128]{3,2,1,0:T(8,128)(2,1)S(1)}, u32[]{:S(2)}, u32[]{:S(2)}) %collective-permute-start.9) | collective-permute-done | bytes 262176 | tf_op jit(solution)/shard_map/ppermute | solution.py:452
  32.7 1.5 %collective-permute-start.14 = (bf16[3,4,128,128]{3,2,1,0:T(8,128)(2,1)S(1)}, bf16[3,4,128,128]{3,2,1,0:T(8,128)(2,1)S(1)}, u32[]{:S(2)}, u32[]{:S(2)}) collective-permute-start(bf16[3,4,128,128]{3,2,1,0:T(8,128)(2,1)S(1)} %get-tuple-element.45.rest_1_), channel_id=1, source_target_pairs={{0,2},{1,3},{2,0},{3,1},{4,6},{5,7},{6,4},{7,5},{8,10},{9,11},{10,... | collective-permute-start | bytes 1179656 | tf_op jit(solution)/shard_map/ppermute | solution.py:77
  35.6 7.4 %collective-permute-done.17.rest_8_ = bf16[3,4,128,128]{3,2,1,0:T(8,128)(2,1)S(1)} collective-permute-done((bf16[3,4,128,128]{3,2,1,0:T(8,128)(2,1)S(1)}, bf16[3,4,128,128]{3,2,1,0:T(8,128)(2,1)S(1)}, u32[]{:S(2)}, u32[]{:S(2)}) %collective-permute-start.17) | collective-permute-done | bytes 393248 | tf_op jit(solution)/shard_map/ppermute | solution.py:77
  43.5 5.8 %collective-permute-done.18.rest_9_ = bf16[3,4,128,128]{3,2,1,0:T(8,128)(2,1)S(1)} collective-permute-done((bf16[3,4,128,128]{3,2,1,0:T(8,128)(2,1)S(1)}, bf16[3,4,128,128]{3,2,1,0:T(8,128)(2,1)S(1)}, u32[]{:S(2)}, u32[]{:S(2)}) %collective-permute-start.18) | collective-permute-done | bytes 393248 | tf_op jit(solution)/shard_map/ppermute | solution.py:77
  51.0 1.0 collective-permute-done.10.rest_7_
  52.9 5.5 %collective-permute-done.21.rest_3_.rest_12_ = bf16[3,4,128,128]{3,2,1,0:T(8,128)(2,1)S(1)} collective-permute-done((bf16[3,4,128,128]{3,2,1,0:T(8,128)(2,1)S(1)}, bf16[3,4,128,128]{3,2,1,0:T(8,128)(2,1)S(1)}, u32[]{:S(2)}, u32[]{:S(2)}) %collective-permute-start.21) | collective-permute-done | bytes 393248 | tf_op jit(solution)/shard_map/ppermute | solution.py:77
  59.6 1.5 %first.2 = (f32[32,1024]{1,0:T(8,128)S(1)}, f32[32,1024]{1,0:T(8,128)S(1)}, f32[32,1024]{1,0:T(8,128)S(1)}) custom-call(bf16[32,1024]{1,0:T(8,128)(2,1)S(1)} %get-tuple-element.41.front, bf16[3,4,128,128]{3,2,1,0:T(8,128)(2,1)S(1)} %get-tuple-element.44.rest_0_, bf16[3,4,128,128]{3,2,1,0:T(8,128)(2,1)S(1)} %get-tuple-element.45.rest_1_, ...), custom_call_target="tpu_custom_call" | custom-call | flops 150994944 | bytes 4718592 | tf_op jit(solution)/shard_map/first/pallas_call | solution.py:249
  61.9 3.7 %collective-permute-start.27 = (s32[32,768]{1,0:T(8,128)S(1)}, s32[32,768]{1,0:T(8,128)S(1)}, u32[]{:S(2)}, u32[]{:S(2)}) collective-permute-start(s32[32,768]{1,0:T(8,128)S(1)} %pad_add_fusion.5), channel_id=1, source_target_pairs={{0,24},{4,28},{8,16},{12,20},{16,8},{20,12},{24,0},{28,4},{1,25},{... | collective-permute-start | bytes 294920 | tf_op jit(solution)/shard_map/ppermute | solution.py:77
  66.0 0.8 collective-permute-start.25
  67.6 1.7 %assemble.3 = (bf16[1024,1024]{1,0:T(8,128)(2,1)S(1)}, bf16[1024,1024]{1,0:T(8,128)(2,1)S(1)}, bf16[1024,1024]{1,0:T(8,128)(2,1)S(1)}) custom-call(bf16[3,4,128,128]{3,2,1,0:T(8,128)(2,1)S(1)} %get-tuple-element.44.rest_0_, bf16[3,4,128,128]{3,2,1,0:T(8,128)(2,1)S(1)} %get-tuple-element.45.rest_1_, ...), custom_call_target="tpu_custom_call" | custom-call | bytes 12582912 | tf_op jit(solution)/shard_map/assemble/pallas_call | solution.py:280
  69.3 5.0 %collective-permute-done.26.rest_1_ = s32[32,768]{1,0:T(8,128)S(1)} collective-permute-done((s32[32,768]{1,0:T(8,128)S(1)}, s32[32,768]{1,0:T(8,128)S(1)}, u32[]{:S(2)}, u32[]{:S(2)}) %collective-permute-start.26) | collective-permute-done | bytes 98336 | tf_op jit(solution)/shard_map/ppermute | solution.py:77
  74.2 1.0 shard_map.55
  75.3 0.8 shard_map.57
  77.1 3.0 %collective-permute-start.28 = (s32[32,768]{1,0:T(8,128)S(1)}, s32[32,768]{1,0:T(8,128)S(1)}, u32[]{:S(2)}, u32[]{:S(2)}) collective-permute-start(s32[32,768]{1,0:T(8,128)S(1)} %shard_map.56), channel_id=1, source_target_pairs={{0,8},{4,12},{8,0},{12,4},{16,24},{20,28},{24,16},{28,20},{1,9},{5... | collective-permute-start | bytes 294920 | tf_op jit(solution)/shard_map/ppermute | solution.py:77
  80.1 1.3 collective-permute-start.30
  82.2 1.9 %collective-permute-done.29.rest_1_ = s32[32,768]{1,0:T(8,128)S(1)} collective-permute-done((s32[32,768]{1,0:T(8,128)S(1)}, s32[32,768]{1,0:T(8,128)S(1)}, u32[]{:S(2)}, u32[]{:S(2)}) %collective-permute-start.29) | collective-permute-done | bytes 98336 | tf_op jit(solution)/shard_map/ppermute | solution.py:77
  84.1 1.3 collective-permute-done.28.rest_0_
  85.3 1.2 collective-permute-done.30.rest_2_
  86.5 1.0 shard_map.58
  88.4 1.6 %collective-permute-start.31 = (s32[32,768]{1,0:T(8,128)S(1)}, s32[32,768]{1,0:T(8,128)S(1)}, u32[]{:S(2)}, u32[]{:S(2)}) collective-permute-start(s32[32,768]{1,0:T(8,128)S(1)} %shard_map.59), channel_id=1, source_target_pairs={{0,8},{4,12},{8,0},{12,4},{16,24},{20,28},{24,16},{28,20},{1,9},{5... | collective-permute-start | bytes 294920 | tf_op jit(solution)/shard_map/ppermute | solution.py:77
  91.4 2.3 %collective-permute-start.33 = (s32[32,768]{1,0:T(8,128)S(1)}, s32[32,768]{1,0:T(8,128)S(1)}, u32[]{:S(2)}, u32[]{:S(2)}) collective-permute-start(s32[32,768]{1,0:T(8,128)S(1)} %get-tuple-element.58), channel_id=1, source_target_pairs={{0,24},{4,28},{8,16},{12,20},{16,8},{20,12},{24,0},{28,4},{1,25},{... | collective-permute-start | bytes 294920 | tf_op jit(solution)/shard_map/ppermute | solution.py:77
  93.8 6.7 %collective-permute-done.32 = s32[32,768]{1,0:T(8,128)S(1)} collective-permute-done((s32[32,768]{1,0:T(8,128)S(1)}, s32[32,768]{1,0:T(8,128)S(1)}, u32[]{:S(2)}, u32[]{:S(2)}) %collective-permute-start.32) | collective-permute-done | bytes 98336 | tf_op jit(solution)/shard_map/ppermute | solution.py:77
  100.6 1.1 fusion.8
  101.7 2.0 %collective-permute-start.34 = (bf16[32,1024]{1,0:T(8,128)(2,1)S(1)}, bf16[32,1024]{1,0:T(8,128)(2,1)S(1)}, u32[]{:S(2)}, u32[]{:S(2)}) collective-permute-start(bf16[32,1024]{1,0:T(8,128)(2,1)S(1)} %fusion.8), channel_id=1, source_target_pairs={{0,8},{4,12},{8,0},{12,4},{16,24},{20,28},{24,16},{28,20},{1,9},{5... | collective-permute-start | bytes 196616 | tf_op jit(solution)/shard_map/ppermute | solution.py:77
  104.1 2.2 %collective-permute-start.36 = (bf16[32,1024]{1,0:T(8,128)(2,1)S(1)}, bf16[32,1024]{1,0:T(8,128)(2,1)S(1)}, u32[]{:S(2)}, u32[]{:S(2)}) collective-permute-start(bf16[32,1024]{1,0:T(8,128)(2,1)S(1)} %fusion.8), channel_id=1, source_target_pairs={{0,24},{4,28},{8,16},{12,20},{16,8},{20,12},{24,0},{28,4},{1,25},{... | collective-permute-start | bytes 196616 | tf_op jit(solution)/shard_map/ppermute | solution.py:77
  106.7 4.4 %collective-permute-done.35 = bf16[32,1024]{1,0:T(8,128)(2,1)S(1)} collective-permute-done((bf16[32,1024]{1,0:T(8,128)(2,1)S(1)}, bf16[32,1024]{1,0:T(8,128)(2,1)S(1)}, u32[]{:S(2)}, u32[]{:S(2)}) %collective-permute-start.35) | collective-permute-done | bytes 65568 | tf_op jit(solution)/shard_map/ppermute | solution.py:77
  113.0 2.0 %collective-permute-start.38 = (bf16[32,1024]{1,0:T(8,128)(2,1)S(1)}, bf16[32,1024]{1,0:T(8,128)(2,1)S(1)}, u32[]{:S(2)}, u32[]{:S(2)}) collective-permute-start(bf16[32,1024]{1,0:T(8,128)(2,1)S(1)} %get-tuple-element.60), channel_id=1, source_target_pairs={{0,16},{4,20},{8,24},{12,28},{16,0},{20,4},{24,8},{28,12},{1,17},{... | collective-permute-start | bytes 196616 | tf_op jit(solution)/shard_map/ppermute | solution.py:77
  115.0 2.2 %collective-permute-start.39 = (bf16[32,1024]{1,0:T(8,128)(2,1)S(1)}, bf16[32,1024]{1,0:T(8,128)(2,1)S(1)}, u32[]{:S(2)}, u32[]{:S(2)}) collective-permute-start(bf16[32,1024]{1,0:T(8,128)(2,1)S(1)} %get-tuple-element.60), channel_id=1, source_target_pairs={{0,24},{4,28},{8,16},{12,20},{16,8},{20,12},{24,0},{28,4},{1,25},{... | collective-permute-start | bytes 196616 | tf_op jit(solution)/shard_map/ppermute | solution.py:77
  117.2 1.1 collective-permute-done.37
  119.7 1.4 collective-permute-done.39.weight
  121.7 2.8 %collective-permute-start.41 = (bf16[32,1024]{1,0:T(8,128)(2,1)S(1)}, bf16[32,1024]{1,0:T(8,128)(2,1)S(1)}, u32[]{:S(2)}, u32[]{:S(2)}) collective-permute-start(bf16[32,1024]{1,0:T(8,128)(2,1)S(1)} %get-tuple-element.63), channel_id=1, source_target_pairs={{0,16},{4,20},{8,24},{12,28},{16,0},{20,4},{24,8},{28,12},{1,17},{... | collective-permute-start | bytes 196616 | tf_op jit(solution)/shard_map/ppermute | solution.py:77
  124.5 1.6 %collective-permute-start.42 = (bf16[32,1024]{1,0:T(8,128)(2,1)S(1)}, bf16[32,1024]{1,0:T(8,128)(2,1)S(1)}, u32[]{:S(2)}, u32[]{:S(2)}) collective-permute-start(bf16[32,1024]{1,0:T(8,128)(2,1)S(1)} %get-tuple-element.63), channel_id=1, source_target_pairs={{0,24},{4,28},{8,16},{12,20},{16,8},{20,12},{24,0},{28,4},{1,25},{... | collective-permute-start | bytes 196616 | tf_op jit(solution)/shard_map/ppermute | solution.py:77
  127.9 2.7 %collective-permute-done.42.weight = bf16[32,1024]{1,0:T(8,128)(2,1)S(1)} collective-permute-done((bf16[32,1024]{1,0:T(8,128)(2,1)S(1)}, bf16[32,1024]{1,0:T(8,128)(2,1)S(1)}, u32[]{:S(2)}, u32[]{:S(2)}) %collective-permute-start.42) | collective-permute-done | bytes 65568 | tf_op jit(solution)/shard_map/ppermute | solution.py:77
  131.2 1.2 collective-permute-done.43
  132.4 3.6 %collective-permute-start.46 = (f32[2,32,128]{2,1,0:T(8,128)S(1)}, f32[2,32,128]{2,1,0:T(8,128)S(1)}, u32[]{:S(2)}, u32[]{:S(2)}) collective-permute-start(f32[2,32,128]{2,1,0:T(8,128)S(1)} %pad_maximum_fusion.8), channel_id=1, source_target_pairs={{0,6},{1,7},{2,4},{3,5},{4,2},{5,3},{6,0},{7,1},{8,14},{9,15},{10,... | collective-permute-start | bytes 98312 | tf_op jit(solution)/shard_map/ppermute | solution.py:427
  136.0 1.5 %collective-permute-start.45 = (f32[2,32,128]{2,1,0:T(8,128)S(1)}, f32[2,32,128]{2,1,0:T(8,128)S(1)}, u32[]{:S(2)}, u32[]{:S(2)}) collective-permute-start(f32[2,32,128]{2,1,0:T(8,128)S(1)} %pad_maximum_fusion.7), channel_id=1, source_target_pairs={{0,4},{4,0},{8,12},{12,8},{16,20},{20,16},{24,28},{28,24},{1,5},{5... | collective-permute-start | bytes 98312 | tf_op jit(solution)/shard_map/ppermute | solution.py:77
  137.9 2.0 %collective-permute-done.45.rest_2_ = f32[2,32,128]{2,1,0:T(8,128)S(1)} collective-permute-done((f32[2,32,128]{2,1,0:T(8,128)S(1)}, f32[2,32,128]{2,1,0:T(8,128)S(1)}, u32[]{:S(2)}, u32[]{:S(2)}) %collective-permute-start.45) | collective-permute-done | bytes 32800 | tf_op jit(solution)/shard_map/ppermute | solution.py:77
  139.9 1.5 %collective-permute-done.44.rest_1_ = f32[2,32,128]{2,1,0:T(8,128)S(1)} collective-permute-done((f32[2,32,128]{2,1,0:T(8,128)S(1)}, f32[2,32,128]{2,1,0:T(8,128)S(1)}, u32[]{:S(2)}, u32[]{:S(2)}) %collective-permute-start.44) | collective-permute-done | bytes 32800 | tf_op jit(solution)/shard_map/ppermute | solution.py:77
  (117 shorter events, 22.5 us)
Async XLA Ops:
  2.8 6.1 %collective-permute-start = (f32[4,32,128]{2,1,0:T(8,128)S(1)}, f32[4,32,128]{2,1,0:T(8,128)S(1)}, u32[]{:S(2)}, u32[]{:S(2)}) collective-permute-start(f32[4,32,128]{2,1,0:T(8,128)S(1)} %get-tuple-element.39), channel_id=1, source_target_pairs={{0,1},{1,0},{2,3},{3,2},{4,5},{5,4},{6,7},{7,6},{8,9},{9,8},{10,11... | collective-permute-start | bytes 196616 | tf_op jit(solution)/shard_map/ppermute | solution.py:77
  6.4 13.9 %collective-permute-start.5 = (bf16[2,4,128,128]{3,2,1,0:T(8,128)(2,1)S(1)}, bf16[2,4,128,128]{3,2,1,0:T(8,128)(2,1)S(1)}, u32[]{:S(2)}, u32[]{:S(2)}) collective-permute-start(bf16[2,4,128,128]{3,2,1,0:T(8,128)(2,1)S(1)} %get-tuple-element.42.rest_0_), channel_id=1, source_target_pairs={{0,2},{1,3},{2,0},{3,1},{4,6},{5,7},{6,4},{7,5},{8,10},{9,11},{10,... | collective-permute-start | bytes 786440 | tf_op jit(solution)/shard_map/ppermute | solution.py:77
  9.0 7.8 %collective-permute-start.1 = (f32[2,32,128]{2,1,0:T(8,128)S(1)}, f32[2,32,128]{2,1,0:T(8,128)S(1)}, u32[]{:S(2)}, u32[]{:S(2)}) collective-permute-start(f32[2,32,128]{2,1,0:T(8,128)S(1)} %pad_maximum_fusion.2), channel_id=1, source_target_pairs={{0,2},{1,3},{2,0},{3,1},{4,6},{5,7},{6,4},{7,5},{8,10},{9,11},{10,... | collective-permute-start | bytes 98312 | tf_op jit(solution)/shard_map/ppermute | solution.py:77
  9.1 10.7 %collective-permute-start.2 = (f32[2,32,128]{2,1,0:T(8,128)S(1)}, f32[2,32,128]{2,1,0:T(8,128)S(1)}, u32[]{:S(2)}, u32[]{:S(2)}) collective-permute-start(f32[2,32,128]{2,1,0:T(8,128)S(1)} %pad_maximum_fusion.3), channel_id=1, source_target_pairs={{0,4},{4,0},{8,12},{12,8},{16,20},{20,16},{24,28},{28,24},{1,5},{5... | collective-permute-start | bytes 98312 | tf_op jit(solution)/shard_map/ppermute | solution.py:77
  11.1 9.2 %collective-permute-start.3 = (f32[2,32,128]{2,1,0:T(8,128)S(1)}, f32[2,32,128]{2,1,0:T(8,128)S(1)}, u32[]{:S(2)}, u32[]{:S(2)}) collective-permute-start(f32[2,32,128]{2,1,0:T(8,128)S(1)} %pad_maximum_fusion.4), channel_id=1, source_target_pairs={{0,6},{1,7},{2,4},{3,5},{4,2},{5,3},{6,0},{7,1},{8,14},{9,15},{10,... | collective-permute-start | bytes 98312 | tf_op jit(solution)/shard_map/ppermute | solution.py:427
  12.6 22.5 %collective-permute-start.13 = (bf16[3,4,128,128]{3,2,1,0:T(8,128)(2,1)S(1)}, bf16[3,4,128,128]{3,2,1,0:T(8,128)(2,1)S(1)}, u32[]{:S(2)}, u32[]{:S(2)}) collective-permute-start(bf16[3,4,128,128]{3,2,1,0:T(8,128)(2,1)S(1)} %get-tuple-element.44.rest_0_), channel_id=1, source_target_pairs={{0,2},{1,3},{2,0},{3,1},{4,6},{5,7},{6,4},{7,5},{8,10},{9,11},{10,... | collective-permute-start | bytes 1179656 | tf_op jit(solution)/shard_map/ppermute | solution.py:77
  16.8 15.9 %collective-permute-start.9 = (bf16[2,4,128,128]{3,2,1,0:T(8,128)(2,1)S(1)}, bf16[2,4,128,128]{3,2,1,0:T(8,128)(2,1)S(1)}, u32[]{:S(2)}, u32[]{:S(2)}) collective-permute-start(bf16[2,4,128,128]{3,2,1,0:T(8,128)(2,1)S(1)} %get-tuple-element.43), channel_id=1, source_target_pairs={{0,6},{1,7},{2,4},{3,5},{4,2},{5,3},{6,0},{7,1},{8,14},{9,15},{10,... | collective-permute-start | bytes 786440 | tf_op jit(solution)/shard_map/ppermute | solution.py:452
  19.8 14.8 %collective-permute-start.7 = (bf16[2,4,128,128]{3,2,1,0:T(8,128)(2,1)S(1)}, bf16[2,4,128,128]{3,2,1,0:T(8,128)(2,1)S(1)}, u32[]{:S(2)}, u32[]{:S(2)}) collective-permute-start(bf16[2,4,128,128]{3,2,1,0:T(8,128)(2,1)S(1)} %get-tuple-element.43), channel_id=1, source_target_pairs={{0,4},{4,0},{8,12},{12,8},{16,20},{20,16},{24,28},{28,24},{1,5},{5... | collective-permute-start | bytes 786440 | tf_op jit(solution)/shard_map/ppermute | solution.py:77
  20.3 14.8 %collective-permute-start.4 = (bf16[2,4,128,128]{3,2,1,0:T(8,128)(2,1)S(1)}, bf16[2,4,128,128]{3,2,1,0:T(8,128)(2,1)S(1)}, u32[]{:S(2)}, u32[]{:S(2)}) collective-permute-start(bf16[2,4,128,128]{3,2,1,0:T(8,128)(2,1)S(1)} %get-tuple-element.42.rest_0_), channel_id=1, source_target_pairs={{0,1},{1,0},{2,3},{3,2},{4,5},{5,4},{6,7},{7,6},{8,9},{9,8},{10,11... | collective-permute-start | bytes 786440 | tf_op jit(solution)/shard_map/ppermute | solution.py:77
  20.3 22.7 %collective-permute-start.17 = (bf16[3,4,128,128]{3,2,1,0:T(8,128)(2,1)S(1)}, bf16[3,4,128,128]{3,2,1,0:T(8,128)(2,1)S(1)}, u32[]{:S(2)}, u32[]{:S(2)}) collective-permute-start(bf16[3,4,128,128]{3,2,1,0:T(8,128)(2,1)S(1)} %get-tuple-element.45.rest_1_), channel_id=1, source_target_pairs={{0,4},{4,0},{8,12},{12,8},{16,20},{20,16},{24,28},{28,24},{1,5},{5... | collective-permute-start | bytes 1179656 | tf_op jit(solution)/shard_map/ppermute | solution.py:77
  32.7 10.6 %collective-permute-start.14 = (bf16[3,4,128,128]{3,2,1,0:T(8,128)(2,1)S(1)}, bf16[3,4,128,128]{3,2,1,0:T(8,128)(2,1)S(1)}, u32[]{:S(2)}, u32[]{:S(2)}) collective-permute-start(bf16[3,4,128,128]{3,2,1,0:T(8,128)(2,1)S(1)} %get-tuple-element.45.rest_1_), channel_id=1, source_target_pairs={{0,2},{1,3},{2,0},{3,1},{4,6},{5,7},{6,4},{7,5},{8,10},{9,11},{10,... | collective-permute-start | bytes 1179656 | tf_op jit(solution)/shard_map/ppermute | solution.py:77
  34.6 14.8 %collective-permute-start.18 = (bf16[3,4,128,128]{3,2,1,0:T(8,128)(2,1)S(1)}, bf16[3,4,128,128]{3,2,1,0:T(8,128)(2,1)S(1)}, u32[]{:S(2)}, u32[]{:S(2)}) collective-permute-start(bf16[3,4,128,128]{3,2,1,0:T(8,128)(2,1)S(1)} %get-tuple-element.44.rest_0_), channel_id=1, source_target_pairs={{0,4},{4,0},{8,12},{12,8},{16,20},{20,16},{24,28},{28,24},{1,5},{5... | collective-permute-start | bytes 1179656 | tf_op jit(solution)/shard_map/ppermute | solution.py:77
  35.1 14.8 %collective-permute-start.11 = (bf16[3,4,128,128]{3,2,1,0:T(8,128)(2,1)S(1)}, bf16[3,4,128,128]{3,2,1,0:T(8,128)(2,1)S(1)}, u32[]{:S(2)}, u32[]{:S(2)}) collective-permute-start(bf16[3,4,128,128]{3,2,1,0:T(8,128)(2,1)S(1)} %get-tuple-element.44.rest_0_), channel_id=1, source_target_pairs={{0,1},{1,0},{2,3},{3,2},{4,5},{5,4},{6,7},{7,6},{8,9},{9,8},{10,11... | collective-permute-start | bytes 1179656 | tf_op jit(solution)/shard_map/ppermute | solution.py:77
  35.1 15.3 %collective-permute-start.12 = (bf16[3,4,128,128]{3,2,1,0:T(8,128)(2,1)S(1)}, bf16[3,4,128,128]{3,2,1,0:T(8,128)(2,1)S(1)}, u32[]{:S(2)}, u32[]{:S(2)}) collective-permute-start(bf16[3,4,128,128]{3,2,1,0:T(8,128)(2,1)S(1)} %get-tuple-element.45.rest_1_), channel_id=1, source_target_pairs={{0,1},{1,0},{2,3},{3,2},{4,5},{5,4},{6,7},{7,6},{8,9},{9,8},{10,11... | collective-permute-start | bytes 1179656 | tf_op jit(solution)/shard_map/ppermute | solution.py:77
  43.0 7.4 %collective-permute-start.6 = (bf16[2,4,128,128]{3,2,1,0:T(8,128)(2,1)S(1)}, bf16[2,4,128,128]{3,2,1,0:T(8,128)(2,1)S(1)}, u32[]{:S(2)}, u32[]{:S(2)}) collective-permute-start(bf16[2,4,128,128]{3,2,1,0:T(8,128)(2,1)S(1)} %collective-permute-done.5.rest_2_), channel_id=1, source_target_pairs={{0,1},{1,0},{2,3},{3,2},{4,5},{5,4},{6,7},{7,6},{8,9},{9,8},{10,11... | collective-permute-start | bytes 786440 | tf_op jit(solution)/shard_map/ppermute | solution.py:77
  43.3 9.2 %collective-permute-start.15 = (bf16[3,4,128,128]{3,2,1,0:T(8,128)(2,1)S(1)}, bf16[3,4,128,128]{3,2,1,0:T(8,128)(2,1)S(1)}, u32[]{:S(2)}, u32[]{:S(2)}) collective-permute-start(bf16[3,4,128,128]{3,2,1,0:T(8,128)(2,1)S(1)} %collective-permute-done.13.rest_4_), channel_id=1, source_target_pairs={{0,1},{1,0},{2,3},{3,2},{4,5},{5,4},{6,7},{7,6},{8,9},{9,8},{10,11... | collective-permute-start | bytes 1179656 | tf_op jit(solution)/shard_map/ppermute | solution.py:77
  49.4 9.1 %collective-permute-start.21 = (bf16[3,4,128,128]{3,2,1,0:T(8,128)(2,1)S(1)}, bf16[3,4,128,128]{3,2,1,0:T(8,128)(2,1)S(1)}, u32[]{:S(2)}, u32[]{:S(2)}) collective-permute-start(bf16[3,4,128,128]{3,2,1,0:T(8,128)(2,1)S(1)} %collective-permute-done.17.rest_8_), channel_id=1, source_target_pairs={{0,2},{1,3},{2,0},{3,1},{4,6},{5,7},{6,4},{7,5},{8,10},{9,11},{10,... | collective-permute-start | bytes 1179656 | tf_op jit(solution)/shard_map/ppermute | solution.py:77
  49.9 8.8 %collective-permute-start.22 = (bf16[3,4,128,128]{3,2,1,0:T(8,128)(2,1)S(1)}, bf16[3,4,128,128]{3,2,1,0:T(8,128)(2,1)S(1)}, u32[]{:S(2)}, u32[]{:S(2)}) collective-permute-start(bf16[3,4,128,128]{3,2,1,0:T(8,128)(2,1)S(1)} %collective-permute-done.13.rest_4_), channel_id=1, source_target_pairs={{0,4},{4,0},{8,12},{12,8},{16,20},{20,16},{24,28},{28,24},{1,5},{5... | collective-permute-start | bytes 1179656 | tf_op jit(solution)/shard_map/ppermute | solution.py:77
  50.4 1.5 %collective-permute-start.10 = (bf16[2,4,128,128]{3,2,1,0:T(8,128)(2,1)S(1)}, bf16[2,4,128,128]{3,2,1,0:T(8,128)(2,1)S(1)}, u32[]{:S(2)}, u32[]{:S(2)}) collective-permute-start(bf16[2,4,128,128]{3,2,1,0:T(8,128)(2,1)S(1)} %collective-permute-done.9.rest_6_), channel_id=1, source_target_pairs={{0,1},{1,0},{2,3},{3,2},{4,5},{5,4},{6,7},{7,6},{8,9},{9,8},{10,11... | collective-permute-start | bytes 786440 | tf_op jit(solution)/shard_map/ppermute | solution.py:77
  50.5 1.9 %collective-permute-start.8 = (bf16[2,4,128,128]{3,2,1,0:T(8,128)(2,1)S(1)}, bf16[2,4,128,128]{3,2,1,0:T(8,128)(2,1)S(1)}, u32[]{:S(2)}, u32[]{:S(2)}) collective-permute-start(bf16[2,4,128,128]{3,2,1,0:T(8,128)(2,1)S(1)} %collective-permute-done.7.rest_4_), channel_id=1, source_target_pairs={{0,1},{1,0},{2,3},{3,2},{4,5},{5,4},{6,7},{7,6},{8,9},{9,8},{10,11... | collective-permute-start | bytes 786440 | tf_op jit(solution)/shard_map/ppermute | solution.py:77
  52.0 7.5 %collective-permute-start.19 = (bf16[3,4,128,128]{3,2,1,0:T(8,128)(2,1)S(1)}, bf16[3,4,128,128]{3,2,1,0:T(8,128)(2,1)S(1)}, u32[]{:S(2)}, u32[]{:S(2)}) collective-permute-start(bf16[3,4,128,128]{3,2,1,0:T(8,128)(2,1)S(1)} %collective-permute-done.17.rest_8_), channel_id=1, source_target_pairs={{0,1},{1,0},{2,3},{3,2},{4,5},{5,4},{6,7},{7,6},{8,9},{9,8},{10,11... | collective-permute-start | bytes 1179656 | tf_op jit(solution)/shard_map/ppermute | solution.py:77
  52.4 7.2 %collective-permute-start.16 = (bf16[3,4,128,128]{3,2,1,0:T(8,128)(2,1)S(1)}, bf16[3,4,128,128]{3,2,1,0:T(8,128)(2,1)S(1)}, u32[]{:S(2)}, u32[]{:S(2)}) collective-permute-start(bf16[3,4,128,128]{3,2,1,0:T(8,128)(2,1)S(1)} %collective-permute-done.14.rest_5_), channel_id=1, source_target_pairs={{0,1},{1,0},{2,3},{3,2},{4,5},{5,4},{6,7},{7,6},{8,9},{9,8},{10,11... | collective-permute-start | bytes 1179656 | tf_op jit(solution)/shard_map/ppermute | solution.py:77
  52.5 7.0 %collective-permute-start.20 = (bf16[3,4,128,128]{3,2,1,0:T(8,128)(2,1)S(1)}, bf16[3,4,128,128]{3,2,1,0:T(8,128)(2,1)S(1)}, u32[]{:S(2)}, u32[]{:S(2)}) collective-permute-start(bf16[3,4,128,128]{3,2,1,0:T(8,128)(2,1)S(1)} %collective-permute-done.18.rest_9_), channel_id=1, source_target_pairs={{0,1},{1,0},{2,3},{3,2},{4,5},{5,4},{6,7},{7,6},{8,9},{9,8},{10,11... | collective-permute-start | bytes 1179656 | tf_op jit(solution)/shard_map/ppermute | solution.py:77
  58.4 2.6 %collective-permute-start.23 = (bf16[3,4,128,128]{3,2,1,0:T(8,128)(2,1)S(1)}, bf16[3,4,128,128]{3,2,1,0:T(8,128)(2,1)S(1)}, u32[]{:S(2)}, u32[]{:S(2)}) collective-permute-start(bf16[3,4,128,128]{3,2,1,0:T(8,128)(2,1)S(1)} %collective-permute-done.21.rest_3_.rest_12_), channel_id=1, source_target_pairs={{0,1},{1,0},{2,3},{3,2},{4,5},{5,4},{6,7},{7,6},{8,9},{9,8},{10,11... | collective-permute-start | bytes 1179656 | tf_op jit(solution)/shard_map/ppermute | solution.py:77
  58.7 2.4 %collective-permute-start.24 = (bf16[3,4,128,128]{3,2,1,0:T(8,128)(2,1)S(1)}, bf16[3,4,128,128]{3,2,1,0:T(8,128)(2,1)S(1)}, u32[]{:S(2)}, u32[]{:S(2)}) collective-permute-start(bf16[3,4,128,128]{3,2,1,0:T(8,128)(2,1)S(1)} %collective-permute-done.22.rest_4_.rest_13_), channel_id=1, source_target_pairs={{0,1},{1,0},{2,3},{3,2},{4,5},{5,4},{6,7},{7,6},{8,9},{9,8},{10,11... | collective-permute-start | bytes 1179656 | tf_op jit(solution)/shard_map/ppermute | solution.py:77
  61.9 7.4 %collective-permute-start.27 = (s32[32,768]{1,0:T(8,128)S(1)}, s32[32,768]{1,0:T(8,128)S(1)}, u32[]{:S(2)}, u32[]{:S(2)}) collective-permute-start(s32[32,768]{1,0:T(8,128)S(1)} %pad_add_fusion.5), channel_id=1, source_target_pairs={{0,24},{4,28},{8,16},{12,20},{16,8},{20,12},{24,0},{28,4},{1,25},{... | collective-permute-start | bytes 294920 | tf_op jit(solution)/shard_map/ppermute | solution.py:77
  65.9 8.3 %collective-permute-start.26 = (s32[32,768]{1,0:T(8,128)S(1)}, s32[32,768]{1,0:T(8,128)S(1)}, u32[]{:S(2)}, u32[]{:S(2)}) collective-permute-start(s32[32,768]{1,0:T(8,128)S(1)} %pad_add_fusion.4), channel_id=1, source_target_pairs={{0,16},{4,20},{8,24},{12,28},{16,0},{20,4},{24,8},{28,12},{1,17},{... | collective-permute-start | bytes 294920 | tf_op jit(solution)/shard_map/ppermute | solution.py:77
  66.0 8.2 %collective-permute-start.25 = (s32[32,768]{1,0:T(8,128)S(1)}, s32[32,768]{1,0:T(8,128)S(1)}, u32[]{:S(2)}, u32[]{:S(2)}) collective-permute-start(s32[32,768]{1,0:T(8,128)S(1)} %pad_add_fusion.3), channel_id=1, source_target_pairs={{0,8},{4,12},{8,0},{12,4},{16,24},{20,28},{24,16},{28,20},{1,9},{5... | collective-permute-start | bytes 294920 | tf_op jit(solution)/shard_map/ppermute | solution.py:77
  76.1 8.0 %collective-permute-start.29 = (s32[32,768]{1,0:T(8,128)S(1)}, s32[32,768]{1,0:T(8,128)S(1)}, u32[]{:S(2)}, u32[]{:S(2)}) collective-permute-start(s32[32,768]{1,0:T(8,128)S(1)} %shard_map.57), channel_id=1, source_target_pairs={{0,16},{4,20},{8,24},{12,28},{16,0},{20,4},{24,8},{28,12},{1,17},{... | collective-permute-start | bytes 294920 | tf_op jit(solution)/shard_map/ppermute | solution.py:77
  77.1 8.2 %collective-permute-start.28 = (s32[32,768]{1,0:T(8,128)S(1)}, s32[32,768]{1,0:T(8,128)S(1)}, u32[]{:S(2)}, u32[]{:S(2)}) collective-permute-start(s32[32,768]{1,0:T(8,128)S(1)} %shard_map.56), channel_id=1, source_target_pairs={{0,8},{4,12},{8,0},{12,4},{16,24},{20,28},{24,16},{28,20},{1,9},{5... | collective-permute-start | bytes 294920 | tf_op jit(solution)/shard_map/ppermute | solution.py:77
  80.1 6.4 %collective-permute-start.30 = (s32[32,768]{1,0:T(8,128)S(1)}, s32[32,768]{1,0:T(8,128)S(1)}, u32[]{:S(2)}, u32[]{:S(2)}) collective-permute-start(s32[32,768]{1,0:T(8,128)S(1)} %get-tuple-element.56), channel_id=1, source_target_pairs={{0,24},{4,28},{8,16},{12,20},{16,8},{20,12},{24,0},{28,4},{1,25},{... | collective-permute-start | bytes 294920 | tf_op jit(solution)/shard_map/ppermute | solution.py:77
  88.4 5.4 %collective-permute-start.31 = (s32[32,768]{1,0:T(8,128)S(1)}, s32[32,768]{1,0:T(8,128)S(1)}, u32[]{:S(2)}, u32[]{:S(2)}) collective-permute-start(s32[32,768]{1,0:T(8,128)S(1)} %shard_map.59), channel_id=1, source_target_pairs={{0,8},{4,12},{8,0},{12,4},{16,24},{20,28},{24,16},{28,20},{1,9},{5... | collective-permute-start | bytes 294920 | tf_op jit(solution)/shard_map/ppermute | solution.py:77
  90.8 9.7 %collective-permute-start.32 = (s32[32,768]{1,0:T(8,128)S(1)}, s32[32,768]{1,0:T(8,128)S(1)}, u32[]{:S(2)}, u32[]{:S(2)}) collective-permute-start(s32[32,768]{1,0:T(8,128)S(1)} %shard_map.60), channel_id=1, source_target_pairs={{0,16},{4,20},{8,24},{12,28},{16,0},{20,4},{24,8},{28,12},{1,17},{... | collective-permute-start | bytes 294920 | tf_op jit(solution)/shard_map/ppermute | solution.py:77
  91.4 9.1 %collective-permute-start.33 = (s32[32,768]{1,0:T(8,128)S(1)}, s32[32,768]{1,0:T(8,128)S(1)}, u32[]{:S(2)}, u32[]{:S(2)}) collective-permute-start(s32[32,768]{1,0:T(8,128)S(1)} %get-tuple-element.58), channel_id=1, source_target_pairs={{0,24},{4,28},{8,16},{12,20},{16,8},{20,12},{24,0},{28,4},{1,25},{... | collective-permute-start | bytes 294920 | tf_op jit(solution)/shard_map/ppermute | solution.py:77
  100.6 3.2 %copy-start.2 = (f32[128,256]{1,0:T(8,128)S(1)}, f32[128,256]{1,0:T(8,128)}, u32[]{:S(2)}) copy-start(f32[128,256]{1,0:T(8,128)} %paths_in.1) | copy-start | bytes 393220
  101.7 4.5 %collective-permute-start.34 = (bf16[32,1024]{1,0:T(8,128)(2,1)S(1)}, bf16[32,1024]{1,0:T(8,128)(2,1)S(1)}, u32[]{:S(2)}, u32[]{:S(2)}) collective-permute-start(bf16[32,1024]{1,0:T(8,128)(2,1)S(1)} %fusion.8), channel_id=1, source_target_pairs={{0,8},{4,12},{8,0},{12,4},{16,24},{20,28},{24,16},{28,20},{1,9},{5... | collective-permute-start | bytes 196616 | tf_op jit(solution)/shard_map/ppermute | solution.py:77
  103.8 7.4 %collective-permute-start.35 = (bf16[32,1024]{1,0:T(8,128)(2,1)S(1)}, bf16[32,1024]{1,0:T(8,128)(2,1)S(1)}, u32[]{:S(2)}, u32[]{:S(2)}) collective-permute-start(bf16[32,1024]{1,0:T(8,128)(2,1)S(1)} %fusion.8), channel_id=1, source_target_pairs={{0,16},{4,20},{8,24},{12,28},{16,0},{20,4},{24,8},{28,12},{1,17},{... | collective-permute-start | bytes 196616 | tf_op jit(solution)/shard_map/ppermute | solution.py:77
  104.1 8.1 %collective-permute-start.36 = (bf16[32,1024]{1,0:T(8,128)(2,1)S(1)}, bf16[32,1024]{1,0:T(8,128)(2,1)S(1)}, u32[]{:S(2)}, u32[]{:S(2)}) collective-permute-start(bf16[32,1024]{1,0:T(8,128)(2,1)S(1)} %fusion.8), channel_id=1, source_target_pairs={{0,24},{4,28},{8,16},{12,20},{16,8},{20,12},{24,0},{28,4},{1,25},{... | collective-permute-start | bytes 196616 | tf_op jit(solution)/shard_map/ppermute | solution.py:77
  112.7 5.6 %collective-permute-start.37 = (bf16[32,1024]{1,0:T(8,128)(2,1)S(1)}, bf16[32,1024]{1,0:T(8,128)(2,1)S(1)}, u32[]{:S(2)}, u32[]{:S(2)}) collective-permute-start(bf16[32,1024]{1,0:T(8,128)(2,1)S(1)} %get-tuple-element.60), channel_id=1, source_target_pairs={{0,8},{4,12},{8,0},{12,4},{16,24},{20,28},{24,16},{28,20},{1,9},{5... | collective-permute-start | bytes 196616 | tf_op jit(solution)/shard_map/ppermute | solution.py:77
  113.0 5.7 %collective-permute-start.38 = (bf16[32,1024]{1,0:T(8,128)(2,1)S(1)}, bf16[32,1024]{1,0:T(8,128)(2,1)S(1)}, u32[]{:S(2)}, u32[]{:S(2)}) collective-permute-start(bf16[32,1024]{1,0:T(8,128)(2,1)S(1)} %get-tuple-element.60), channel_id=1, source_target_pairs={{0,16},{4,20},{8,24},{12,28},{16,0},{20,4},{24,8},{28,12},{1,17},{... | collective-permute-start | bytes 196616 | tf_op jit(solution)/shard_map/ppermute | solution.py:77
  115.0 6.1 %collective-permute-start.39 = (bf16[32,1024]{1,0:T(8,128)(2,1)S(1)}, bf16[32,1024]{1,0:T(8,128)(2,1)S(1)}, u32[]{:S(2)}, u32[]{:S(2)}) collective-permute-start(bf16[32,1024]{1,0:T(8,128)(2,1)S(1)} %get-tuple-element.60), channel_id=1, source_target_pairs={{0,24},{4,28},{8,16},{12,20},{16,8},{20,12},{24,0},{28,4},{1,25},{... | collective-permute-start | bytes 196616 | tf_op jit(solution)/shard_map/ppermute | solution.py:77
  121.6 4.6 %collective-permute-start.40 = (bf16[32,1024]{1,0:T(8,128)(2,1)S(1)}, bf16[32,1024]{1,0:T(8,128)(2,1)S(1)}, u32[]{:S(2)}, u32[]{:S(2)}) collective-permute-start(bf16[32,1024]{1,0:T(8,128)(2,1)S(1)} %get-tuple-element.63), channel_id=1, source_target_pairs={{0,8},{4,12},{8,0},{12,4},{16,24},{20,28},{24,16},{28,20},{1,9},{5... | collective-permute-start | bytes 196616 | tf_op jit(solution)/shard_map/ppermute | solution.py:77
  121.7 5.2 %collective-permute-start.41 = (bf16[32,1024]{1,0:T(8,128)(2,1)S(1)}, bf16[32,1024]{1,0:T(8,128)(2,1)S(1)}, u32[]{:S(2)}, u32[]{:S(2)}) collective-permute-start(bf16[32,1024]{1,0:T(8,128)(2,1)S(1)} %get-tuple-element.63), channel_id=1, source_target_pairs={{0,16},{4,20},{8,24},{12,28},{16,0},{20,4},{24,8},{28,12},{1,17},{... | collective-permute-start | bytes 196616 | tf_op jit(solution)/shard_map/ppermute | solution.py:77
  124.5 6.1 %collective-permute-start.42 = (bf16[32,1024]{1,0:T(8,128)(2,1)S(1)}, bf16[32,1024]{1,0:T(8,128)(2,1)S(1)}, u32[]{:S(2)}, u32[]{:S(2)}) collective-permute-start(bf16[32,1024]{1,0:T(8,128)(2,1)S(1)} %get-tuple-element.63), channel_id=1, source_target_pairs={{0,24},{4,28},{8,16},{12,20},{16,8},{20,12},{24,0},{28,4},{1,25},{... | collective-permute-start | bytes 196616 | tf_op jit(solution)/shard_map/ppermute | solution.py:77
  131.1 1.3 collective-permute-start.43
  132.4 5.5 %collective-permute-start.46 = (f32[2,32,128]{2,1,0:T(8,128)S(1)}, f32[2,32,128]{2,1,0:T(8,128)S(1)}, u32[]{:S(2)}, u32[]{:S(2)}) collective-permute-start(f32[2,32,128]{2,1,0:T(8,128)S(1)} %pad_maximum_fusion.8), channel_id=1, source_target_pairs={{0,6},{1,7},{2,4},{3,5},{4,2},{5,3},{6,0},{7,1},{8,14},{9,15},{10,... | collective-permute-start | bytes 98312 | tf_op jit(solution)/shard_map/ppermute | solution.py:427
  136.0 3.9 %collective-permute-start.45 = (f32[2,32,128]{2,1,0:T(8,128)S(1)}, f32[2,32,128]{2,1,0:T(8,128)S(1)}, u32[]{:S(2)}, u32[]{:S(2)}) collective-permute-start(f32[2,32,128]{2,1,0:T(8,128)S(1)} %pad_maximum_fusion.7), channel_id=1, source_target_pairs={{0,4},{4,0},{8,12},{12,8},{16,20},{20,16},{24,28},{28,24},{1,5},{5... | collective-permute-start | bytes 98312 | tf_op jit(solution)/shard_map/ppermute | solution.py:77
  137.5 3.9 %collective-permute-start.44 = (f32[2,32,128]{2,1,0:T(8,128)S(1)}, f32[2,32,128]{2,1,0:T(8,128)S(1)}, u32[]{:S(2)}, u32[]{:S(2)}) collective-permute-start(f32[2,32,128]{2,1,0:T(8,128)S(1)} %pad_maximum_fusion.6), channel_id=1, source_target_pairs={{0,2},{1,3},{2,0},{3,1},{4,6},{5,7},{6,4},{7,5},{8,10},{9,11},{10,... | collective-permute-start | bytes 98312 | tf_op jit(solution)/shard_map/ppermute | solution.py:77
  (6 other events, 8.2 us)

commit v5 on v4

--- a/solution.py
+++ b/solution.py
@@ -84,6 +84,8 @@
 
 GROUP = 8
 LAYERS = 4
+SUMS = (3, 1, 2)
+SPREADS = (3, 1, 2)
 LOWEST = 5
 MANTISSA = 18
 BYTE = 255
@@ -462,34 +464,35 @@
         for block in (same, same_x, same_y, same_d)
         for part in (block, swap(block, "col", 1))
     ]
-    whole = assembled(blocks, 1) + assembled(near + far + last, 2)
-
-    def across(value):
+    others = assembled(near + far + last, 2)
+    whole = assembled(blocks, 1) + others
+
+    def across(order, value):
         got = {}
-        for k in reversed(range(1, LAYERS)):
+        for k in order:
             got[k] = swap(value(k), "row", 2 * k)
         return got
 
-    got = across(lambda k: coded(first[k - 1]))
+    got = across(SUMS, lambda k: coded(first[k - 1]))
     counts = []
     for distance in (1, 2):
         own = across_terms(front, whole[0])
         got = [got[k] for k in range(1, LAYERS)]
-        count, front, words = level_terms(MASKS[distance], own, got, word, whole[-1])
+        count, front, words = level_terms(MASKS[distance], own, got, word, whole[SUMS[0]])
         counts.append(count)
-        got = across(lambda k: words if k == LAYERS - 1 else message(front, whole[k]))
+        got = across(SUMS, lambda k: words if k == SUMS[0] else message(front, whole[k]))
     total = across_terms(front, whole[0])
     for k in range(1, LAYERS):
         total = total + decoded(got[k])
     weight = jnp.where(MASKS[3](word), word / jnp.maximum(total, 1.0), 0.0).astype(jnp.bfloat16)
     found = jnp.zeros_like(word)
     for distance in (2, 1, 0):
-        got = across(lambda k: weight)
+        got = across(SPREADS, lambda k: weight)
         part = jnp.dot(weight, whole[0], preferred_element_type=jnp.float32)
-        for k in (1, 2):
+        for k in SPREADS[:-1]:
             part = part + jnp.dot(got[k], whole[k], preferred_element_type=jnp.float32)
         count = counts[distance - 1] if distance else None
-        found, *weight = back_terms(MASKS[distance], part, got[3], whole[3], count, found, word)
+        found, *weight = back_terms(MASKS[distance], part, got[SPREADS[-1]], whole[SPREADS[-1]], count, found, word)
         weight = weight[0] if weight else None
 
     keep, send = spread_found(found)

time: 142 us -> 139 us (0.979)
  waiting for transfers between devices: 67.1 us -> 65.3 us
  starting transfers between devices: 49.4 us -> 47.9 us
    ppermute x44, waiting for transfers between devices: 55.9 us -> 53.1 us  [swap(): return lax.ppermute(value, axis, partner(axis, bit))]
    ppermute x2, starting transfers between devices: 5.04 us -> 3.34 us  [traded(): from_d = lax.ppermute(held[3], ('row', 'col'), diagonal())]
  transfers between devices with their start and end apart: 47 -> 47, of which waited for: 24 -> 25; matrix products, arithmetic and copies ran while one was open for 4% -> 4% of each run, Pallas kernels for 4% -> 4%
where the time goes in v5:
time: 139 us
  waiting for transfers between devices  65.3 us (47%)
  starting transfers between devices  47.9 us (34%)
  Pallas kernels  12.8 us (9%)
  matrix products  6.81 us (5%)
  local copies, waits for them, and re-layouts  5.04 us (4%)
    ppermute x44, waiting for transfers between devices, swap(): return lax.ppermute(value, axis, partner(axis, bit))  53.1 us
    ppermute x44, starting transfers between devices, swap(): return lax.ppermute(value, axis, partner(axis, bit))  41.5 us
    ppermute x1, waiting for transfers between devices, split_shards(): same_d = lax.ppermute(flipped, ('row', 'col'), diagonal())  10.8 us
    pallas_call x9, Pallas kernels, vmem_call(): pl.pallas_call(kernel, out_shape=outs, in_specs=[IN_VMEM] * len(args), ou...  6.87 us
    unnamed x14, local copies, waits for them, and re-layouts  5 us
    ppermute x2, starting transfers between devices, traded(): from_d = lax.ppermute(held[3], ('row', 'col'), diagonal())  3.34 us
    ppermute x1, starting transfers between devices, split_shards(): same_d = lax.ppermute(flipped, ('row', 'col'), diagonal())  2.98 us
    dot_general x6, matrix products, split_shards(): part = part + jnp.dot(got[k], whole[k], preferred_element_type=jnp.float32)  2.8 us
  transfers between devices with their start and end apart: 47, of which 25 were waited for; matrix products, arithmetic and copies ran while one was open for 4% of the time, Pallas kernels for 4%

profile of v5, /device:TPU:0, one launch (start us, length us, event | category | flops | bytes accessed | tf_op | source)
XLA Modules:
  0.0 138.9 jit_solution(18380516772400272970)
XLA Ops:
  0.0 0.9 copy-done.1
  0.9 0.9 copy-done.3
  1.8 0.9 copy-done.5
  3.4 1.6 %copy-done = s32[1,1,8,4,128,128]{5,4,3,2,1,0:T(8,128)S(1)} copy-done((s32[1,1,8,4,128,128]{5,4,3,2,1,0:T(8,128)S(1)}, s32[1,1,8,4,128,128]{5,4,3,2,1,0:T(8,128)}, u32[]{:S(2)}) %copy-start) | copy-done | bytes 2097176
  6.4 2.6 %collective-permute-start.5 = (bf16[2,4,128,128]{3,2,1,0:T(8,128)(2,1)S(1)}, bf16[2,4,128,128]{3,2,1,0:T(8,128)(2,1)S(1)}, u32[]{:S(2)}, u32[]{:S(2)}) collective-permute-start(bf16[2,4,128,128]{3,2,1,0:T(8,128)(2,1)S(1)} %get-tuple-element.42.rest_0_), channel_id=1, source_target_pairs={{0,2},{1,3},{2,0},{3,1},{4,6},{5,7},{6,4},{7,5},{8,10},{9,11},{10,... | collective-permute-start | bytes 786440 | tf_op jit(solution)/shard_map/ppermute | solution.py:77
  9.1 2.0 %collective-permute-start.2 = (f32[2,32,128]{2,1,0:T(8,128)S(1)}, f32[2,32,128]{2,1,0:T(8,128)S(1)}, u32[]{:S(2)}, u32[]{:S(2)}) collective-permute-start(f32[2,32,128]{2,1,0:T(8,128)S(1)} %pad_maximum_fusion.3), channel_id=1, source_target_pairs={{0,4},{4,0},{8,12},{12,8},{16,20},{20,16},{24,28},{28,24},{1,5},{5... | collective-permute-start | bytes 98312 | tf_op jit(solution)/shard_map/ppermute | solution.py:77
  11.1 1.4 %collective-permute-start.3 = (f32[2,32,128]{2,1,0:T(8,128)S(1)}, f32[2,32,128]{2,1,0:T(8,128)S(1)}, u32[]{:S(2)}, u32[]{:S(2)}) collective-permute-start(f32[2,32,128]{2,1,0:T(8,128)S(1)} %pad_maximum_fusion.4), channel_id=1, source_target_pairs={{0,6},{1,7},{2,4},{3,5},{4,2},{5,3},{6,0},{7,1},{8,14},{9,15},{10,... | collective-permute-start | bytes 98312 | tf_op jit(solution)/shard_map/ppermute | solution.py:429
  12.7 4.2 %collective-permute-done.1.rest_1_ = f32[2,32,128]{2,1,0:T(8,128)S(1)} collective-permute-done((f32[2,32,128]{2,1,0:T(8,128)S(1)}, f32[2,32,128]{2,1,0:T(8,128)S(1)}, u32[]{:S(2)}, u32[]{:S(2)}) %collective-permute-start.1) | collective-permute-done | bytes 32800 | tf_op jit(solution)/shard_map/ppermute | solution.py:77
  16.8 3.0 %collective-permute-start.9 = (bf16[2,4,128,128]{3,2,1,0:T(8,128)(2,1)S(1)}, bf16[2,4,128,128]{3,2,1,0:T(8,128)(2,1)S(1)}, u32[]{:S(2)}, u32[]{:S(2)}) collective-permute-start(bf16[2,4,128,128]{3,2,1,0:T(8,128)(2,1)S(1)} %get-tuple-element.43), channel_id=1, source_target_pairs={{0,6},{1,7},{2,4},{3,5},{4,2},{5,3},{6,0},{7,1},{8,14},{9,15},{10,... | collective-permute-start | bytes 786440 | tf_op jit(solution)/shard_map/ppermute | solution.py:454
  20.3 1.6 %collective-permute-start.17 = (bf16[3,4,128,128]{3,2,1,0:T(8,128)(2,1)S(1)}, bf16[3,4,128,128]{3,2,1,0:T(8,128)(2,1)S(1)}, u32[]{:S(2)}, u32[]{:S(2)}) collective-permute-start(bf16[3,4,128,128]{3,2,1,0:T(8,128)(2,1)S(1)} %get-tuple-element.45.rest_1_), channel_id=1, source_target_pairs={{0,4},{4,0},{8,12},{12,8},{16,20},{20,16},{24,28},{28,24},{1,5},{5... | collective-permute-start | bytes 1179656 | tf_op jit(solution)/shard_map/ppermute | solution.py:77
  21.9 10.8 %collective-permute-done.9.rest_6_ = bf16[2,4,128,128]{3,2,1,0:T(8,128)(2,1)S(1)} collective-permute-done((bf16[2,4,128,128]{3,2,1,0:T(8,128)(2,1)S(1)}, bf16[2,4,128,128]{3,2,1,0:T(8,128)(2,1)S(1)}, u32[]{:S(2)}, u32[]{:S(2)}) %collective-permute-start.9) | collective-permute-done | bytes 262176 | tf_op jit(solution)/shard_map/ppermute | solution.py:454
  32.7 1.5 %collective-permute-start.14 = (bf16[3,4,128,128]{3,2,1,0:T(8,128)(2,1)S(1)}, bf16[3,4,128,128]{3,2,1,0:T(8,128)(2,1)S(1)}, u32[]{:S(2)}, u32[]{:S(2)}) collective-permute-start(bf16[3,4,128,128]{3,2,1,0:T(8,128)(2,1)S(1)} %get-tuple-element.45.rest_1_), channel_id=1, source_target_pairs={{0,2},{1,3},{2,0},{3,1},{4,6},{5,7},{6,4},{7,5},{8,10},{9,11},{10,... | collective-permute-start | bytes 1179656 | tf_op jit(solution)/shard_map/ppermute | solution.py:77
  35.6 7.4 %collective-permute-done.17.rest_8_ = bf16[3,4,128,128]{3,2,1,0:T(8,128)(2,1)S(1)} collective-permute-done((bf16[3,4,128,128]{3,2,1,0:T(8,128)(2,1)S(1)}, bf16[3,4,128,128]{3,2,1,0:T(8,128)(2,1)S(1)}, u32[]{:S(2)}, u32[]{:S(2)}) %collective-permute-start.17) | collective-permute-done | bytes 393248 | tf_op jit(solution)/shard_map/ppermute | solution.py:77
  43.5 5.8 %collective-permute-done.18.rest_9_ = bf16[3,4,128,128]{3,2,1,0:T(8,128)(2,1)S(1)} collective-permute-done((bf16[3,4,128,128]{3,2,1,0:T(8,128)(2,1)S(1)}, bf16[3,4,128,128]{3,2,1,0:T(8,128)(2,1)S(1)}, u32[]{:S(2)}, u32[]{:S(2)}) %collective-permute-start.18) | collective-permute-done | bytes 393248 | tf_op jit(solution)/shard_map/ppermute | solution.py:77
  51.0 1.0 collective-permute-done.10.rest_7_
  52.9 5.5 %collective-permute-done.21.rest_3_.rest_12_ = bf16[3,4,128,128]{3,2,1,0:T(8,128)(2,1)S(1)} collective-permute-done((bf16[3,4,128,128]{3,2,1,0:T(8,128)(2,1)S(1)}, bf16[3,4,128,128]{3,2,1,0:T(8,128)(2,1)S(1)}, u32[]{:S(2)}, u32[]{:S(2)}) %collective-permute-start.21) | collective-permute-done | bytes 393248 | tf_op jit(solution)/shard_map/ppermute | solution.py:77
  59.6 1.5 %first.2 = (f32[32,1024]{1,0:T(8,128)S(1)}, f32[32,1024]{1,0:T(8,128)S(1)}, f32[32,1024]{1,0:T(8,128)S(1)}) custom-call(bf16[32,1024]{1,0:T(8,128)(2,1)S(1)} %get-tuple-element.41.front, bf16[3,4,128,128]{3,2,1,0:T(8,128)(2,1)S(1)} %get-tuple-element.44.rest_0_, bf16[3,4,128,128]{3,2,1,0:T(8,128)(2,1)S(1)} %get-tuple-element.45.rest_1_, ...), custom_call_target="tpu_custom_call" | custom-call | flops 150994944 | bytes 4718592 | tf_op jit(solution)/shard_map/first/pallas_call | solution.py:251
  61.9 3.7 %collective-permute-start.27 = (s32[32,768]{1,0:T(8,128)S(1)}, s32[32,768]{1,0:T(8,128)S(1)}, u32[]{:S(2)}, u32[]{:S(2)}) collective-permute-start(s32[32,768]{1,0:T(8,128)S(1)} %pad_add_fusion.5), channel_id=1, source_target_pairs={{0,24},{4,28},{8,16},{12,20},{16,8},{20,12},{24,0},{28,4},{1,25},{... | collective-permute-start | bytes 294920 | tf_op jit(solution)/shard_map/ppermute | solution.py:77
  67.6 1.7 %assemble.3 = (bf16[1024,1024]{1,0:T(8,128)(2,1)S(1)}, bf16[1024,1024]{1,0:T(8,128)(2,1)S(1)}, bf16[1024,1024]{1,0:T(8,128)(2,1)S(1)}) custom-call(bf16[3,4,128,128]{3,2,1,0:T(8,128)(2,1)S(1)} %get-tuple-element.44.rest_0_, bf16[3,4,128,128]{3,2,1,0:T(8,128)(2,1)S(1)} %get-tuple-element.45.rest_1_, ...), custom_call_target="tpu_custom_call" | custom-call | bytes 12582912 | tf_op jit(solution)/shard_map/assemble/pallas_call | solution.py:282
  69.3 5.0 %collective-permute-done.26.rest_1_ = s32[32,768]{1,0:T(8,128)S(1)} collective-permute-done((s32[32,768]{1,0:T(8,128)S(1)}, s32[32,768]{1,0:T(8,128)S(1)}, u32[]{:S(2)}, u32[]{:S(2)}) %collective-permute-start.26) | collective-permute-done | bytes 98336 | tf_op jit(solution)/shard_map/ppermute | solution.py:77
  74.2 1.0 shard_map.55
  77.1 3.0 %collective-permute-start.28 = (s32[32,768]{1,0:T(8,128)S(1)}, s32[32,768]{1,0:T(8,128)S(1)}, u32[]{:S(2)}, u32[]{:S(2)}) collective-permute-start(s32[32,768]{1,0:T(8,128)S(1)} %shard_map.56), channel_id=1, source_target_pairs={{0,8},{4,12},{8,0},{12,4},{16,24},{20,28},{24,16},{28,20},{1,9},{5... | collective-permute-start | bytes 294920 | tf_op jit(solution)/shard_map/ppermute | solution.py:77
  80.1 1.3 collective-permute-start.30
  82.2 1.9 %collective-permute-done.29.rest_1_ = s32[32,768]{1,0:T(8,128)S(1)} collective-permute-done((s32[32,768]{1,0:T(8,128)S(1)}, s32[32,768]{1,0:T(8,128)S(1)}, u32[]{:S(2)}, u32[]{:S(2)}) %collective-permute-start.29) | collective-permute-done | bytes 98336 | tf_op jit(solution)/shard_map/ppermute | solution.py:77
  84.1 1.3 collective-permute-done.28.rest_0_
  85.3 1.2 collective-permute-done.30.rest_2_
  86.5 1.0 shard_map.58
  88.4 1.6 %collective-permute-start.31 = (s32[32,768]{1,0:T(8,128)S(1)}, s32[32,768]{1,0:T(8,128)S(1)}, u32[]{:S(2)}, u32[]{:S(2)}) collective-permute-start(s32[32,768]{1,0:T(8,128)S(1)} %shard_map.59), channel_id=1, source_target_pairs={{0,8},{4,12},{8,0},{12,4},{16,24},{20,28},{24,16},{28,20},{1,9},{5... | collective-permute-start | bytes 294920 | tf_op jit(solution)/shard_map/ppermute | solution.py:77
  91.4 2.3 %collective-permute-start.33 = (s32[32,768]{1,0:T(8,128)S(1)}, s32[32,768]{1,0:T(8,128)S(1)}, u32[]{:S(2)}, u32[]{:S(2)}) collective-permute-start(s32[32,768]{1,0:T(8,128)S(1)} %get-tuple-element.58), channel_id=1, source_target_pairs={{0,24},{4,28},{8,16},{12,20},{16,8},{20,12},{24,0},{28,4},{1,25},{... | collective-permute-start | bytes 294920 | tf_op jit(solution)/shard_map/ppermute | solution.py:77
  93.8 6.7 %collective-permute-done.32 = s32[32,768]{1,0:T(8,128)S(1)} collective-permute-done((s32[32,768]{1,0:T(8,128)S(1)}, s32[32,768]{1,0:T(8,128)S(1)}, u32[]{:S(2)}, u32[]{:S(2)}) %collective-permute-start.32) | collective-permute-done | bytes 98336 | tf_op jit(solution)/shard_map/ppermute | solution.py:77
  100.6 1.1 fusion.8
  101.7 1.7 %collective-permute-start.34 = (bf16[32,1024]{1,0:T(8,128)(2,1)S(1)}, bf16[32,1024]{1,0:T(8,128)(2,1)S(1)}, u32[]{:S(2)}, u32[]{:S(2)}) collective-permute-start(bf16[32,1024]{1,0:T(8,128)(2,1)S(1)} %fusion.8), channel_id=1, source_target_pairs={{0,24},{4,28},{8,16},{12,20},{16,8},{20,12},{24,0},{28,4},{1,25},{... | collective-permute-start | bytes 196616 | tf_op jit(solution)/shard_map/ppermute | solution.py:77
  103.4 1.0 collective-permute-start.35
  104.5 1.8 %collective-permute-start.36 = (bf16[32,1024]{1,0:T(8,128)(2,1)S(1)}, bf16[32,1024]{1,0:T(8,128)(2,1)S(1)}, u32[]{:S(2)}, u32[]{:S(2)}) collective-permute-start(bf16[32,1024]{1,0:T(8,128)(2,1)S(1)} %fusion.8), channel_id=1, source_target_pairs={{0,16},{4,20},{8,24},{12,28},{16,0},{20,4},{24,8},{28,12},{1,17},{... | collective-permute-start | bytes 196616 | tf_op jit(solution)/shard_map/ppermute | solution.py:77
  106.3 2.4 %collective-permute-done.34 = bf16[32,1024]{1,0:T(8,128)(2,1)S(1)} collective-permute-done((bf16[32,1024]{1,0:T(8,128)(2,1)S(1)}, bf16[32,1024]{1,0:T(8,128)(2,1)S(1)}, u32[]{:S(2)}, u32[]{:S(2)}) %collective-permute-start.34) | collective-permute-done | bytes 65568 | tf_op jit(solution)/shard_map/ppermute | solution.py:77
  111.4 1.8 %collective-permute-start.37 = (bf16[32,1024]{1,0:T(8,128)(2,1)S(1)}, bf16[32,1024]{1,0:T(8,128)(2,1)S(1)}, u32[]{:S(2)}, u32[]{:S(2)}) collective-permute-start(bf16[32,1024]{1,0:T(8,128)(2,1)S(1)} %get-tuple-element.60), channel_id=1, source_target_pairs={{0,24},{4,28},{8,16},{12,20},{16,8},{20,12},{24,0},{28,4},{1,25},{... | collective-permute-start | bytes 196616 | tf_op jit(solution)/shard_map/ppermute | solution.py:77
  113.3 2.7 %collective-permute-start.39 = (bf16[32,1024]{1,0:T(8,128)(2,1)S(1)}, bf16[32,1024]{1,0:T(8,128)(2,1)S(1)}, u32[]{:S(2)}, u32[]{:S(2)}) collective-permute-start(bf16[32,1024]{1,0:T(8,128)(2,1)S(1)} %get-tuple-element.60), channel_id=1, source_target_pairs={{0,16},{4,20},{8,24},{12,28},{16,0},{20,4},{24,8},{28,12},{1,17},{... | collective-permute-start | bytes 196616 | tf_op jit(solution)/shard_map/ppermute | solution.py:77
  116.0 1.7 %collective-permute-done.37 = bf16[32,1024]{1,0:T(8,128)(2,1)S(1)} collective-permute-done((bf16[32,1024]{1,0:T(8,128)(2,1)S(1)}, bf16[32,1024]{1,0:T(8,128)(2,1)S(1)}, u32[]{:S(2)}, u32[]{:S(2)}) %collective-permute-start.37) | collective-permute-done | bytes 65568 | tf_op jit(solution)/shard_map/ppermute | solution.py:77
  118.1 0.9 collective-permute-done.38
  120.5 1.9 %collective-permute-start.40 = (bf16[32,1024]{1,0:T(8,128)(2,1)S(1)}, bf16[32,1024]{1,0:T(8,128)(2,1)S(1)}, u32[]{:S(2)}, u32[]{:S(2)}) collective-permute-start(bf16[32,1024]{1,0:T(8,128)(2,1)S(1)} %get-tuple-element.63), channel_id=1, source_target_pairs={{0,24},{4,28},{8,16},{12,20},{16,8},{20,12},{24,0},{28,4},{1,25},{... | collective-permute-start | bytes 196616 | tf_op jit(solution)/shard_map/ppermute | solution.py:77
  122.5 2.5 %collective-permute-start.42 = (bf16[32,1024]{1,0:T(8,128)(2,1)S(1)}, bf16[32,1024]{1,0:T(8,128)(2,1)S(1)}, u32[]{:S(2)}, u32[]{:S(2)}) collective-permute-start(bf16[32,1024]{1,0:T(8,128)(2,1)S(1)} %get-tuple-element.63), channel_id=1, source_target_pairs={{0,16},{4,20},{8,24},{12,28},{16,0},{20,4},{24,8},{28,12},{1,17},{... | collective-permute-start | bytes 196616 | tf_op jit(solution)/shard_map/ppermute | solution.py:77
  125.0 1.7 %collective-permute-done.40 = bf16[32,1024]{1,0:T(8,128)(2,1)S(1)} collective-permute-done((bf16[32,1024]{1,0:T(8,128)(2,1)S(1)}, bf16[32,1024]{1,0:T(8,128)(2,1)S(1)}, u32[]{:S(2)}, u32[]{:S(2)}) %collective-permute-start.40) | collective-permute-done | bytes 65568 | tf_op jit(solution)/shard_map/ppermute | solution.py:77
  127.1 0.9 collective-permute-done.41
  129.6 1.2 collective-permute-done.43
  130.8 1.9 %collective-permute-start.46 = (f32[2,32,128]{2,1,0:T(8,128)S(1)}, f32[2,32,128]{2,1,0:T(8,128)S(1)}, u32[]{:S(2)}, u32[]{:S(2)}) collective-permute-start(f32[2,32,128]{2,1,0:T(8,128)S(1)} %pad_maximum_fusion.8), channel_id=1, source_target_pairs={{0,6},{1,7},{2,4},{3,5},{4,2},{5,3},{6,0},{7,1},{8,14},{9,15},{10,... | collective-permute-start | bytes 98312 | tf_op jit(solution)/shard_map/ppermute | solution.py:429
  132.7 1.5 %collective-permute-start.45 = (f32[2,32,128]{2,1,0:T(8,128)S(1)}, f32[2,32,128]{2,1,0:T(8,128)S(1)}, u32[]{:S(2)}, u32[]{:S(2)}) collective-permute-start(f32[2,32,128]{2,1,0:T(8,128)S(1)} %pad_maximum_fusion.7), channel_id=1, source_target_pairs={{0,4},{4,0},{8,12},{12,8},{16,20},{20,16},{24,28},{28,24},{1,5},{5... | collective-permute-start | bytes 98312 | tf_op jit(solution)/shard_map/ppermute | solution.py:77
  134.4 1.4 %collective-permute-done.46.rest_3_ = f32[2,32,128]{2,1,0:T(8,128)S(1)} collective-permute-done((f32[2,32,128]{2,1,0:T(8,128)S(1)}, f32[2,32,128]{2,1,0:T(8,128)S(1)}, u32[]{:S(2)}, u32[]{:S(2)}) %collective-permute-start.46) | collective-permute-done | bytes 32800 | tf_op jit(solution)/shard_map/ppermute | solution.py:429
  136.7 1.5 %collective-permute-done.44.rest_1_ = f32[2,32,128]{2,1,0:T(8,128)S(1)} collective-permute-done((f32[2,32,128]{2,1,0:T(8,128)S(1)}, f32[2,32,128]{2,1,0:T(8,128)S(1)}, u32[]{:S(2)}, u32[]{:S(2)}) %collective-permute-start.44) | collective-permute-done | bytes 32800 | tf_op jit(solution)/shard_map/ppermute | solution.py:77
  (117 shorter events, 24.7 us)
Async XLA Ops:
  2.8 6.1 %collective-permute-start = (f32[4,32,128]{2,1,0:T(8,128)S(1)}, f32[4,32,128]{2,1,0:T(8,128)S(1)}, u32[]{:S(2)}, u32[]{:S(2)}) collective-permute-start(f32[4,32,128]{2,1,0:T(8,128)S(1)} %get-tuple-element.39), channel_id=1, source_target_pairs={{0,1},{1,0},{2,3},{3,2},{4,5},{5,4},{6,7},{7,6},{8,9},{9,8},{10,11... | collective-permute-start | bytes 196616 | tf_op jit(solution)/shard_map/ppermute | solution.py:77
  6.4 13.9 %collective-permute-start.5 = (bf16[2,4,128,128]{3,2,1,0:T(8,128)(2,1)S(1)}, bf16[2,4,128,128]{3,2,1,0:T(8,128)(2,1)S(1)}, u32[]{:S(2)}, u32[]{:S(2)}) collective-permute-start(bf16[2,4,128,128]{3,2,1,0:T(8,128)(2,1)S(1)} %get-tuple-element.42.rest_0_), channel_id=1, source_target_pairs={{0,2},{1,3},{2,0},{3,1},{4,6},{5,7},{6,4},{7,5},{8,10},{9,11},{10,... | collective-permute-start | bytes 786440 | tf_op jit(solution)/shard_map/ppermute | solution.py:77
  9.0 7.8 %collective-permute-start.1 = (f32[2,32,128]{2,1,0:T(8,128)S(1)}, f32[2,32,128]{2,1,0:T(8,128)S(1)}, u32[]{:S(2)}, u32[]{:S(2)}) collective-permute-start(f32[2,32,128]{2,1,0:T(8,128)S(1)} %pad_maximum_fusion.2), channel_id=1, source_target_pairs={{0,2},{1,3},{2,0},{3,1},{4,6},{5,7},{6,4},{7,5},{8,10},{9,11},{10,... | collective-permute-start | bytes 98312 | tf_op jit(solution)/shard_map/ppermute | solution.py:77
  9.1 10.7 %collective-permute-start.2 = (f32[2,32,128]{2,1,0:T(8,128)S(1)}, f32[2,32,128]{2,1,0:T(8,128)S(1)}, u32[]{:S(2)}, u32[]{:S(2)}) collective-permute-start(f32[2,32,128]{2,1,0:T(8,128)S(1)} %pad_maximum_fusion.3), channel_id=1, source_target_pairs={{0,4},{4,0},{8,12},{12,8},{16,20},{20,16},{24,28},{28,24},{1,5},{5... | collective-permute-start | bytes 98312 | tf_op jit(solution)/shard_map/ppermute | solution.py:77
  11.1 9.2 %collective-permute-start.3 = (f32[2,32,128]{2,1,0:T(8,128)S(1)}, f32[2,32,128]{2,1,0:T(8,128)S(1)}, u32[]{:S(2)}, u32[]{:S(2)}) collective-permute-start(f32[2,32,128]{2,1,0:T(8,128)S(1)} %pad_maximum_fusion.4), channel_id=1, source_target_pairs={{0,6},{1,7},{2,4},{3,5},{4,2},{5,3},{6,0},{7,1},{8,14},{9,15},{10,... | collective-permute-start | bytes 98312 | tf_op jit(solution)/shard_map/ppermute | solution.py:429
  12.6 22.5 %collective-permute-start.13 = (bf16[3,4,128,128]{3,2,1,0:T(8,128)(2,1)S(1)}, bf16[3,4,128,128]{3,2,1,0:T(8,128)(2,1)S(1)}, u32[]{:S(2)}, u32[]{:S(2)}) collective-permute-start(bf16[3,4,128,128]{3,2,1,0:T(8,128)(2,1)S(1)} %get-tuple-element.44.rest_0_), channel_id=1, source_target_pairs={{0,2},{1,3},{2,0},{3,1},{4,6},{5,7},{6,4},{7,5},{8,10},{9,11},{10,... | collective-permute-start | bytes 1179656 | tf_op jit(solution)/shard_map/ppermute | solution.py:77
  16.8 15.9 %collective-permute-start.9 = (bf16[2,4,128,128]{3,2,1,0:T(8,128)(2,1)S(1)}, bf16[2,4,128,128]{3,2,1,0:T(8,128)(2,1)S(1)}, u32[]{:S(2)}, u32[]{:S(2)}) collective-permute-start(bf16[2,4,128,128]{3,2,1,0:T(8,128)(2,1)S(1)} %get-tuple-element.43), channel_id=1, source_target_pairs={{0,6},{1,7},{2,4},{3,5},{4,2},{5,3},{6,0},{7,1},{8,14},{9,15},{10,... | collective-permute-start | bytes 786440 | tf_op jit(solution)/shard_map/ppermute | solution.py:454
  19.8 14.8 %collective-permute-start.7 = (bf16[2,4,128,128]{3,2,1,0:T(8,128)(2,1)S(1)}, bf16[2,4,128,128]{3,2,1,0:T(8,128)(2,1)S(1)}, u32[]{:S(2)}, u32[]{:S(2)}) collective-permute-start(bf16[2,4,128,128]{3,2,1,0:T(8,128)(2,1)S(1)} %get-tuple-element.43), channel_id=1, source_target_pairs={{0,4},{4,0},{8,12},{12,8},{16,20},{20,16},{24,28},{28,24},{1,5},{5... | collective-permute-start | bytes 786440 | tf_op jit(solution)/shard_map/ppermute | solution.py:77
  20.3 14.8 %collective-permute-start.4 = (bf16[2,4,128,128]{3,2,1,0:T(8,128)(2,1)S(1)}, bf16[2,4,128,128]{3,2,1,0:T(8,128)(2,1)S(1)}, u32[]{:S(2)}, u32[]{:S(2)}) collective-permute-start(bf16[2,4,128,128]{3,2,1,0:T(8,128)(2,1)S(1)} %get-tuple-element.42.rest_0_), channel_id=1, source_target_pairs={{0,1},{1,0},{2,3},{3,2},{4,5},{5,4},{6,7},{7,6},{8,9},{9,8},{10,11... | collective-permute-start | bytes 786440 | tf_op jit(solution)/shard_map/ppermute | solution.py:77
  20.3 22.7 %collective-permute-start.17 = (bf16[3,4,128,128]{3,2,1,0:T(8,128)(2,1)S(1)}, bf16[3,4,128,128]{3,2,1,0:T(8,128)(2,1)S(1)}, u32[]{:S(2)}, u32[]{:S(2)}) collective-permute-start(bf16[3,4,128,128]{3,2,1,0:T(8,128)(2,1)S(1)} %get-tuple-element.45.rest_1_), channel_id=1, source_target_pairs={{0,4},{4,0},{8,12},{12,8},{16,20},{20,16},{24,28},{28,24},{1,5},{5... | collective-permute-start | bytes 1179656 | tf_op jit(solution)/shard_map/ppermute | solution.py:77
  32.7 10.6 %collective-permute-start.14 = (bf16[3,4,128,128]{3,2,1,0:T(8,128)(2,1)S(1)}, bf16[3,4,128,128]{3,2,1,0:T(8,128)(2,1)S(1)}, u32[]{:S(2)}, u32[]{:S(2)}) collective-permute-start(bf16[3,4,128,128]{3,2,1,0:T(8,128)(2,1)S(1)} %get-tuple-element.45.rest_1_), channel_id=1, source_target_pairs={{0,2},{1,3},{2,0},{3,1},{4,6},{5,7},{6,4},{7,5},{8,10},{9,11},{10,... | collective-permute-start | bytes 1179656 | tf_op jit(solution)/shard_map/ppermute | solution.py:77
  34.6 14.8 %collective-permute-start.18 = (bf16[3,4,128,128]{3,2,1,0:T(8,128)(2,1)S(1)}, bf16[3,4,128,128]{3,2,1,0:T(8,128)(2,1)S(1)}, u32[]{:S(2)}, u32[]{:S(2)}) collective-permute-start(bf16[3,4,128,128]{3,2,1,0:T(8,128)(2,1)S(1)} %get-tuple-element.44.rest_0_), channel_id=1, source_target_pairs={{0,4},{4,0},{8,12},{12,8},{16,20},{20,16},{24,28},{28,24},{1,5},{5... | collective-permute-start | bytes 1179656 | tf_op jit(solution)/shard_map/ppermute | solution.py:77
  35.1 14.8 %collective-permute-start.11 = (bf16[3,4,128,128]{3,2,1,0:T(8,128)(2,1)S(1)}, bf16[3,4,128,128]{3,2,1,0:T(8,128)(2,1)S(1)}, u32[]{:S(2)}, u32[]{:S(2)}) collective-permute-start(bf16[3,4,128,128]{3,2,1,0:T(8,128)(2,1)S(1)} %get-tuple-element.44.rest_0_), channel_id=1, source_target_pairs={{0,1},{1,0},{2,3},{3,2},{4,5},{5,4},{6,7},{7,6},{8,9},{9,8},{10,11... | collective-permute-start | bytes 1179656 | tf_op jit(solution)/shard_map/ppermute | solution.py:77
  35.1 15.3 %collective-permute-start.12 = (bf16[3,4,128,128]{3,2,1,0:T(8,128)(2,1)S(1)}, bf16[3,4,128,128]{3,2,1,0:T(8,128)(2,1)S(1)}, u32[]{:S(2)}, u32[]{:S(2)}) collective-permute-start(bf16[3,4,128,128]{3,2,1,0:T(8,128)(2,1)S(1)} %get-tuple-element.45.rest_1_), channel_id=1, source_target_pairs={{0,1},{1,0},{2,3},{3,2},{4,5},{5,4},{6,7},{7,6},{8,9},{9,8},{10,11... | collective-permute-start | bytes 1179656 | tf_op jit(solution)/shard_map/ppermute | solution.py:77
  43.0 7.4 %collective-permute-start.6 = (bf16[2,4,128,128]{3,2,1,0:T(8,128)(2,1)S(1)}, bf16[2,4,128,128]{3,2,1,0:T(8,128)(2,1)S(1)}, u32[]{:S(2)}, u32[]{:S(2)}) collective-permute-start(bf16[2,4,128,128]{3,2,1,0:T(8,128)(2,1)S(1)} %collective-permute-done.5.rest_2_), channel_id=1, source_target_pairs={{0,1},{1,0},{2,3},{3,2},{4,5},{5,4},{6,7},{7,6},{8,9},{9,8},{10,11... | collective-permute-start | bytes 786440 | tf_op jit(solution)/shard_map/ppermute | solution.py:77
  43.3 9.2 %collective-permute-start.15 = (bf16[3,4,128,128]{3,2,1,0:T(8,128)(2,1)S(1)}, bf16[3,4,128,128]{3,2,1,0:T(8,128)(2,1)S(1)}, u32[]{:S(2)}, u32[]{:S(2)}) collective-permute-start(bf16[3,4,128,128]{3,2,1,0:T(8,128)(2,1)S(1)} %collective-permute-done.13.rest_4_), channel_id=1, source_target_pairs={{0,1},{1,0},{2,3},{3,2},{4,5},{5,4},{6,7},{7,6},{8,9},{9,8},{10,11... | collective-permute-start | bytes 1179656 | tf_op jit(solution)/shard_map/ppermute | solution.py:77
  49.4 9.1 %collective-permute-start.21 = (bf16[3,4,128,128]{3,2,1,0:T(8,128)(2,1)S(1)}, bf16[3,4,128,128]{3,2,1,0:T(8,128)(2,1)S(1)}, u32[]{:S(2)}, u32[]{:S(2)}) collective-permute-start(bf16[3,4,128,128]{3,2,1,0:T(8,128)(2,1)S(1)} %collective-permute-done.17.rest_8_), channel_id=1, source_target_pairs={{0,2},{1,3},{2,0},{3,1},{4,6},{5,7},{6,4},{7,5},{8,10},{9,11},{10,... | collective-permute-start | bytes 1179656 | tf_op jit(solution)/shard_map/ppermute | solution.py:77
  49.9 8.8 %collective-permute-start.22 = (bf16[3,4,128,128]{3,2,1,0:T(8,128)(2,1)S(1)}, bf16[3,4,128,128]{3,2,1,0:T(8,128)(2,1)S(1)}, u32[]{:S(2)}, u32[]{:S(2)}) collective-permute-start(bf16[3,4,128,128]{3,2,1,0:T(8,128)(2,1)S(1)} %collective-permute-done.13.rest_4_), channel_id=1, source_target_pairs={{0,4},{4,0},{8,12},{12,8},{16,20},{20,16},{24,28},{28,24},{1,5},{5... | collective-permute-start | bytes 1179656 | tf_op jit(solution)/shard_map/ppermute | solution.py:77
  50.4 1.5 %collective-permute-start.10 = (bf16[2,4,128,128]{3,2,1,0:T(8,128)(2,1)S(1)}, bf16[2,4,128,128]{3,2,1,0:T(8,128)(2,1)S(1)}, u32[]{:S(2)}, u32[]{:S(2)}) collective-permute-start(bf16[2,4,128,128]{3,2,1,0:T(8,128)(2,1)S(1)} %collective-permute-done.9.rest_6_), channel_id=1, source_target_pairs={{0,1},{1,0},{2,3},{3,2},{4,5},{5,4},{6,7},{7,6},{8,9},{9,8},{10,11... | collective-permute-start | bytes 786440 | tf_op jit(solution)/shard_map/ppermute | solution.py:77
  50.5 1.9 %collective-permute-start.8 = (bf16[2,4,128,128]{3,2,1,0:T(8,128)(2,1)S(1)}, bf16[2,4,128,128]{3,2,1,0:T(8,128)(2,1)S(1)}, u32[]{:S(2)}, u32[]{:S(2)}) collective-permute-start(bf16[2,4,128,128]{3,2,1,0:T(8,128)(2,1)S(1)} %collective-permute-done.7.rest_4_), channel_id=1, source_target_pairs={{0,1},{1,0},{2,3},{3,2},{4,5},{5,4},{6,7},{7,6},{8,9},{9,8},{10,11... | collective-permute-start | bytes 786440 | tf_op jit(solution)/shard_map/ppermute | solution.py:77
  52.0 7.5 %collective-permute-start.19 = (bf16[3,4,128,128]{3,2,1,0:T(8,128)(2,1)S(1)}, bf16[3,4,128,128]{3,2,1,0:T(8,128)(2,1)S(1)}, u32[]{:S(2)}, u32[]{:S(2)}) collective-permute-start(bf16[3,4,128,128]{3,2,1,0:T(8,128)(2,1)S(1)} %collective-permute-done.17.rest_8_), channel_id=1, source_target_pairs={{0,1},{1,0},{2,3},{3,2},{4,5},{5,4},{6,7},{7,6},{8,9},{9,8},{10,11... | collective-permute-start | bytes 1179656 | tf_op jit(solution)/shard_map/ppermute | solution.py:77
  52.4 7.2 %collective-permute-start.16 = (bf16[3,4,128,128]{3,2,1,0:T(8,128)(2,1)S(1)}, bf16[3,4,128,128]{3,2,1,0:T(8,128)(2,1)S(1)}, u32[]{:S(2)}, u32[]{:S(2)}) collective-permute-start(bf16[3,4,128,128]{3,2,1,0:T(8,128)(2,1)S(1)} %collective-permute-done.14.rest_5_), channel_id=1, source_target_pairs={{0,1},{1,0},{2,3},{3,2},{4,5},{5,4},{6,7},{7,6},{8,9},{9,8},{10,11... | collective-permute-start | bytes 1179656 | tf_op jit(solution)/shard_map/ppermute | solution.py:77
  52.5 7.0 %collective-permute-start.20 = (bf16[3,4,128,128]{3,2,1,0:T(8,128)(2,1)S(1)}, bf16[3,4,128,128]{3,2,1,0:T(8,128)(2,1)S(1)}, u32[]{:S(2)}, u32[]{:S(2)}) collective-permute-start(bf16[3,4,128,128]{3,2,1,0:T(8,128)(2,1)S(1)} %collective-permute-done.18.rest_9_), channel_id=1, source_target_pairs={{0,1},{1,0},{2,3},{3,2},{4,5},{5,4},{6,7},{7,6},{8,9},{9,8},{10,11... | collective-permute-start | bytes 1179656 | tf_op jit(solution)/shard_map/ppermute | solution.py:77
  58.4 2.6 %collective-permute-start.23 = (bf16[3,4,128,128]{3,2,1,0:T(8,128)(2,1)S(1)}, bf16[3,4,128,128]{3,2,1,0:T(8,128)(2,1)S(1)}, u32[]{:S(2)}, u32[]{:S(2)}) collective-permute-start(bf16[3,4,128,128]{3,2,1,0:T(8,128)(2,1)S(1)} %collective-permute-done.21.rest_3_.rest_12_), channel_id=1, source_target_pairs={{0,1},{1,0},{2,3},{3,2},{4,5},{5,4},{6,7},{7,6},{8,9},{9,8},{10,11... | collective-permute-start | bytes 1179656 | tf_op jit(solution)/shard_map/ppermute | solution.py:77
  58.7 2.4 %collective-permute-start.24 = (bf16[3,4,128,128]{3,2,1,0:T(8,128)(2,1)S(1)}, bf16[3,4,128,128]{3,2,1,0:T(8,128)(2,1)S(1)}, u32[]{:S(2)}, u32[]{:S(2)}) collective-permute-start(bf16[3,4,128,128]{3,2,1,0:T(8,128)(2,1)S(1)} %collective-permute-done.22.rest_4_.rest_13_), channel_id=1, source_target_pairs={{0,1},{1,0},{2,3},{3,2},{4,5},{5,4},{6,7},{7,6},{8,9},{9,8},{10,11... | collective-permute-start | bytes 1179656 | tf_op jit(solution)/shard_map/ppermute | solution.py:77
  61.9 7.4 %collective-permute-start.27 = (s32[32,768]{1,0:T(8,128)S(1)}, s32[32,768]{1,0:T(8,128)S(1)}, u32[]{:S(2)}, u32[]{:S(2)}) collective-permute-start(s32[32,768]{1,0:T(8,128)S(1)} %pad_add_fusion.5), channel_id=1, source_target_pairs={{0,24},{4,28},{8,16},{12,20},{16,8},{20,12},{24,0},{28,4},{1,25},{... | collective-permute-start | bytes 294920 | tf_op jit(solution)/shard_map/ppermute | solution.py:77
  65.9 8.3 %collective-permute-start.26 = (s32[32,768]{1,0:T(8,128)S(1)}, s32[32,768]{1,0:T(8,128)S(1)}, u32[]{:S(2)}, u32[]{:S(2)}) collective-permute-start(s32[32,768]{1,0:T(8,128)S(1)} %pad_add_fusion.4), channel_id=1, source_target_pairs={{0,16},{4,20},{8,24},{12,28},{16,0},{20,4},{24,8},{28,12},{1,17},{... | collective-permute-start | bytes 294920 | tf_op jit(solution)/shard_map/ppermute | solution.py:77
  66.0 8.2 %collective-permute-start.25 = (s32[32,768]{1,0:T(8,128)S(1)}, s32[32,768]{1,0:T(8,128)S(1)}, u32[]{:S(2)}, u32[]{:S(2)}) collective-permute-start(s32[32,768]{1,0:T(8,128)S(1)} %pad_add_fusion.3), channel_id=1, source_target_pairs={{0,8},{4,12},{8,0},{12,4},{16,24},{20,28},{24,16},{28,20},{1,9},{5... | collective-permute-start | bytes 294920 | tf_op jit(solution)/shard_map/ppermute | solution.py:77
  76.1 8.0 %collective-permute-start.29 = (s32[32,768]{1,0:T(8,128)S(1)}, s32[32,768]{1,0:T(8,128)S(1)}, u32[]{:S(2)}, u32[]{:S(2)}) collective-permute-start(s32[32,768]{1,0:T(8,128)S(1)} %shard_map.57), channel_id=1, source_target_pairs={{0,16},{4,20},{8,24},{12,28},{16,0},{20,4},{24,8},{28,12},{1,17},{... | collective-permute-start | bytes 294920 | tf_op jit(solution)/shard_map/ppermute | solution.py:77
  77.1 8.2 %collective-permute-start.28 = (s32[32,768]{1,0:T(8,128)S(1)}, s32[32,768]{1,0:T(8,128)S(1)}, u32[]{:S(2)}, u32[]{:S(2)}) collective-permute-start(s32[32,768]{1,0:T(8,128)S(1)} %shard_map.56), channel_id=1, source_target_pairs={{0,8},{4,12},{8,0},{12,4},{16,24},{20,28},{24,16},{28,20},{1,9},{5... | collective-permute-start | bytes 294920 | tf_op jit(solution)/shard_map/ppermute | solution.py:77
  80.1 6.4 %collective-permute-start.30 = (s32[32,768]{1,0:T(8,128)S(1)}, s32[32,768]{1,0:T(8,128)S(1)}, u32[]{:S(2)}, u32[]{:S(2)}) collective-permute-start(s32[32,768]{1,0:T(8,128)S(1)} %get-tuple-element.56), channel_id=1, source_target_pairs={{0,24},{4,28},{8,16},{12,20},{16,8},{20,12},{24,0},{28,4},{1,25},{... | collective-permute-start | bytes 294920 | tf_op jit(solution)/shard_map/ppermute | solution.py:77
  88.4 5.4 %collective-permute-start.31 = (s32[32,768]{1,0:T(8,128)S(1)}, s32[32,768]{1,0:T(8,128)S(1)}, u32[]{:S(2)}, u32[]{:S(2)}) collective-permute-start(s32[32,768]{1,0:T(8,128)S(1)} %shard_map.59), channel_id=1, source_target_pairs={{0,8},{4,12},{8,0},{12,4},{16,24},{20,28},{24,16},{28,20},{1,9},{5... | collective-permute-start | bytes 294920 | tf_op jit(solution)/shard_map/ppermute | solution.py:77
  90.8 9.7 %collective-permute-start.32 = (s32[32,768]{1,0:T(8,128)S(1)}, s32[32,768]{1,0:T(8,128)S(1)}, u32[]{:S(2)}, u32[]{:S(2)}) collective-permute-start(s32[32,768]{1,0:T(8,128)S(1)} %shard_map.60), channel_id=1, source_target_pairs={{0,16},{4,20},{8,24},{12,28},{16,0},{20,4},{24,8},{28,12},{1,17},{... | collective-permute-start | bytes 294920 | tf_op jit(solution)/shard_map/ppermute | solution.py:77
  91.4 9.1 %collective-permute-start.33 = (s32[32,768]{1,0:T(8,128)S(1)}, s32[32,768]{1,0:T(8,128)S(1)}, u32[]{:S(2)}, u32[]{:S(2)}) collective-permute-start(s32[32,768]{1,0:T(8,128)S(1)} %get-tuple-element.58), channel_id=1, source_target_pairs={{0,24},{4,28},{8,16},{12,20},{16,8},{20,12},{24,0},{28,4},{1,25},{... | collective-permute-start | bytes 294920 | tf_op jit(solution)/shard_map/ppermute | solution.py:77
  100.6 2.9 %copy-start.2 = (f32[128,256]{1,0:T(8,128)S(1)}, f32[128,256]{1,0:T(8,128)}, u32[]{:S(2)}) copy-start(f32[128,256]{1,0:T(8,128)} %paths_in.1) | copy-start | bytes 393220
  101.7 6.9 %collective-permute-start.34 = (bf16[32,1024]{1,0:T(8,128)(2,1)S(1)}, bf16[32,1024]{1,0:T(8,128)(2,1)S(1)}, u32[]{:S(2)}, u32[]{:S(2)}) collective-permute-start(bf16[32,1024]{1,0:T(8,128)(2,1)S(1)} %fusion.8), channel_id=1, source_target_pairs={{0,24},{4,28},{8,16},{12,20},{16,8},{20,12},{24,0},{28,4},{1,25},{... | collective-permute-start | bytes 196616 | tf_op jit(solution)/shard_map/ppermute | solution.py:77
  103.4 5.7 %collective-permute-start.35 = (bf16[32,1024]{1,0:T(8,128)(2,1)S(1)}, bf16[32,1024]{1,0:T(8,128)(2,1)S(1)}, u32[]{:S(2)}, u32[]{:S(2)}) collective-permute-start(bf16[32,1024]{1,0:T(8,128)(2,1)S(1)} %fusion.8), channel_id=1, source_target_pairs={{0,8},{4,12},{8,0},{12,4},{16,24},{20,28},{24,16},{28,20},{1,9},{5... | collective-permute-start | bytes 196616 | tf_op jit(solution)/shard_map/ppermute | solution.py:77
  104.5 6.5 %collective-permute-start.36 = (bf16[32,1024]{1,0:T(8,128)(2,1)S(1)}, bf16[32,1024]{1,0:T(8,128)(2,1)S(1)}, u32[]{:S(2)}, u32[]{:S(2)}) collective-permute-start(bf16[32,1024]{1,0:T(8,128)(2,1)S(1)} %fusion.8), channel_id=1, source_target_pairs={{0,16},{4,20},{8,24},{12,28},{16,0},{20,4},{24,8},{28,12},{1,17},{... | collective-permute-start | bytes 196616 | tf_op jit(solution)/shard_map/ppermute | solution.py:77
  111.4 6.2 %collective-permute-start.37 = (bf16[32,1024]{1,0:T(8,128)(2,1)S(1)}, bf16[32,1024]{1,0:T(8,128)(2,1)S(1)}, u32[]{:S(2)}, u32[]{:S(2)}) collective-permute-start(bf16[32,1024]{1,0:T(8,128)(2,1)S(1)} %get-tuple-element.60), channel_id=1, source_target_pairs={{0,24},{4,28},{8,16},{12,20},{16,8},{20,12},{24,0},{28,4},{1,25},{... | collective-permute-start | bytes 196616 | tf_op jit(solution)/shard_map/ppermute | solution.py:77
  113.2 5.8 %collective-permute-start.38 = (bf16[32,1024]{1,0:T(8,128)(2,1)S(1)}, bf16[32,1024]{1,0:T(8,128)(2,1)S(1)}, u32[]{:S(2)}, u32[]{:S(2)}) collective-permute-start(bf16[32,1024]{1,0:T(8,128)(2,1)S(1)} %get-tuple-element.60), channel_id=1, source_target_pairs={{0,8},{4,12},{8,0},{12,4},{16,24},{20,28},{24,16},{28,20},{1,9},{5... | collective-permute-start | bytes 196616 | tf_op jit(solution)/shard_map/ppermute | solution.py:77
  113.3 6.7 %collective-permute-start.39 = (bf16[32,1024]{1,0:T(8,128)(2,1)S(1)}, bf16[32,1024]{1,0:T(8,128)(2,1)S(1)}, u32[]{:S(2)}, u32[]{:S(2)}) collective-permute-start(bf16[32,1024]{1,0:T(8,128)(2,1)S(1)} %get-tuple-element.60), channel_id=1, source_target_pairs={{0,16},{4,20},{8,24},{12,28},{16,0},{20,4},{24,8},{28,12},{1,17},{... | collective-permute-start | bytes 196616 | tf_op jit(solution)/shard_map/ppermute | solution.py:77
  120.5 6.2 %collective-permute-start.40 = (bf16[32,1024]{1,0:T(8,128)(2,1)S(1)}, bf16[32,1024]{1,0:T(8,128)(2,1)S(1)}, u32[]{:S(2)}, u32[]{:S(2)}) collective-permute-start(bf16[32,1024]{1,0:T(8,128)(2,1)S(1)} %get-tuple-element.63), channel_id=1, source_target_pairs={{0,24},{4,28},{8,16},{12,20},{16,8},{20,12},{24,0},{28,4},{1,25},{... | collective-permute-start | bytes 196616 | tf_op jit(solution)/shard_map/ppermute | solution.py:77
  122.4 5.6 %collective-permute-start.41 = (bf16[32,1024]{1,0:T(8,128)(2,1)S(1)}, bf16[32,1024]{1,0:T(8,128)(2,1)S(1)}, u32[]{:S(2)}, u32[]{:S(2)}) collective-permute-start(bf16[32,1024]{1,0:T(8,128)(2,1)S(1)} %get-tuple-element.63), channel_id=1, source_target_pairs={{0,8},{4,12},{8,0},{12,4},{16,24},{20,28},{24,16},{28,20},{1,9},{5... | collective-permute-start | bytes 196616 | tf_op jit(solution)/shard_map/ppermute | solution.py:77
  122.5 6.5 %collective-permute-start.42 = (bf16[32,1024]{1,0:T(8,128)(2,1)S(1)}, bf16[32,1024]{1,0:T(8,128)(2,1)S(1)}, u32[]{:S(2)}, u32[]{:S(2)}) collective-permute-start(bf16[32,1024]{1,0:T(8,128)(2,1)S(1)} %get-tuple-element.63), channel_id=1, source_target_pairs={{0,16},{4,20},{8,24},{12,28},{16,0},{20,4},{24,8},{28,12},{1,17},{... | collective-permute-start | bytes 196616 | tf_op jit(solution)/shard_map/ppermute | solution.py:77
  129.5 1.3 collective-permute-start.43
  130.8 5.0 %collective-permute-start.46 = (f32[2,32,128]{2,1,0:T(8,128)S(1)}, f32[2,32,128]{2,1,0:T(8,128)S(1)}, u32[]{:S(2)}, u32[]{:S(2)}) collective-permute-start(f32[2,32,128]{2,1,0:T(8,128)S(1)} %pad_maximum_fusion.8), channel_id=1, source_target_pairs={{0,6},{1,7},{2,4},{3,5},{4,2},{5,3},{6,0},{7,1},{8,14},{9,15},{10,... | collective-permute-start | bytes 98312 | tf_op jit(solution)/shard_map/ppermute | solution.py:429
  132.7 3.9 %collective-permute-start.45 = (f32[2,32,128]{2,1,0:T(8,128)S(1)}, f32[2,32,128]{2,1,0:T(8,128)S(1)}, u32[]{:S(2)}, u32[]{:S(2)}) collective-permute-start(f32[2,32,128]{2,1,0:T(8,128)S(1)} %pad_maximum_fusion.7), channel_id=1, source_target_pairs={{0,4},{4,0},{8,12},{12,8},{16,20},{20,16},{24,28},{28,24},{1,5},{5... | collective-permute-start | bytes 98312 | tf_op jit(solution)/shard_map/ppermute | solution.py:77
  134.3 3.9 %collective-permute-start.44 = (f32[2,32,128]{2,1,0:T(8,128)S(1)}, f32[2,32,128]{2,1,0:T(8,128)S(1)}, u32[]{:S(2)}, u32[]{:S(2)}) collective-permute-start(f32[2,32,128]{2,1,0:T(8,128)S(1)} %pad_maximum_fusion.6), channel_id=1, source_target_pairs={{0,2},{1,3},{2,0},{3,1},{4,6},{5,7},{6,4},{7,5},{8,10},{9,11},{10,... | collective-permute-start | bytes 98312 | tf_op jit(solution)/shard_map/ppermute | solution.py:77
  (6 other events, 7.8 us)

commit v6 on v5

--- a/solution.py
+++ b/solution.py
@@ -421,9 +421,20 @@
     )(factor, *pieces)
 
 
+def stack_kernel(keep, got, *outs):
+    for at, out in enumerate(outs):
+        out[0] = keep[at]
+        out[1] = got[at]
+
+
+def stacked(keep, got):
+    pair = jax.ShapeDtypeStruct((2, *keep.shape[1:]), keep.dtype)
+    return vmem_call(stack_kernel, [pair] * (GROUP // 2), [keep, got], 0)
+
+
 def traded(keep, send):
     got = swap(send, "col", 1)
-    held = [jnp.stack([keep[at], got[at]]) for at in range(GROUP // 2)]
+    held = stacked(keep, got)
     from_y = swap(held[2], "row", 1)
     from_x = swap(held[1], "col", 2)
     from_d = lax.ppermute(held[3], ("row", "col"), diagonal())

time: 139 us -> 136 us (0.978)
  local copies, waits for them, and re-layouts: 5.04 us -> 2.3 us
    unnamed x14 -> x10, local copies, waits for them, and re-layouts: 5 us -> 2.28 us
    ppermute x2, starting transfers between devices: 3.34 us -> 1.46 us  [traded(): from_d = lax.ppermute(held[3], ('row', 'col'), diagonal())]
    pallas_call x9 -> x11, Pallas kernels: 6.87 us -> 6.88 us  [vmem_call(): pl.pallas_call(kernel, out_shape=outs, in_specs=[IN_VMEM] * len(args), ou...]
  transfers between devices with their start and end apart: 47 -> 47, of which waited for: 25 -> 23; matrix products, arithmetic and copies ran while one was open for 4% -> 5% of each run, Pallas kernels for 4% -> 4%
where the time goes in v6:
time: 136 us
  waiting for transfers between devices  65.1 us (48%)
  starting transfers between devices  47.4 us (35%)
  Pallas kernels  12.8 us (9%)
  matrix products  6.88 us (5%)
  local copies, waits for them, and re-layouts  2.3 us (2%)
    ppermute x44, waiting for transfers between devices, swap(): return lax.ppermute(value, axis, partner(axis, bit))  52.6 us
    ppermute x44, starting transfers between devices, swap(): return lax.ppermute(value, axis, partner(axis, bit))  42.9 us
    ppermute x1, waiting for transfers between devices, split_shards(): same_d = lax.ppermute(flipped, ('row', 'col'), diagonal())  10.1 us
    pallas_call x11, Pallas kernels, vmem_call(): pl.pallas_call(kernel, out_shape=outs, in_specs=[IN_VMEM] * len(args), ou...  6.88 us
    ppermute x1, starting transfers between devices, split_shards(): same_d = lax.ppermute(flipped, ('row', 'col'), diagonal())  3.05 us
    dot_general x6, matrix products, split_shards(): part = part + jnp.dot(got[k], whole[k], preferred_element_type=jnp.float32)  2.81 us
  transfers between devices with their start and end apart: 47, of which 23 were waited for; matrix products, arithmetic and copies ran while one was open for 5% of the time, Pallas kernels for 4%

profile of v6, /device:TPU:0, one launch (start us, length us, event | category | flops | bytes accessed | tf_op | source)
XLA Modules:
  0.0 135.6 jit_solution(15243461512670128747)
XLA Ops:
  0.0 1.6 %copy-done = s32[1,1,8,4,128,128]{5,4,3,2,1,0:T(8,128)S(1)} copy-done((s32[1,1,8,4,128,128]{5,4,3,2,1,0:T(8,128)S(1)}, s32[1,1,8,4,128,128]{5,4,3,2,1,0:T(8,128)}, u32[]{:S(2)}) %copy-start) | copy-done | bytes 2097176
  3.0 3.0 %collective-permute-start.5 = (bf16[2,4,128,128]{3,2,1,0:T(8,128)(2,1)S(1)}, bf16[2,4,128,128]{3,2,1,0:T(8,128)(2,1)S(1)}, u32[]{:S(2)}, u32[]{:S(2)}) collective-permute-start(bf16[2,4,128,128]{3,2,1,0:T(8,128)(2,1)S(1)} %get-tuple-element.54.rest_0_), channel_id=1, source_target_pairs={{0,2},{1,3},{2,0},{3,1},{4,6},{5,7},{6,4},{7,5},{8,10},{9,11},{10,... | collective-permute-start | bytes 786440 | tf_op jit(solution)/shard_map/ppermute | solution.py:77
  6.3 1.2 collective-permute-done.got
  7.8 1.8 %collective-permute-start.2 = (f32[2,32,128]{2,1,0:T(8,128)S(1)}, f32[2,32,128]{2,1,0:T(8,128)S(1)}, u32[]{:S(2)}, u32[]{:S(2)}) collective-permute-start(f32[2,32,128]{2,1,0:T(8,128)S(1)} %get-tuple-element.50), channel_id=1, source_target_pairs={{0,4},{4,0},{8,12},{12,8},{16,20},{20,16},{24,28},{28,24},{1,5},{5... | collective-permute-start | bytes 98312 | tf_op jit(solution)/shard_map/ppermute | solution.py:77
  9.6 1.4 %collective-permute-start.3 = (f32[2,32,128]{2,1,0:T(8,128)S(1)}, f32[2,32,128]{2,1,0:T(8,128)S(1)}, u32[]{:S(2)}, u32[]{:S(2)}) collective-permute-start(f32[2,32,128]{2,1,0:T(8,128)S(1)} %get-tuple-element.51), channel_id=1, source_target_pairs={{0,6},{1,7},{2,4},{3,5},{4,2},{5,3},{6,0},{7,1},{8,14},{9,15},{10,... | collective-permute-start | bytes 98312 | tf_op jit(solution)/shard_map/ppermute | solution.py:440
  11.3 2.5 %collective-permute-done.1.rest_1_ = f32[2,32,128]{2,1,0:T(8,128)S(1)} collective-permute-done((f32[2,32,128]{2,1,0:T(8,128)S(1)}, f32[2,32,128]{2,1,0:T(8,128)S(1)}, u32[]{:S(2)}, u32[]{:S(2)}) %collective-permute-start.1) | collective-permute-done | bytes 32800 | tf_op jit(solution)/shard_map/ppermute | solution.py:77
  13.8 3.1 %collective-permute-start.9 = (bf16[2,4,128,128]{3,2,1,0:T(8,128)(2,1)S(1)}, bf16[2,4,128,128]{3,2,1,0:T(8,128)(2,1)S(1)}, u32[]{:S(2)}, u32[]{:S(2)}) collective-permute-start(bf16[2,4,128,128]{3,2,1,0:T(8,128)(2,1)S(1)} %get-tuple-element.55), channel_id=1, source_target_pairs={{0,6},{1,7},{2,4},{3,5},{4,2},{5,3},{6,0},{7,1},{8,14},{9,15},{10,... | collective-permute-start | bytes 786440 | tf_op jit(solution)/shard_map/ppermute | solution.py:465
  17.4 1.6 %collective-permute-start.17 = (bf16[3,4,128,128]{3,2,1,0:T(8,128)(2,1)S(1)}, bf16[3,4,128,128]{3,2,1,0:T(8,128)(2,1)S(1)}, u32[]{:S(2)}, u32[]{:S(2)}) collective-permute-start(bf16[3,4,128,128]{3,2,1,0:T(8,128)(2,1)S(1)} %get-tuple-element.57.rest_1_), channel_id=1, source_target_pairs={{0,4},{4,0},{8,12},{12,8},{16,20},{20,16},{24,28},{28,24},{1,5},{5... | collective-permute-start | bytes 1179656 | tf_op jit(solution)/shard_map/ppermute | solution.py:77
  19.0 10.1 %collective-permute-done.9.rest_6_ = bf16[2,4,128,128]{3,2,1,0:T(8,128)(2,1)S(1)} collective-permute-done((bf16[2,4,128,128]{3,2,1,0:T(8,128)(2,1)S(1)}, bf16[2,4,128,128]{3,2,1,0:T(8,128)(2,1)S(1)}, u32[]{:S(2)}, u32[]{:S(2)}) %collective-permute-start.9) | collective-permute-done | bytes 262176 | tf_op jit(solution)/shard_map/ppermute | solution.py:465
  29.1 1.5 %collective-permute-start.14 = (bf16[3,4,128,128]{3,2,1,0:T(8,128)(2,1)S(1)}, bf16[3,4,128,128]{3,2,1,0:T(8,128)(2,1)S(1)}, u32[]{:S(2)}, u32[]{:S(2)}) collective-permute-start(bf16[3,4,128,128]{3,2,1,0:T(8,128)(2,1)S(1)} %get-tuple-element.57.rest_1_), channel_id=1, source_target_pairs={{0,2},{1,3},{2,0},{3,1},{4,6},{5,7},{6,4},{7,5},{8,10},{9,11},{10,... | collective-permute-start | bytes 1179656 | tf_op jit(solution)/shard_map/ppermute | solution.py:77
  30.6 1.0 collective-permute-done.7.rest_4_
  32.2 7.9 %collective-permute-done.17.rest_8_ = bf16[3,4,128,128]{3,2,1,0:T(8,128)(2,1)S(1)} collective-permute-done((bf16[3,4,128,128]{3,2,1,0:T(8,128)(2,1)S(1)}, bf16[3,4,128,128]{3,2,1,0:T(8,128)(2,1)S(1)}, u32[]{:S(2)}, u32[]{:S(2)}) %collective-permute-start.17) | collective-permute-done | bytes 393248 | tf_op jit(solution)/shard_map/ppermute | solution.py:77
  40.6 5.2 %collective-permute-done.18.rest_9_ = bf16[3,4,128,128]{3,2,1,0:T(8,128)(2,1)S(1)} collective-permute-done((bf16[3,4,128,128]{3,2,1,0:T(8,128)(2,1)S(1)}, bf16[3,4,128,128]{3,2,1,0:T(8,128)(2,1)S(1)}, u32[]{:S(2)}, u32[]{:S(2)}) %collective-permute-start.18) | collective-permute-done | bytes 393248 | tf_op jit(solution)/shard_map/ppermute | solution.py:77
  46.8 1.0 collective-permute-done.10.rest_7_
  48.7 5.4 %collective-permute-done.21.rest_3_.rest_12_ = bf16[3,4,128,128]{3,2,1,0:T(8,128)(2,1)S(1)} collective-permute-done((bf16[3,4,128,128]{3,2,1,0:T(8,128)(2,1)S(1)}, bf16[3,4,128,128]{3,2,1,0:T(8,128)(2,1)S(1)}, u32[]{:S(2)}, u32[]{:S(2)}) %collective-permute-start.21) | collective-permute-done | bytes 393248 | tf_op jit(solution)/shard_map/ppermute | solution.py:77
  55.2 1.5 %first.2 = (f32[32,1024]{1,0:T(8,128)S(1)}, f32[32,1024]{1,0:T(8,128)S(1)}, f32[32,1024]{1,0:T(8,128)S(1)}) custom-call(bf16[32,1024]{1,0:T(8,128)(2,1)S(1)} %get-tuple-element.53.front, bf16[3,4,128,128]{3,2,1,0:T(8,128)(2,1)S(1)} %get-tuple-element.56.rest_0_, bf16[3,4,128,128]{3,2,1,0:T(8,128)(2,1)S(1)} %get-tuple-element.57.rest_1_, ...), custom_call_target="tpu_custom_call" | custom-call | flops 150994944 | bytes 4718592 | tf_op jit(solution)/shard_map/first/pallas_call | solution.py:251
  57.5 3.7 %collective-permute-start.27 = (s32[32,768]{1,0:T(8,128)S(1)}, s32[32,768]{1,0:T(8,128)S(1)}, u32[]{:S(2)}, u32[]{:S(2)}) collective-permute-start(s32[32,768]{1,0:T(8,128)S(1)} %pad_add_fusion.5), channel_id=1, source_target_pairs={{0,24},{4,28},{8,16},{12,20},{16,8},{20,12},{24,0},{28,4},{1,25},{... | collective-permute-start | bytes 294920 | tf_op jit(solution)/shard_map/ppermute | solution.py:77
  61.7 0.8 collective-permute-start.25
  63.3 1.7 %assemble.3 = (bf16[1024,1024]{1,0:T(8,128)(2,1)S(1)}, bf16[1024,1024]{1,0:T(8,128)(2,1)S(1)}, bf16[1024,1024]{1,0:T(8,128)(2,1)S(1)}) custom-call(bf16[3,4,128,128]{3,2,1,0:T(8,128)(2,1)S(1)} %get-tuple-element.56.rest_0_, bf16[3,4,128,128]{3,2,1,0:T(8,128)(2,1)S(1)} %get-tuple-element.57.rest_1_, ...), custom_call_target="tpu_custom_call" | custom-call | bytes 12582912 | tf_op jit(solution)/shard_map/assemble/pallas_call | solution.py:282
  64.9 4.9 %collective-permute-done.26.rest_1_ = s32[32,768]{1,0:T(8,128)S(1)} collective-permute-done((s32[32,768]{1,0:T(8,128)S(1)}, s32[32,768]{1,0:T(8,128)S(1)}, u32[]{:S(2)}, u32[]{:S(2)}) %collective-permute-start.26) | collective-permute-done | bytes 98336 | tf_op jit(solution)/shard_map/ppermute | solution.py:77
  69.8 1.0 shard_map.56
  70.8 0.8 shard_map.58
  72.7 3.0 %collective-permute-start.28 = (s32[32,768]{1,0:T(8,128)S(1)}, s32[32,768]{1,0:T(8,128)S(1)}, u32[]{:S(2)}, u32[]{:S(2)}) collective-permute-start(s32[32,768]{1,0:T(8,128)S(1)} %shard_map.57), channel_id=1, source_target_pairs={{0,8},{4,12},{8,0},{12,4},{16,24},{20,28},{24,16},{28,20},{1,9},{5... | collective-permute-start | bytes 294920 | tf_op jit(solution)/shard_map/ppermute | solution.py:77
  75.7 1.3 collective-permute-start.30
  77.7 1.9 %collective-permute-done.29.rest_1_ = s32[32,768]{1,0:T(8,128)S(1)} collective-permute-done((s32[32,768]{1,0:T(8,128)S(1)}, s32[32,768]{1,0:T(8,128)S(1)}, u32[]{:S(2)}, u32[]{:S(2)}) %collective-permute-start.29) | collective-permute-done | bytes 98336 | tf_op jit(solution)/shard_map/ppermute | solution.py:77
  79.6 1.2 collective-permute-done.28.rest_0_
  80.8 1.3 collective-permute-done.30.rest_2_
  82.1 1.0 shard_map.59
  84.0 1.5 %collective-permute-start.31 = (s32[32,768]{1,0:T(8,128)S(1)}, s32[32,768]{1,0:T(8,128)S(1)}, u32[]{:S(2)}, u32[]{:S(2)}) collective-permute-start(s32[32,768]{1,0:T(8,128)S(1)} %shard_map.60), channel_id=1, source_target_pairs={{0,8},{4,12},{8,0},{12,4},{16,24},{20,28},{24,16},{28,20},{1,9},{5... | collective-permute-start | bytes 294920 | tf_op jit(solution)/shard_map/ppermute | solution.py:77
  87.0 2.3 %collective-permute-start.33 = (s32[32,768]{1,0:T(8,128)S(1)}, s32[32,768]{1,0:T(8,128)S(1)}, u32[]{:S(2)}, u32[]{:S(2)}) collective-permute-start(s32[32,768]{1,0:T(8,128)S(1)} %get-tuple-element.70), channel_id=1, source_target_pairs={{0,24},{4,28},{8,16},{12,20},{16,8},{20,12},{24,0},{28,4},{1,25},{... | collective-permute-start | bytes 294920 | tf_op jit(solution)/shard_map/ppermute | solution.py:77
  89.3 6.7 %collective-permute-done.32 = s32[32,768]{1,0:T(8,128)S(1)} collective-permute-done((s32[32,768]{1,0:T(8,128)S(1)}, s32[32,768]{1,0:T(8,128)S(1)}, u32[]{:S(2)}, u32[]{:S(2)}) %collective-permute-start.32) | collective-permute-done | bytes 98336 | tf_op jit(solution)/shard_map/ppermute | solution.py:77
  96.1 1.2 fusion.8
  97.3 1.7 %collective-permute-start.34 = (bf16[32,1024]{1,0:T(8,128)(2,1)S(1)}, bf16[32,1024]{1,0:T(8,128)(2,1)S(1)}, u32[]{:S(2)}, u32[]{:S(2)}) collective-permute-start(bf16[32,1024]{1,0:T(8,128)(2,1)S(1)} %fusion.8), channel_id=1, source_target_pairs={{0,24},{4,28},{8,16},{12,20},{16,8},{20,12},{24,0},{28,4},{1,25},{... | collective-permute-start | bytes 196616 | tf_op jit(solution)/shard_map/ppermute | solution.py:77
  99.1 1.0 collective-permute-start.35
  100.0 1.8 %collective-permute-start.36 = (bf16[32,1024]{1,0:T(8,128)(2,1)S(1)}, bf16[32,1024]{1,0:T(8,128)(2,1)S(1)}, u32[]{:S(2)}, u32[]{:S(2)}) collective-permute-start(bf16[32,1024]{1,0:T(8,128)(2,1)S(1)} %fusion.8), channel_id=1, source_target_pairs={{0,16},{4,20},{8,24},{12,28},{16,0},{20,4},{24,8},{28,12},{1,17},{... | collective-permute-start | bytes 196616 | tf_op jit(solution)/shard_map/ppermute | solution.py:77
  101.8 2.2 %collective-permute-done.34 = bf16[32,1024]{1,0:T(8,128)(2,1)S(1)} collective-permute-done((bf16[32,1024]{1,0:T(8,128)(2,1)S(1)}, bf16[32,1024]{1,0:T(8,128)(2,1)S(1)}, u32[]{:S(2)}, u32[]{:S(2)}) %collective-permute-start.34) | collective-permute-done | bytes 65568 | tf_op jit(solution)/shard_map/ppermute | solution.py:77
  105.5 1.0 collective-permute-done.36.weight
  107.0 1.9 %collective-permute-start.37 = (bf16[32,1024]{1,0:T(8,128)(2,1)S(1)}, bf16[32,1024]{1,0:T(8,128)(2,1)S(1)}, u32[]{:S(2)}, u32[]{:S(2)}) collective-permute-start(bf16[32,1024]{1,0:T(8,128)(2,1)S(1)} %get-tuple-element.72), channel_id=1, source_target_pairs={{0,24},{4,28},{8,16},{12,20},{16,8},{20,12},{24,0},{28,4},{1,25},{... | collective-permute-start | bytes 196616 | tf_op jit(solution)/shard_map/ppermute | solution.py:77
  108.9 2.5 %collective-permute-start.39 = (bf16[32,1024]{1,0:T(8,128)(2,1)S(1)}, bf16[32,1024]{1,0:T(8,128)(2,1)S(1)}, u32[]{:S(2)}, u32[]{:S(2)}) collective-permute-start(bf16[32,1024]{1,0:T(8,128)(2,1)S(1)} %get-tuple-element.72), channel_id=1, source_target_pairs={{0,16},{4,20},{8,24},{12,28},{16,0},{20,4},{24,8},{28,12},{1,17},{... | collective-permute-start | bytes 196616 | tf_op jit(solution)/shard_map/ppermute | solution.py:77
  111.4 2.4 %collective-permute-done.37 = bf16[32,1024]{1,0:T(8,128)(2,1)S(1)} collective-permute-done((bf16[32,1024]{1,0:T(8,128)(2,1)S(1)}, bf16[32,1024]{1,0:T(8,128)(2,1)S(1)}, u32[]{:S(2)}, u32[]{:S(2)}) %collective-permute-start.37) | collective-permute-done | bytes 65568 | tf_op jit(solution)/shard_map/ppermute | solution.py:77
  115.8 1.8 %collective-permute-start.40 = (bf16[32,1024]{1,0:T(8,128)(2,1)S(1)}, bf16[32,1024]{1,0:T(8,128)(2,1)S(1)}, u32[]{:S(2)}, u32[]{:S(2)}) collective-permute-start(bf16[32,1024]{1,0:T(8,128)(2,1)S(1)} %get-tuple-element.75), channel_id=1, source_target_pairs={{0,24},{4,28},{8,16},{12,20},{16,8},{20,12},{24,0},{28,4},{1,25},{... | collective-permute-start | bytes 196616 | tf_op jit(solution)/shard_map/ppermute | solution.py:77
  117.8 2.5 %collective-permute-start.42 = (bf16[32,1024]{1,0:T(8,128)(2,1)S(1)}, bf16[32,1024]{1,0:T(8,128)(2,1)S(1)}, u32[]{:S(2)}, u32[]{:S(2)}) collective-permute-start(bf16[32,1024]{1,0:T(8,128)(2,1)S(1)} %get-tuple-element.75), channel_id=1, source_target_pairs={{0,16},{4,20},{8,24},{12,28},{16,0},{20,4},{24,8},{28,12},{1,17},{... | collective-permute-start | bytes 196616 | tf_op jit(solution)/shard_map/ppermute | solution.py:77
  120.3 2.1 %collective-permute-done.40 = bf16[32,1024]{1,0:T(8,128)(2,1)S(1)} collective-permute-done((bf16[32,1024]{1,0:T(8,128)(2,1)S(1)}, bf16[32,1024]{1,0:T(8,128)(2,1)S(1)}, u32[]{:S(2)}, u32[]{:S(2)}) %collective-permute-start.40) | collective-permute-done | bytes 65568 | tf_op jit(solution)/shard_map/ppermute | solution.py:77
  125.1 1.2 collective-permute-done.43.got
  126.4 2.1 %collective-permute-start.44 = (f32[2,32,128]{2,1,0:T(8,128)S(1)}, f32[2,32,128]{2,1,0:T(8,128)S(1)}, u32[]{:S(2)}, u32[]{:S(2)}) collective-permute-start(f32[2,32,128]{2,1,0:T(8,128)S(1)} %get-tuple-element.80), channel_id=1, source_target_pairs={{0,2},{1,3},{2,0},{3,1},{4,6},{5,7},{6,4},{7,5},{8,10},{9,11},{10,... | collective-permute-start | bytes 98312 | tf_op jit(solution)/shard_map/ppermute | solution.py:77
  128.5 1.5 %collective-permute-start.45 = (f32[2,32,128]{2,1,0:T(8,128)S(1)}, f32[2,32,128]{2,1,0:T(8,128)S(1)}, u32[]{:S(2)}, u32[]{:S(2)}) collective-permute-start(f32[2,32,128]{2,1,0:T(8,128)S(1)} %get-tuple-element.81), channel_id=1, source_target_pairs={{0,4},{4,0},{8,12},{12,8},{16,20},{20,16},{24,28},{28,24},{1,5},{5... | collective-permute-start | bytes 98312 | tf_op jit(solution)/shard_map/ppermute | solution.py:77
  130.4 2.0 %collective-permute-done.45.rest_2_ = f32[2,32,128]{2,1,0:T(8,128)S(1)} collective-permute-done((f32[2,32,128]{2,1,0:T(8,128)S(1)}, f32[2,32,128]{2,1,0:T(8,128)S(1)}, u32[]{:S(2)}, u32[]{:S(2)}) %collective-permute-start.45) | collective-permute-done | bytes 32800 | tf_op jit(solution)/shard_map/ppermute | solution.py:77
  132.4 2.4 %collective-permute-done.46.rest_3_ = f32[2,32,128]{2,1,0:T(8,128)S(1)} collective-permute-done((f32[2,32,128]{2,1,0:T(8,128)S(1)}, f32[2,32,128]{2,1,0:T(8,128)S(1)}, u32[]{:S(2)}, u32[]{:S(2)}) %collective-permute-start.46) | collective-permute-done | bytes 32800 | tf_op jit(solution)/shard_map/ppermute | solution.py:440
  (103 shorter events, 20.8 us)
Async XLA Ops:
  2.3 3.8 %copy-start.3 = (f32[128,256]{1,0:T(8,128)S(1)}, f32[128,256]{1,0:T(8,128)}, u32[]{:S(2)}) copy-start(f32[128,256]{1,0:T(8,128)} %dep_in.1) | copy-start | bytes 393220
  3.0 14.4 %collective-permute-start.5 = (bf16[2,4,128,128]{3,2,1,0:T(8,128)(2,1)S(1)}, bf16[2,4,128,128]{3,2,1,0:T(8,128)(2,1)S(1)}, u32[]{:S(2)}, u32[]{:S(2)}) collective-permute-start(bf16[2,4,128,128]{3,2,1,0:T(8,128)(2,1)S(1)} %get-tuple-element.54.rest_0_), channel_id=1, source_target_pairs={{0,2},{1,3},{2,0},{3,1},{4,6},{5,7},{6,4},{7,5},{8,10},{9,11},{10,... | collective-permute-start | bytes 786440 | tf_op jit(solution)/shard_map/ppermute | solution.py:77
  6.2 1.3 collective-permute-start
  7.5 6.3 %collective-permute-start.1 = (f32[2,32,128]{2,1,0:T(8,128)S(1)}, f32[2,32,128]{2,1,0:T(8,128)S(1)}, u32[]{:S(2)}, u32[]{:S(2)}) collective-permute-start(f32[2,32,128]{2,1,0:T(8,128)S(1)} %get-tuple-element.49), channel_id=1, source_target_pairs={{0,2},{1,3},{2,0},{3,1},{4,6},{5,7},{6,4},{7,5},{8,10},{9,11},{10,... | collective-permute-start | bytes 98312 | tf_op jit(solution)/shard_map/ppermute | solution.py:77
  7.8 9.1 %collective-permute-start.2 = (f32[2,32,128]{2,1,0:T(8,128)S(1)}, f32[2,32,128]{2,1,0:T(8,128)S(1)}, u32[]{:S(2)}, u32[]{:S(2)}) collective-permute-start(f32[2,32,128]{2,1,0:T(8,128)S(1)} %get-tuple-element.50), channel_id=1, source_target_pairs={{0,4},{4,0},{8,12},{12,8},{16,20},{20,16},{24,28},{28,24},{1,5},{5... | collective-permute-start | bytes 98312 | tf_op jit(solution)/shard_map/ppermute | solution.py:77
  9.6 7.8 %collective-permute-start.3 = (f32[2,32,128]{2,1,0:T(8,128)S(1)}, f32[2,32,128]{2,1,0:T(8,128)S(1)}, u32[]{:S(2)}, u32[]{:S(2)}) collective-permute-start(f32[2,32,128]{2,1,0:T(8,128)S(1)} %get-tuple-element.51), channel_id=1, source_target_pairs={{0,6},{1,7},{2,4},{3,5},{4,2},{5,3},{6,0},{7,1},{8,14},{9,15},{10,... | collective-permute-start | bytes 98312 | tf_op jit(solution)/shard_map/ppermute | solution.py:440
  11.1 20.6 %collective-permute-start.13 = (bf16[3,4,128,128]{3,2,1,0:T(8,128)(2,1)S(1)}, bf16[3,4,128,128]{3,2,1,0:T(8,128)(2,1)S(1)}, u32[]{:S(2)}, u32[]{:S(2)}) collective-permute-start(bf16[3,4,128,128]{3,2,1,0:T(8,128)(2,1)S(1)} %get-tuple-element.56.rest_0_), channel_id=1, source_target_pairs={{0,2},{1,3},{2,0},{3,1},{4,6},{5,7},{6,4},{7,5},{8,10},{9,11},{10,... | collective-permute-start | bytes 1179656 | tf_op jit(solution)/shard_map/ppermute | solution.py:77
  13.8 15.3 %collective-permute-start.9 = (bf16[2,4,128,128]{3,2,1,0:T(8,128)(2,1)S(1)}, bf16[2,4,128,128]{3,2,1,0:T(8,128)(2,1)S(1)}, u32[]{:S(2)}, u32[]{:S(2)}) collective-permute-start(bf16[2,4,128,128]{3,2,1,0:T(8,128)(2,1)S(1)} %get-tuple-element.55), channel_id=1, source_target_pairs={{0,6},{1,7},{2,4},{3,5},{4,2},{5,3},{6,0},{7,1},{8,14},{9,15},{10,... | collective-permute-start | bytes 786440 | tf_op jit(solution)/shard_map/ppermute | solution.py:465
  16.9 14.7 %collective-permute-start.7 = (bf16[2,4,128,128]{3,2,1,0:T(8,128)(2,1)S(1)}, bf16[2,4,128,128]{3,2,1,0:T(8,128)(2,1)S(1)}, u32[]{:S(2)}, u32[]{:S(2)}) collective-permute-start(bf16[2,4,128,128]{3,2,1,0:T(8,128)(2,1)S(1)} %get-tuple-element.55), channel_id=1, source_target_pairs={{0,4},{4,0},{8,12},{12,8},{16,20},{20,16},{24,28},{28,24},{1,5},{5... | collective-permute-start | bytes 786440 | tf_op jit(solution)/shard_map/ppermute | solution.py:77
  17.4 14.2 %collective-permute-start.4 = (bf16[2,4,128,128]{3,2,1,0:T(8,128)(2,1)S(1)}, bf16[2,4,128,128]{3,2,1,0:T(8,128)(2,1)S(1)}, u32[]{:S(2)}, u32[]{:S(2)}) collective-permute-start(bf16[2,4,128,128]{3,2,1,0:T(8,128)(2,1)S(1)} %get-tuple-element.54.rest_0_), channel_id=1, source_target_pairs={{0,1},{1,0},{2,3},{3,2},{4,5},{5,4},{6,7},{7,6},{8,9},{9,8},{10,11... | collective-permute-start | bytes 786440 | tf_op jit(solution)/shard_map/ppermute | solution.py:77
  17.4 22.7 %collective-permute-start.17 = (bf16[3,4,128,128]{3,2,1,0:T(8,128)(2,1)S(1)}, bf16[3,4,128,128]{3,2,1,0:T(8,128)(2,1)S(1)}, u32[]{:S(2)}, u32[]{:S(2)}) collective-permute-start(bf16[3,4,128,128]{3,2,1,0:T(8,128)(2,1)S(1)} %get-tuple-element.57.rest_1_), channel_id=1, source_target_pairs={{0,4},{4,0},{8,12},{12,8},{16,20},{20,16},{24,28},{28,24},{1,5},{5... | collective-permute-start | bytes 1179656 | tf_op jit(solution)/shard_map/ppermute | solution.py:77
  29.1 11.0 %collective-permute-start.14 = (bf16[3,4,128,128]{3,2,1,0:T(8,128)(2,1)S(1)}, bf16[3,4,128,128]{3,2,1,0:T(8,128)(2,1)S(1)}, u32[]{:S(2)}, u32[]{:S(2)}) collective-permute-start(bf16[3,4,128,128]{3,2,1,0:T(8,128)(2,1)S(1)} %get-tuple-element.57.rest_1_), channel_id=1, source_target_pairs={{0,2},{1,3},{2,0},{3,1},{4,6},{5,7},{6,4},{7,5},{8,10},{9,11},{10,... | collective-permute-start | bytes 1179656 | tf_op jit(solution)/shard_map/ppermute | solution.py:77
  31.6 14.1 %collective-permute-start.18 = (bf16[3,4,128,128]{3,2,1,0:T(8,128)(2,1)S(1)}, bf16[3,4,128,128]{3,2,1,0:T(8,128)(2,1)S(1)}, u32[]{:S(2)}, u32[]{:S(2)}) collective-permute-start(bf16[3,4,128,128]{3,2,1,0:T(8,128)(2,1)S(1)} %get-tuple-element.56.rest_0_), channel_id=1, source_target_pairs={{0,4},{4,0},{8,12},{12,8},{16,20},{20,16},{24,28},{28,24},{1,5},{5... | collective-permute-start | bytes 1179656 | tf_op jit(solution)/shard_map/ppermute | solution.py:77
  31.6 14.4 %collective-permute-start.11 = (bf16[3,4,128,128]{3,2,1,0:T(8,128)(2,1)S(1)}, bf16[3,4,128,128]{3,2,1,0:T(8,128)(2,1)S(1)}, u32[]{:S(2)}, u32[]{:S(2)}) collective-permute-start(bf16[3,4,128,128]{3,2,1,0:T(8,128)(2,1)S(1)} %get-tuple-element.56.rest_0_), channel_id=1, source_target_pairs={{0,1},{1,0},{2,3},{3,2},{4,5},{5,4},{6,7},{7,6},{8,9},{9,8},{10,11... | collective-permute-start | bytes 1179656 | tf_op jit(solution)/shard_map/ppermute | solution.py:77
  31.7 14.6 %collective-permute-start.12 = (bf16[3,4,128,128]{3,2,1,0:T(8,128)(2,1)S(1)}, bf16[3,4,128,128]{3,2,1,0:T(8,128)(2,1)S(1)}, u32[]{:S(2)}, u32[]{:S(2)}) collective-permute-start(bf16[3,4,128,128]{3,2,1,0:T(8,128)(2,1)S(1)} %get-tuple-element.57.rest_1_), channel_id=1, source_target_pairs={{0,1},{1,0},{2,3},{3,2},{4,5},{5,4},{6,7},{7,6},{8,9},{9,8},{10,11... | collective-permute-start | bytes 1179656 | tf_op jit(solution)/shard_map/ppermute | solution.py:77
  40.1 6.3 %collective-permute-start.6 = (bf16[2,4,128,128]{3,2,1,0:T(8,128)(2,1)S(1)}, bf16[2,4,128,128]{3,2,1,0:T(8,128)(2,1)S(1)}, u32[]{:S(2)}, u32[]{:S(2)}) collective-permute-start(bf16[2,4,128,128]{3,2,1,0:T(8,128)(2,1)S(1)} %collective-permute-done.5.rest_2_), channel_id=1, source_target_pairs={{0,1},{1,0},{2,3},{3,2},{4,5},{5,4},{6,7},{7,6},{8,9},{9,8},{10,11... | collective-permute-start | bytes 786440 | tf_op jit(solution)/shard_map/ppermute | solution.py:77
  40.1 8.3 %collective-permute-start.15 = (bf16[3,4,128,128]{3,2,1,0:T(8,128)(2,1)S(1)}, bf16[3,4,128,128]{3,2,1,0:T(8,128)(2,1)S(1)}, u32[]{:S(2)}, u32[]{:S(2)}) collective-permute-start(bf16[3,4,128,128]{3,2,1,0:T(8,128)(2,1)S(1)} %collective-permute-done.13.rest_4_), channel_id=1, source_target_pairs={{0,1},{1,0},{2,3},{3,2},{4,5},{5,4},{6,7},{7,6},{8,9},{9,8},{10,11... | collective-permute-start | bytes 1179656 | tf_op jit(solution)/shard_map/ppermute | solution.py:77
  45.8 8.3 %collective-permute-start.21 = (bf16[3,4,128,128]{3,2,1,0:T(8,128)(2,1)S(1)}, bf16[3,4,128,128]{3,2,1,0:T(8,128)(2,1)S(1)}, u32[]{:S(2)}, u32[]{:S(2)}) collective-permute-start(bf16[3,4,128,128]{3,2,1,0:T(8,128)(2,1)S(1)} %collective-permute-done.17.rest_8_), channel_id=1, source_target_pairs={{0,2},{1,3},{2,0},{3,1},{4,6},{5,7},{6,4},{7,5},{8,10},{9,11},{10,... | collective-permute-start | bytes 1179656 | tf_op jit(solution)/shard_map/ppermute | solution.py:77
  46.0 8.2 %collective-permute-start.22 = (bf16[3,4,128,128]{3,2,1,0:T(8,128)(2,1)S(1)}, bf16[3,4,128,128]{3,2,1,0:T(8,128)(2,1)S(1)}, u32[]{:S(2)}, u32[]{:S(2)}) collective-permute-start(bf16[3,4,128,128]{3,2,1,0:T(8,128)(2,1)S(1)} %collective-permute-done.13.rest_4_), channel_id=1, source_target_pairs={{0,4},{4,0},{8,12},{12,8},{16,20},{20,16},{24,28},{28,24},{1,5},{5... | collective-permute-start | bytes 1179656 | tf_op jit(solution)/shard_map/ppermute | solution.py:77
  46.3 1.5 %collective-permute-start.10 = (bf16[2,4,128,128]{3,2,1,0:T(8,128)(2,1)S(1)}, bf16[2,4,128,128]{3,2,1,0:T(8,128)(2,1)S(1)}, u32[]{:S(2)}, u32[]{:S(2)}) collective-permute-start(bf16[2,4,128,128]{3,2,1,0:T(8,128)(2,1)S(1)} %collective-permute-done.9.rest_6_), channel_id=1, source_target_pairs={{0,1},{1,0},{2,3},{3,2},{4,5},{5,4},{6,7},{7,6},{8,9},{9,8},{10,11... | collective-permute-start | bytes 786440 | tf_op jit(solution)/shard_map/ppermute | solution.py:77
  46.3 1.9 %collective-permute-start.8 = (bf16[2,4,128,128]{3,2,1,0:T(8,128)(2,1)S(1)}, bf16[2,4,128,128]{3,2,1,0:T(8,128)(2,1)S(1)}, u32[]{:S(2)}, u32[]{:S(2)}) collective-permute-start(bf16[2,4,128,128]{3,2,1,0:T(8,128)(2,1)S(1)} %collective-permute-done.7.rest_4_), channel_id=1, source_target_pairs={{0,1},{1,0},{2,3},{3,2},{4,5},{5,4},{6,7},{7,6},{8,9},{9,8},{10,11... | collective-permute-start | bytes 786440 | tf_op jit(solution)/shard_map/ppermute | solution.py:77
  47.8 7.4 %collective-permute-start.19 = (bf16[3,4,128,128]{3,2,1,0:T(8,128)(2,1)S(1)}, bf16[3,4,128,128]{3,2,1,0:T(8,128)(2,1)S(1)}, u32[]{:S(2)}, u32[]{:S(2)}) collective-permute-start(bf16[3,4,128,128]{3,2,1,0:T(8,128)(2,1)S(1)} %collective-permute-done.17.rest_8_), channel_id=1, source_target_pairs={{0,1},{1,0},{2,3},{3,2},{4,5},{5,4},{6,7},{7,6},{8,9},{9,8},{10,11... | collective-permute-start | bytes 1179656 | tf_op jit(solution)/shard_map/ppermute | solution.py:77
  48.2 7.0 %collective-permute-start.16 = (bf16[3,4,128,128]{3,2,1,0:T(8,128)(2,1)S(1)}, bf16[3,4,128,128]{3,2,1,0:T(8,128)(2,1)S(1)}, u32[]{:S(2)}, u32[]{:S(2)}) collective-permute-start(bf16[3,4,128,128]{3,2,1,0:T(8,128)(2,1)S(1)} %collective-permute-done.14.rest_5_), channel_id=1, source_target_pairs={{0,1},{1,0},{2,3},{3,2},{4,5},{5,4},{6,7},{7,6},{8,9},{9,8},{10,11... | collective-permute-start | bytes 1179656 | tf_op jit(solution)/shard_map/ppermute | solution.py:77
  48.4 6.9 %collective-permute-start.20 = (bf16[3,4,128,128]{3,2,1,0:T(8,128)(2,1)S(1)}, bf16[3,4,128,128]{3,2,1,0:T(8,128)(2,1)S(1)}, u32[]{:S(2)}, u32[]{:S(2)}) collective-permute-start(bf16[3,4,128,128]{3,2,1,0:T(8,128)(2,1)S(1)} %collective-permute-done.18.rest_9_), channel_id=1, source_target_pairs={{0,1},{1,0},{2,3},{3,2},{4,5},{5,4},{6,7},{7,6},{8,9},{9,8},{10,11... | collective-permute-start | bytes 1179656 | tf_op jit(solution)/shard_map/ppermute | solution.py:77
  54.1 2.6 %collective-permute-start.23 = (bf16[3,4,128,128]{3,2,1,0:T(8,128)(2,1)S(1)}, bf16[3,4,128,128]{3,2,1,0:T(8,128)(2,1)S(1)}, u32[]{:S(2)}, u32[]{:S(2)}) collective-permute-start(bf16[3,4,128,128]{3,2,1,0:T(8,128)(2,1)S(1)} %collective-permute-done.21.rest_3_.rest_12_), channel_id=1, source_target_pairs={{0,1},{1,0},{2,3},{3,2},{4,5},{5,4},{6,7},{7,6},{8,9},{9,8},{10,11... | collective-permute-start | bytes 1179656 | tf_op jit(solution)/shard_map/ppermute | solution.py:77
  54.2 2.6 %collective-permute-start.24 = (bf16[3,4,128,128]{3,2,1,0:T(8,128)(2,1)S(1)}, bf16[3,4,128,128]{3,2,1,0:T(8,128)(2,1)S(1)}, u32[]{:S(2)}, u32[]{:S(2)}) collective-permute-start(bf16[3,4,128,128]{3,2,1,0:T(8,128)(2,1)S(1)} %collective-permute-done.22.rest_4_.rest_13_), channel_id=1, source_target_pairs={{0,1},{1,0},{2,3},{3,2},{4,5},{5,4},{6,7},{7,6},{8,9},{9,8},{10,11... | collective-permute-start | bytes 1179656 | tf_op jit(solution)/shard_map/ppermute | solution.py:77
  57.5 7.4 %collective-permute-start.27 = (s32[32,768]{1,0:T(8,128)S(1)}, s32[32,768]{1,0:T(8,128)S(1)}, u32[]{:S(2)}, u32[]{:S(2)}) collective-permute-start(s32[32,768]{1,0:T(8,128)S(1)} %pad_add_fusion.5), channel_id=1, source_target_pairs={{0,24},{4,28},{8,16},{12,20},{16,8},{20,12},{24,0},{28,4},{1,25},{... | collective-permute-start | bytes 294920 | tf_op jit(solution)/shard_map/ppermute | solution.py:77
  61.6 8.2 %collective-permute-start.26 = (s32[32,768]{1,0:T(8,128)S(1)}, s32[32,768]{1,0:T(8,128)S(1)}, u32[]{:S(2)}, u32[]{:S(2)}) collective-permute-start(s32[32,768]{1,0:T(8,128)S(1)} %pad_add_fusion.4), channel_id=1, source_target_pairs={{0,16},{4,20},{8,24},{12,28},{16,0},{20,4},{24,8},{28,12},{1,17},{... | collective-permute-start | bytes 294920 | tf_op jit(solution)/shard_map/ppermute | solution.py:77
  61.7 8.1 %collective-permute-start.25 = (s32[32,768]{1,0:T(8,128)S(1)}, s32[32,768]{1,0:T(8,128)S(1)}, u32[]{:S(2)}, u32[]{:S(2)}) collective-permute-start(s32[32,768]{1,0:T(8,128)S(1)} %pad_add_fusion.3), channel_id=1, source_target_pairs={{0,8},{4,12},{8,0},{12,4},{16,24},{20,28},{24,16},{28,20},{1,9},{5... | collective-permute-start | bytes 294920 | tf_op jit(solution)/shard_map/ppermute | solution.py:77
  71.7 8.0 %collective-permute-start.29 = (s32[32,768]{1,0:T(8,128)S(1)}, s32[32,768]{1,0:T(8,128)S(1)}, u32[]{:S(2)}, u32[]{:S(2)}) collective-permute-start(s32[32,768]{1,0:T(8,128)S(1)} %shard_map.58), channel_id=1, source_target_pairs={{0,16},{4,20},{8,24},{12,28},{16,0},{20,4},{24,8},{28,12},{1,17},{... | collective-permute-start | bytes 294920 | tf_op jit(solution)/shard_map/ppermute | solution.py:77
  72.7 8.1 %collective-permute-start.28 = (s32[32,768]{1,0:T(8,128)S(1)}, s32[32,768]{1,0:T(8,128)S(1)}, u32[]{:S(2)}, u32[]{:S(2)}) collective-permute-start(s32[32,768]{1,0:T(8,128)S(1)} %shard_map.57), channel_id=1, source_target_pairs={{0,8},{4,12},{8,0},{12,4},{16,24},{20,28},{24,16},{28,20},{1,9},{5... | collective-permute-start | bytes 294920 | tf_op jit(solution)/shard_map/ppermute | solution.py:77
  75.7 6.4 %collective-permute-start.30 = (s32[32,768]{1,0:T(8,128)S(1)}, s32[32,768]{1,0:T(8,128)S(1)}, u32[]{:S(2)}, u32[]{:S(2)}) collective-permute-start(s32[32,768]{1,0:T(8,128)S(1)} %get-tuple-element.68), channel_id=1, source_target_pairs={{0,24},{4,28},{8,16},{12,20},{16,8},{20,12},{24,0},{28,4},{1,25},{... | collective-permute-start | bytes 294920 | tf_op jit(solution)/shard_map/ppermute | solution.py:77
  84.0 5.4 %collective-permute-start.31 = (s32[32,768]{1,0:T(8,128)S(1)}, s32[32,768]{1,0:T(8,128)S(1)}, u32[]{:S(2)}, u32[]{:S(2)}) collective-permute-start(s32[32,768]{1,0:T(8,128)S(1)} %shard_map.60), channel_id=1, source_target_pairs={{0,8},{4,12},{8,0},{12,4},{16,24},{20,28},{24,16},{28,20},{1,9},{5... | collective-permute-start | bytes 294920 | tf_op jit(solution)/shard_map/ppermute | solution.py:77
  86.3 9.8 %collective-permute-start.32 = (s32[32,768]{1,0:T(8,128)S(1)}, s32[32,768]{1,0:T(8,128)S(1)}, u32[]{:S(2)}, u32[]{:S(2)}) collective-permute-start(s32[32,768]{1,0:T(8,128)S(1)} %shard_map.61), channel_id=1, source_target_pairs={{0,16},{4,20},{8,24},{12,28},{16,0},{20,4},{24,8},{28,12},{1,17},{... | collective-permute-start | bytes 294920 | tf_op jit(solution)/shard_map/ppermute | solution.py:77
  87.0 9.1 %collective-permute-start.33 = (s32[32,768]{1,0:T(8,128)S(1)}, s32[32,768]{1,0:T(8,128)S(1)}, u32[]{:S(2)}, u32[]{:S(2)}) collective-permute-start(s32[32,768]{1,0:T(8,128)S(1)} %get-tuple-element.70), channel_id=1, source_target_pairs={{0,24},{4,28},{8,16},{12,20},{16,8},{20,12},{24,0},{28,4},{1,25},{... | collective-permute-start | bytes 294920 | tf_op jit(solution)/shard_map/ppermute | solution.py:77
  97.3 6.7 %collective-permute-start.34 = (bf16[32,1024]{1,0:T(8,128)(2,1)S(1)}, bf16[32,1024]{1,0:T(8,128)(2,1)S(1)}, u32[]{:S(2)}, u32[]{:S(2)}) collective-permute-start(bf16[32,1024]{1,0:T(8,128)(2,1)S(1)} %fusion.8), channel_id=1, source_target_pairs={{0,24},{4,28},{8,16},{12,20},{16,8},{20,12},{24,0},{28,4},{1,25},{... | collective-permute-start | bytes 196616 | tf_op jit(solution)/shard_map/ppermute | solution.py:77
  99.1 5.4 %collective-permute-start.35 = (bf16[32,1024]{1,0:T(8,128)(2,1)S(1)}, bf16[32,1024]{1,0:T(8,128)(2,1)S(1)}, u32[]{:S(2)}, u32[]{:S(2)}) collective-permute-start(bf16[32,1024]{1,0:T(8,128)(2,1)S(1)} %fusion.8), channel_id=1, source_target_pairs={{0,8},{4,12},{8,0},{12,4},{16,24},{20,28},{24,16},{28,20},{1,9},{5... | collective-permute-start | bytes 196616 | tf_op jit(solution)/shard_map/ppermute | solution.py:77
  100.0 6.4 %collective-permute-start.36 = (bf16[32,1024]{1,0:T(8,128)(2,1)S(1)}, bf16[32,1024]{1,0:T(8,128)(2,1)S(1)}, u32[]{:S(2)}, u32[]{:S(2)}) collective-permute-start(bf16[32,1024]{1,0:T(8,128)(2,1)S(1)} %fusion.8), channel_id=1, source_target_pairs={{0,16},{4,20},{8,24},{12,28},{16,0},{20,4},{24,8},{28,12},{1,17},{... | collective-permute-start | bytes 196616 | tf_op jit(solution)/shard_map/ppermute | solution.py:77
  107.0 6.9 %collective-permute-start.37 = (bf16[32,1024]{1,0:T(8,128)(2,1)S(1)}, bf16[32,1024]{1,0:T(8,128)(2,1)S(1)}, u32[]{:S(2)}, u32[]{:S(2)}) collective-permute-start(bf16[32,1024]{1,0:T(8,128)(2,1)S(1)} %get-tuple-element.72), channel_id=1, source_target_pairs={{0,24},{4,28},{8,16},{12,20},{16,8},{20,12},{24,0},{28,4},{1,25},{... | collective-permute-start | bytes 196616 | tf_op jit(solution)/shard_map/ppermute | solution.py:77
  108.9 5.4 %collective-permute-start.38 = (bf16[32,1024]{1,0:T(8,128)(2,1)S(1)}, bf16[32,1024]{1,0:T(8,128)(2,1)S(1)}, u32[]{:S(2)}, u32[]{:S(2)}) collective-permute-start(bf16[32,1024]{1,0:T(8,128)(2,1)S(1)} %get-tuple-element.72), channel_id=1, source_target_pairs={{0,8},{4,12},{8,0},{12,4},{16,24},{20,28},{24,16},{28,20},{1,9},{5... | collective-permute-start | bytes 196616 | tf_op jit(solution)/shard_map/ppermute | solution.py:77
  108.9 6.4 %collective-permute-start.39 = (bf16[32,1024]{1,0:T(8,128)(2,1)S(1)}, bf16[32,1024]{1,0:T(8,128)(2,1)S(1)}, u32[]{:S(2)}, u32[]{:S(2)}) collective-permute-start(bf16[32,1024]{1,0:T(8,128)(2,1)S(1)} %get-tuple-element.72), channel_id=1, source_target_pairs={{0,16},{4,20},{8,24},{12,28},{16,0},{20,4},{24,8},{28,12},{1,17},{... | collective-permute-start | bytes 196616 | tf_op jit(solution)/shard_map/ppermute | solution.py:77
  115.8 6.6 %collective-permute-start.40 = (bf16[32,1024]{1,0:T(8,128)(2,1)S(1)}, bf16[32,1024]{1,0:T(8,128)(2,1)S(1)}, u32[]{:S(2)}, u32[]{:S(2)}) collective-permute-start(bf16[32,1024]{1,0:T(8,128)(2,1)S(1)} %get-tuple-element.75), channel_id=1, source_target_pairs={{0,24},{4,28},{8,16},{12,20},{16,8},{20,12},{24,0},{28,4},{1,25},{... | collective-permute-start | bytes 196616 | tf_op jit(solution)/shard_map/ppermute | solution.py:77
  117.6 6.0 %collective-permute-start.41 = (bf16[32,1024]{1,0:T(8,128)(2,1)S(1)}, bf16[32,1024]{1,0:T(8,128)(2,1)S(1)}, u32[]{:S(2)}, u32[]{:S(2)}) collective-permute-start(bf16[32,1024]{1,0:T(8,128)(2,1)S(1)} %get-tuple-element.75), channel_id=1, source_target_pairs={{0,8},{4,12},{8,0},{12,4},{16,24},{20,28},{24,16},{28,20},{1,9},{5... | collective-permute-start | bytes 196616 | tf_op jit(solution)/shard_map/ppermute | solution.py:77
  117.8 6.7 %collective-permute-start.42 = (bf16[32,1024]{1,0:T(8,128)(2,1)S(1)}, bf16[32,1024]{1,0:T(8,128)(2,1)S(1)}, u32[]{:S(2)}, u32[]{:S(2)}) collective-permute-start(bf16[32,1024]{1,0:T(8,128)(2,1)S(1)} %get-tuple-element.75), channel_id=1, source_target_pairs={{0,16},{4,20},{8,24},{12,28},{16,0},{20,4},{24,8},{28,12},{1,17},{... | collective-permute-start | bytes 196616 | tf_op jit(solution)/shard_map/ppermute | solution.py:77
  125.0 1.3 collective-permute-start.43
  126.4 4.0 %collective-permute-start.44 = (f32[2,32,128]{2,1,0:T(8,128)S(1)}, f32[2,32,128]{2,1,0:T(8,128)S(1)}, u32[]{:S(2)}, u32[]{:S(2)}) collective-permute-start(f32[2,32,128]{2,1,0:T(8,128)S(1)} %get-tuple-element.80), channel_id=1, source_target_pairs={{0,2},{1,3},{2,0},{3,1},{4,6},{5,7},{6,4},{7,5},{8,10},{9,11},{10,... | collective-permute-start | bytes 98312 | tf_op jit(solution)/shard_map/ppermute | solution.py:77
  128.5 3.9 %collective-permute-start.45 = (f32[2,32,128]{2,1,0:T(8,128)S(1)}, f32[2,32,128]{2,1,0:T(8,128)S(1)}, u32[]{:S(2)}, u32[]{:S(2)}) collective-permute-start(f32[2,32,128]{2,1,0:T(8,128)S(1)} %get-tuple-element.81), channel_id=1, source_target_pairs={{0,4},{4,0},{8,12},{12,8},{16,20},{20,16},{24,28},{28,24},{1,5},{5... | collective-permute-start | bytes 98312 | tf_op jit(solution)/shard_map/ppermute | solution.py:77
  130.0 4.8 %collective-permute-start.46 = (f32[2,32,128]{2,1,0:T(8,128)S(1)}, f32[2,32,128]{2,1,0:T(8,128)S(1)}, u32[]{:S(2)}, u32[]{:S(2)}) collective-permute-start(f32[2,32,128]{2,1,0:T(8,128)S(1)} %get-tuple-element.82), channel_id=1, source_target_pairs={{0,6},{1,7},{2,4},{3,5},{4,2},{5,3},{6,0},{7,1},{8,14},{9,15},{10,... | collective-permute-start | bytes 98312 | tf_op jit(solution)/shard_map/ppermute | solution.py:440
  (4 other events, 9.8 us)
